TPU v7x, 32 devices: a whole 2x2x4 slice. The times are simulated.
32 devices in a mesh: blk: 8 (over z, x), task: 4 (over y, core).
Axes of the slice: x: 2, y: 2, z: 4, core: 2. Of those that a mesh axis runs over, the one named last changes fastest.
Arguments:
- amplitudes: bfloat16 [1024, 1024, 128], P('blk', 'task'), may hold values from -6 to 6
- integral_tiles: bfloat16 [8, 4, 4, 2, 1024, 128], P('blk', 'task'), may hold values from -0.09375 to 0.09375
- task_list: int32 [8, 4, 4, 2], P(None, 'task'), may hold values from 0 to 255
- block_offsets: int32 [8, 4, 4, 2], P(None, 'task'), may hold values from 0 to 15
- tile_counts: int32 [8, 4, 4], P(None, 'task'), may hold values from 1 to 2, as said below
Outputs:
- ladder: float32 [128, 2048], P('blk', 'task')
Inputs may be any that keep to these rules, and one draw needn't show every extreme that they name: `tile_counts`: in each blk group exactly one worker receives 2 live tiles from every producer of that group, and every other worker receives exactly 1 live tile from each producer.
All inputs are finite; a program needn't handle non-finite values.
Results may differ from a plain program's by a relative error of at most 0.0003.
Values may be sent and summed in bfloat16 or wider, within the bound.
No kernel may reach another device: no remote copies, remote signals or barrier semaphores. Data moves between devices by JAX's collectives and lax.ppermute only.
A program may use at most 128 MiB of HBM per device.

v0:
```python
import jax
import jax.numpy as jnp
from jax import lax
from jax.sharding import PartitionSpec as P

NRB = 16


def slot_layout(lists_row, offsets_row, counts_row, block_total):
    slot_rank = jnp.arange(lists_row.shape[-1], dtype=jnp.int32)[None, :]
    live_mask = (slot_rank < counts_row).reshape(-1)
    block_ids = jnp.arange(block_total, dtype=jnp.int32)[None, :]
    matched = (offsets_row.reshape(-1)[:, None] == block_ids) & live_mask[:, None]
    placement = jnp.where(matched, 1.0, 0.0).astype(jnp.float32)
    return (lists_row.reshape(-1), placement)


def contract(amplitude_block, columns, slice_set, placement):
    picked = jnp.take(amplitude_block, columns, axis=1)
    products = jnp.einsum("cnp,ncr->npr", picked, slice_set, preferred_element_type=jnp.float32)
    return jnp.einsum("nb,npr->pbr", placement, products, precision=lax.Precision.HIGHEST)


def body(amplitudes, integral_tiles, task_list, block_offsets, tile_counts):
    lists_in, offsets_in, counts_in = (
        lax.all_to_all(task_list, "task", split_axis=2, concat_axis=1, tiled=True),
        lax.all_to_all(block_offsets, "task", split_axis=2, concat_axis=1, tiled=True),
        lax.all_to_all(tile_counts, "task", split_axis=2, concat_axis=1, tiled=True),
    )
    arrived = lax.all_to_all(integral_tiles, "task", split_axis=2, concat_axis=1, tiled=True)
    slot_total = arrived.shape[1] * arrived.shape[3]
    virt_total = arrived.shape[4]
    row_block = arrived.shape[5]
    pair_total = amplitudes.shape[2]
    slices = arrived.reshape(slot_total, virt_total, row_block)
    blk_group = lax.axis_index("blk")
    columns, placement = slot_layout(
        lax.dynamic_index_in_dim(lists_in, blk_group, 0, keepdims=False),
        lax.dynamic_index_in_dim(offsets_in, blk_group, 0, keepdims=False),
        lax.dynamic_index_in_dim(counts_in, blk_group, 0, keepdims=False),
        NRB,
    )
    full_amplitudes = lax.all_gather(amplitudes, "blk", axis=0, tiled=True)
    partial_value = contract(full_amplitudes, columns, slices, placement)
    partial_value = partial_value.reshape(pair_total, NRB * row_block)
    shared_rows = lax.psum_scatter(partial_value, "task", scatter_dimension=1, tiled=True)
    ladder = lax.psum_scatter(shared_rows, "blk", scatter_dimension=0, tiled=True)
    return ladder


def solution(mesh):
    placed = (
        P("blk", "task", None),
        P("blk", "task", None, None, None, None),
        P(None, "task", None, None),
        P(None, "task", None, None),
        P(None, "task", None),
    )
    return jax.shard_map(
        body, mesh=mesh, in_specs=placed, out_specs=P("blk", "task"), check_vma=False
    )
```

profile of v0, /device:TPU:0, one launch (start us, length us, event | category | flops | bytes accessed | tf_op | source)
XLA Modules:
  0.0 1394.0 jit_solution(2455465173747659894)
XLA Ops:
  6.5 0.0 all-gather.2.cloned.1.call-start
  6.5 12.0 copy.15
  18.5 0.0 copy-start.2
  18.5 0.0 copy-start
  18.5 0.0 copy-start.1
  18.5 0.0 all-gather.2.cloned.1.call-update
  18.5 0.7 copy-done.2
  19.2 7.8 all_to_all.16
  27.0 0.0 copy-done
  27.0 6.1 all_to_all.17
  33.1 0.0 copy-done.1
  33.1 6.1 all_to_all.18
  39.2 3.6 all-to-all-start.1
  42.8 0.0 reduce-scatter.3.cloned.1.call-start
  42.9 0.2 dynamic-slice_reduce_fusion.2
  43.1 0.1 iota_compare_fusion.1
  43.2 0.1 lt.51
  43.3 0.2 dynamic-slice_reduce_fusion.1
  43.5 0.1 reshape.86
  43.6 0.1 reshape.85
  43.7 0.2 dynamic-slice_reduce_fusion
  43.9 0.1 eq.15
  44.0 1244.3 %all-gather.2.cloned.1.call-done = bf16[1024,256,128]{2,0,1:T(8,128)(2,1)} async-done(((bf16[128,256,128]{2,0,1:T(8,128)(2,1)}), bf16[1024,256,128]{2,0,1:T(8,128)(2,1)}) %all-gather.2.cloned.1.call-update) | async-done | bytes 67108880 | tf_op jit(solution)/shard_map/all_gather | solution.py:43
  1288.3 3.5 gather_fusion
  1291.8 0.0 all-to-all-done.1
  1291.8 2.5 fusion
  1294.3 1.3 fusion.5
  1295.6 1.3 copy.26
  1296.9 0.0 reduce-scatter.3.cloned.1.call-update
  1296.9 0.0 reduce-scatter.5.cloned.1.call-start
  1297.0 25.0 %reduce-scatter.3.cloned.1.call-done = f32[128,512]{1,0:T(8,128)} async-done(((f32[128,2048]{1,0:T(8,128)}), f32[128,512]{1,0:T(8,128)}) %reduce-scatter.3.cloned.1.call-update) | async-done | bytes 262160 | tf_op jit(solution)/shard_map/reduce_scatter | solution.py:46
  1321.9 0.0 reduce-scatter.5.cloned.1.call-update
  1322.0 65.5 %reduce-scatter.5.cloned.1.call-done = f32[16,512]{1,0:T(8,128)} async-done(((f32[128,512]{1,0:T(8,128)}), f32[16,512]{1,0:T(8,128)}) %reduce-scatter.5.cloned.1.call-update) | async-done | bytes 32784 | tf_op jit(solution)/shard_map/reduce_scatter | solution.py:47
  (3 shorter events, 0.0 us)
Async XLA Ops:
  6.5 1281.8 %all-gather.2.cloned.1.call-start = ((), (), s32[]{:S(2)}) async-start(), calls=%async_computation.6 | async-start | bytes 75497472 | tf_op jit(solution)/shard_map/all_gather | solution.py:43
  18.5 0.7 copy-start.2
  18.5 8.5 copy-start
  18.5 14.6 %copy-start.1 = (s32[8,1,4,2]{0,3,2,1:T(2,128)S(1)}, s32[8,1,4,2]{0,3,2,1:T(2,128)}, u32[]{:S(2)}) copy-start(s32[8,1,4,2]{0,3,2,1:T(2,128)} %param.8) | copy-start | bytes 772
  39.2 1252.6 %all-to-all-start.1 = ((bf16[1,1,4,2,1024,128]{5,4,3,1,0,2:T(8,128)(2,1)}), bf16[1,1,4,2,1024,128]{5,4,3,1,0,2:T(8,128)(2,1)S(1)}, u32[]{:S(2)}, u32[]{:S(2)}) async-start(bf16[1,1,4,2,1024,128]{5,4,3,1,0,2:T(8,128)(2,1)} %bitcast.3), calls=%async_computation.1 | async-start | bytes 4194304 | tf_op jit(solution)/shard_map/all_to_all | solution.py:30
  42.8 1279.1 %reduce-scatter.3.cloned.1.call-start = ((), (), s32[]{:S(2)}) async-start(), calls=%async_computation.7 | async-start | bytes 1310720 | tf_op jit(solution)/shard_map/reduce_scatter | solution.py:46
  1296.9 90.6 %reduce-scatter.5.cloned.1.call-start = ((), (), s32[]{:S(2)}) async-start(), calls=%async_computation.8 | async-start | bytes 294912 | tf_op jit(solution)/shard_map/reduce_scatter | solution.py:47
Sparse Core Ops, SparseCore 0:
  18.6 1269.5 all-gather.1
  1297.0 24.8 reduce-scatter.2
  1325.6 61.8 reduce-scatter.4
where the time goes:
time: 1390 us
  waiting for transfers between devices  1330 us (96%)
  blocking collectives  20 us (1%)
  local copies, waits for them, and re-layouts  18.5 us (1%)
    all_gather x1, waiting for transfers between devices, body(): full_amplitudes = lax.all_gather(amplitudes, 'blk', axis=0, tiled=True)  1240 us
    reduce_scatter x1, waiting for transfers between devices, body(): lax.psum_scatter(shared_rows, 'blk', scatter_dimension=0, tiled=True)  65.5 us
  transfers between devices with their start and end apart: 4, of which 3 were waited for; matrix products, arithmetic and copies ran while one was open for 0% of the time, Pallas kernels for 0%

commit v1 on v0

v1 whole, which is shorter than its diff:
```python
import functools

import jax
import jax.numpy as jnp
from jax import lax
from jax.experimental import pallas as pl
from jax.experimental.pallas import tpu as pltpu
from jax.sharding import Mesh, PartitionSpec as P

NRB = 16
TASK = ("ty", "core")
EVERY = ("blk", "ty", "core")


def ladder_kernel(meta, columns, tiles, keep, send, total, *, group, row_tasks, pair_blocks):
    step = pl.program_id(0)
    slots = pl.num_programs(0) * group

    @pl.when(step == 0)
    def _():
        total[...] = jnp.zeros_like(total)

    def add_slot(n, carry):
        slot = step * group + n

        @pl.when(meta[slots + slot] > 0)
        def _():
            product = lax.dot_general(
                columns[n], tiles[n], (((0,), (0,)), ((), ())), preferred_element_type=jnp.float32
            )
            total[meta[slot]] += product

        return carry

    lax.fori_loop(0, group, add_slot, 0, unroll=True)

    @pl.when(step == pl.num_programs(0) - 1)
    def _():
        core = meta[2 * slots]
        rows = NRB // (2 * row_tasks)
        pairs = total.shape[1] // pair_blocks
        for task in range(row_tasks):
            for block in range(pair_blocks):
                span = pl.ds(block * pairs, pairs)
                for row in range(rows):
                    keep[block, task, row] = total[(2 * task + core) * rows + row, span, :]
                    send[block, task, row] = total[(2 * task + 1 - core) * rows + row, span, :]


def body(amplitudes, integral_tiles, task_list, block_offsets, tile_counts, *, shape):
    blocks, row_tasks = shape
    tasks = 2 * row_tasks
    chunk, _, pair_total = amplitudes.shape
    capacity, row_block = integral_tiles.shape[3], integral_tiles.shape[5]
    slots = blocks * tasks * capacity

    cut = integral_tiles.reshape(tasks, capacity, blocks, chunk, row_block)
    cut = jnp.transpose(cut, (2, 0, 1, 3, 4)).reshape(blocks * tasks, capacity, chunk, row_block)
    arrived = lax.all_to_all(cut, EVERY, 0, 0, tiled=True).reshape(slots, chunk, row_block)

    rank = jnp.arange(capacity, dtype=jnp.int32)
    live = (rank < tile_counts[..., None]).astype(jnp.int32)
    packed = (task_list * NRB + block_offsets) * 2 + live
    lists = lax.all_gather(packed, TASK, axis=1, tiled=True)
    core = lax.axis_index("core").astype(jnp.int32)
    worker = lax.axis_index("ty") * 2 + core
    mine = lax.dynamic_index_in_dim(lists, worker, 2, keepdims=False).reshape(slots)
    column = mine // (2 * NRB)
    meta = jnp.concatenate([(mine // 2) % NRB, mine % 2, core[None]])
    picked = jnp.take(jnp.transpose(amplitudes, (1, 0, 2)), column, axis=0, mode="clip")

    group = 8
    rows, pairs = NRB // tasks, pair_total // blocks
    part = jax.ShapeDtypeStruct((blocks, row_tasks, rows, pairs, row_block), jnp.float32)
    whole = pl.BlockSpec(part.shape, lambda i, m: (0,) * 5)
    keep, send = pl.pallas_call(
        functools.partial(ladder_kernel, group=group, row_tasks=row_tasks, pair_blocks=blocks),
        out_shape=(part, part),
        grid_spec=pltpu.PrefetchScalarGridSpec(
            num_scalar_prefetch=1,
            grid=(slots // group,),
            in_specs=[
                pl.BlockSpec((group, chunk, pair_total), lambda i, m: (i, 0, 0)),
                pl.BlockSpec((group, chunk, row_block), lambda i, m: (i, 0, 0)),
            ],
            out_specs=(whole, whole),
            scratch_shapes=[pltpu.VMEM((NRB, pair_total, row_block), jnp.float32)],
        ),
        compiler_params=pltpu.CompilerParams(vmem_limit_bytes=24 << 20),
        cost_estimate=pl.CostEstimate(
            flops=2 * slots * chunk * pair_total * row_block,
            bytes_accessed=2 * slots * chunk * (pair_total + row_block) + 8 * NRB * pair_total * row_block,
            transcendentals=0,
        ),
        name="ladder",
    )(meta, picked, arrived)

    other = lax.ppermute(send, "core", [(0, 1), (1, 0)])
    half = (keep + other).reshape(blocks * row_tasks, rows, pairs, row_block)
    parts = lax.all_to_all(half, ("blk", "ty"), 0, 0, tiled=True)
    out = jnp.sum(parts, axis=0)
    return jnp.transpose(out, (1, 0, 2)).reshape(pairs, rows * row_block)


def solution(mesh):
    blocks, tasks = mesh.shape["blk"], mesh.shape["task"]
    fine = Mesh(mesh.devices.reshape(blocks, tasks // 2, 2), EVERY)
    placed = (
        P("blk", TASK, None),
        P("blk", TASK, None, None, None, None),
        P(None, TASK, None, None),
        P(None, TASK, None, None),
        P(None, TASK, None),
    )
    return jax.shard_map(
        functools.partial(body, shape=(blocks, tasks // 2)),
        mesh=fine, in_specs=placed, out_specs=P("blk", TASK), check_vma=False,
    )
```

time: 1390 us -> 93.3 us (0.07)
  waiting for transfers between devices: 1330 us -> 25.5 us
    all_gather x1 -> x0, waiting for transfers between devices: 1240 us -> none  [body(): full_amplitudes = lax.all_gather(amplitudes, 'blk', axis=0, tiled=True)]
    reduce_scatter x2 -> x0, waiting for transfers between devices: 90.5 us -> none  [the longest x1 65.5 us: body(): lax.psum_scatter(shared_rows, 'blk', scatter_dimension=0, tiled=True)]
    all_to_all x1, waiting for transfers between devices: 0.01 us -> 23.6 us  [body(): lax.all_to_all(cut, EVERY, 0, 0, tiled=True)]
  transfers between devices with their start and end apart: 4 -> 2, of which waited for: 3 -> 2; matrix products, arithmetic and copies ran while one was open for 0% -> 19% of each run, Pallas kernels for 0% -> 0%
where the time goes in v1:
time: 93.3 us; the launch traced here: 92.4 us
  blocking collectives  27.4 us (29%)
  waiting for transfers between devices  25.5 us (27%)
  local copies, waits for them, and re-layouts  23.3 us (25%)
  Pallas kernels  8.45 us (9%)
  starting transfers between devices  7.37 us (8%)
    all_to_all x1, waiting for transfers between devices, body(): lax.all_to_all(cut, EVERY, 0, 0, tiled=True)  23.6 us
    all_to_all x1, blocking collectives, body(): parts = lax.all_to_all(half, ('blk', 'ty'), 0, 0, tiled=True)  20.3 us
    unnamed x9, local copies, waits for them, and re-layouts  13.6 us
    pallas_call x1, Pallas kernels, body(): pl.pallas_call(functools.partial(ladder_kernel, group=group, row_tasks=ro...  8.45 us
    all_to_all x1, starting transfers between devices, body(): lax.all_to_all(cut, EVERY, 0, 0, tiled=True)  7.3 us
    all_gather x1, blocking collectives, body(): lists = lax.all_gather(packed, TASK, axis=1, tiled=True)  7.14 us
    gather x1, local copies, waits for them, and re-layouts, body(): jnp.take(jnp.transpose(amplitudes, (1, 0, 2)), column, axis=0, mode='clip')  5.53 us
    transpose x1, local copies, waits for them, and re-layouts, body(): jnp.transpose(cut, (2, 0, 1, 3, 4))  3.2 us
  transfers between devices with their start and end apart: 2, of which 2 were waited for; matrix products, arithmetic and copies ran while one was open for 19% of the time, Pallas kernels for 0%

profile of v1, /device:TPU:0, one launch (start us, length us, event | category | flops | bytes accessed | tf_op | source)
XLA Modules:
  0.0 92.4 jit_solution(17685857454729914680)
XLA Ops:
  0.0 3.2 %copy.24 = bf16[8,4,2,128,128]{4,3,2,1,0:T(8,128)(2,1)} copy(bf16[8,4,2,128,128]{4,3,0,2,1:T(8,128)(2,1)} %bitcast.27) | data formatting | bytes 4194304 | tf_op jit(solution)/shard_map/transpose | solution.py:58
  3.2 0.0 copy-start.1
  3.2 0.0 copy-start.2
  3.2 0.0 copy-start.3
  3.2 7.3 %all-to-all-start = ((bf16[32,2,128,128]{3,2,1,0:T(8,128)(2,1)}), bf16[32,2,128,128]{3,2,1,0:T(8,128)(2,1)S(1)}, u32[]{:S(2)}, u32[]{:S(2)}) async-start(bf16[32,2,128,128]{3,2,1,0:T(8,128)(2,1)} %bitcast.25), calls=%async_computation | async-start | bytes 4194304 | tf_op jit(solution)/shard_map/all_to_all | solution.py:59
  10.5 0.0 copy-done.1
  10.5 0.0 copy-done.2
  10.5 0.0 copy-done.3
  10.6 7.1 %all_gather.3 = s32[8,4,4,2]{0,2,3,1:T(4,128)S(1)} all-gather(s32[8,1,4,2]{0,2,3,1:T(4,128)S(1)} %fusion.1), channel_id=1, replica_groups=mesh['blk'=8,'ty'=2,'core'=2] {'ty','core'}, dimensions={1}, use_global_device_ids=true | all-gather | bytes 1280 | tf_op jit(solution)/shard_map/all_gather | solution.py:64
  17.7 0.1 copy.21
  17.8 0.1 reshape.106
  17.9 0.1 reshape.107
  18.0 12.0 %copy.37 = bf16[128,256,128]{2,0,1:T(8,128)(2,1)} copy(bf16[128,256,128]{2,1,0:T(8,128)(2,1)} %param.5) | data formatting | bytes 16777216 | tf_op args[0]
  30.1 5.5 %gather_fusion = bf16[64,128,128]{2,1,0:T(8,128)(2,1)} fusion(bf16[256,128,128]{2,1,0:T(8,128)(2,1)} %bitcast.24, s32[1024]{0:T(1024)S(1)} %pad_clamp_fusion), kind=kCustom, calls=%fused_computation | custom fusion | bytes 4194560 | tf_op jit(solution)/shard_map/jit(_take)/gather | solution.py:70
  35.6 0.1 pad_add_fusion.meta
  35.7 23.6 %all-to-all-done = bf16[32,2,128,128]{3,2,1,0:T(8,128)(2,1)S(1)} async-done(((bf16[32,2,128,128]{3,2,1,0:T(8,128)(2,1)}), bf16[32,2,128,128]{3,2,1,0:T(8,128)(2,1)S(1)}, u32[]{:S(2)}, u32[]{:S(2)}) %all-to-all-start) | async-done | bytes 2097184 | tf_op jit(solution)/shard_map/all_to_all | solution.py:59
  59.3 0.0 copy-start
  59.3 1.6 %copy-done = bf16[64,128,128]{2,1,0:T(8,128)(2,1)S(1)} copy-done((bf16[64,128,128]{2,1,0:T(8,128)(2,1)S(1)}, bf16[64,128,128]{2,1,0:T(8,128)(2,1)}, u32[]{:S(2)}) %copy-start) | copy-done | bytes 2097176
  60.9 8.4 %ladder.1 = (f32[8,2,4,16,128]{4,3,2,1,0:T(8,128)S(1)}, f32[8,2,4,16,128]{4,3,2,1,0:T(8,128)S(1)}) custom-call(s32[129]{0:T(256)S(1)} %pad_add_fusion.meta, bf16[64,128,128]{2,1,0:T(8,128)(2,1)S(1)} %copy-done, bf16[64,128,128]{2,1,0:T(8,128)(2,1)S(1)} %bitcast.23), custom_call_target="tpu_custom_call" | custom-call | flops 268435456 | bytes 6291456 | tf_op jit(solution)/shard_map/ladder/pallas_call | solution.py:76
  69.3 0.1 collective-permute-start
  69.4 1.9 %collective-permute-done = f32[8,2,4,16,128]{4,3,2,1,0:T(8,128)S(1)} collective-permute-done((f32[8,2,4,16,128]{4,3,2,1,0:T(8,128)S(1)}, f32[8,2,4,16,128]{4,3,2,1,0:T(8,128)S(1)}, u32[]{:S(2)}, u32[]{:S(2)}) %collective-permute-start) | collective-permute-done | bytes 524320 | tf_op jit(solution)/shard_map/ppermute | solution.py:98
  71.3 0.1 add.41
  71.4 20.3 %all_to_all.10 = f32[16,4,16,128]{3,2,1,0:T(8,128)S(1)} all-to-all(f32[16,4,16,128]{3,2,1,0:T(8,128)S(1)} %bitcast.26), channel_id=1, replica_groups=mesh['blk'=8,'ty'=2,'core'=2] {'blk','ty'}, dimensions={0} | all-to-all | bytes 1048576 | tf_op jit(solution)/shard_map/all_to_all | solution.py:100
  91.7 0.6 copy_bitcast_fusion.1
  (6 shorter events, 0.1 us)
Async XLA Ops:
  3.2 7.3 %copy-start.1 = (s32[8,1,4,2]{0,3,2,1:T(2,128)S(1)}, s32[8,1,4,2]{0,3,2,1:T(2,128)}, u32[]{:S(2)}) copy-start(s32[8,1,4,2]{0,3,2,1:T(2,128)} %param.8) | copy-start | bytes 772
  3.2 7.3 %copy-start.2 = (s32[8,1,4,2]{0,3,2,1:T(2,128)S(1)}, s32[8,1,4,2]{0,3,2,1:T(2,128)}, u32[]{:S(2)}) copy-start(s32[8,1,4,2]{0,3,2,1:T(2,128)} %param.7) | copy-start | bytes 772
  3.2 7.3 %copy-start.3 = (s32[8,1,4]{0,2,1:T(4,128)S(1)}, s32[8,1,4]{0,2,1:T(4,128)}, u32[]{:S(2)}) copy-start(s32[8,1,4]{0,2,1:T(4,128)} %param.9) | copy-start | bytes 388
  3.2 56.1 %all-to-all-start = ((bf16[32,2,128,128]{3,2,1,0:T(8,128)(2,1)}), bf16[32,2,128,128]{3,2,1,0:T(8,128)(2,1)S(1)}, u32[]{:S(2)}, u32[]{:S(2)}) async-start(bf16[32,2,128,128]{3,2,1,0:T(8,128)(2,1)} %bitcast.25), calls=%async_computation | async-start | bytes 4194304 | tf_op jit(solution)/shard_map/all_to_all | solution.py:59
  59.3 1.6 %copy-start = (bf16[64,128,128]{2,1,0:T(8,128)(2,1)S(1)}, bf16[64,128,128]{2,1,0:T(8,128)(2,1)}, u32[]{:S(2)}) copy-start(bf16[64,128,128]{2,1,0:T(8,128)(2,1)} %gather_fusion) | copy-start | bytes 6291460
  69.3 2.0 %collective-permute-start = (f32[8,2,4,16,128]{4,3,2,1,0:T(8,128)S(1)}, f32[8,2,4,16,128]{4,3,2,1,0:T(8,128)S(1)}, u32[]{:S(2)}, u32[]{:S(2)}) collective-permute-start(f32[8,2,4,16,128]{4,3,2,1,0:T(8,128)S(1)} %get-tuple-element.8), channel_id=1, source_target_pairs={{0,1},{1,0},{2,3},{3,2},{4,5},{5,4},{6,7},{7,6},{8,9},{9,8},{10,11... | collective-permute-start | bytes 1572872 | tf_op jit(solution)/shard_map/ppermute | solution.py:98

commit v2 on v1

v2 whole, which is shorter than its diff:
```python
import functools

import jax
import jax.numpy as jnp
from jax import lax
from jax.experimental import pallas as pl
from jax.experimental.pallas import tpu as pltpu
from jax.sharding import Mesh, PartitionSpec as P

NRB = 16
TASK = ("ty", "core")
EVERY = ("blk", "ty", "core")


def pack_kernel(busy, first, second, out):
    chunk = first.shape[1]
    out[:, :chunk] = first[...]
    out[:, chunk:] = second[...]


def pack(integral_tiles, busy, blocks):
    tasks, _, virt_total, row_block = integral_tiles.shape[2:]
    chunk = virt_total // blocks
    piece = chunk // tasks
    flat = integral_tiles.reshape(tasks * 2, blocks, chunk, row_block)
    pieces = integral_tiles.reshape(tasks * 2, blocks, tasks, piece, row_block)
    return pl.pallas_call(
        pack_kernel,
        out_shape=jax.ShapeDtypeStruct((blocks, tasks, chunk + piece, row_block), flat.dtype),
        grid_spec=pltpu.PrefetchScalarGridSpec(
            num_scalar_prefetch=1,
            grid=(tasks,),
            in_specs=[
                pl.BlockSpec((None, blocks, chunk, row_block), lambda w, m: (2 * w, 0, 0, 0)),
                pl.BlockSpec((None, blocks, None, piece, row_block), lambda w, m: (2 * m[0] + 1, 0, w, 0, 0)),
            ],
            out_specs=pl.BlockSpec((blocks, None, chunk + piece, row_block), lambda w, m: (0, w, 0, 0)),
        ),
        compiler_params=pltpu.CompilerParams(vmem_limit_bytes=8 << 20),
        name="pack",
    )(busy, flat, pieces)


def ladder_kernel(meta, columns, extras, tiles, keep, send, total, *, row_tasks, pair_blocks):
    slots, _, chunk = columns.shape
    total[...] = jnp.zeros_like(total)

    def add_slots(step, carry):
        for part in range(4):
            n = step * 4 + part
            total[meta[n]] += jnp.dot(columns[n], tiles[n, :chunk], preferred_element_type=jnp.float32)
            total[meta[slots + n]] += jnp.dot(extras[n], tiles[n, chunk:], preferred_element_type=jnp.float32)
        return carry

    lax.fori_loop(0, slots // 4, add_slots, 0)

    core = meta[2 * slots]
    rows = NRB // (2 * row_tasks)
    pairs = total.shape[1] // pair_blocks
    for task in range(row_tasks):
        for block in range(pair_blocks):
            span = pl.ds(block * pairs, pairs)
            for row in range(rows):
                keep[block, task, row] = total[(2 * task + core) * rows + row, span, :]
                send[block, task, row] = total[(2 * task + 1 - core) * rows + row, span, :]


def body(amplitudes, integral_tiles, task_list, block_offsets, tile_counts, *, shape):
    blocks, row_tasks = shape
    tasks = 2 * row_tasks
    chunk, span, pair_total = amplitudes.shape
    row_block = integral_tiles.shape[5]
    slots = blocks * tasks
    piece = chunk // tasks
    rows, pairs = NRB // tasks, pair_total // blocks
    core = lax.axis_index("core").astype(jnp.int32)
    ty = lax.axis_index("ty").astype(jnp.int32)
    worker = ty * 2 + core

    busy = jnp.argmax(tile_counts[:, 0], axis=-1).astype(jnp.int32)
    own = lax.dynamic_slice_in_dim(busy, lax.axis_index("blk"), 1)
    sent = pack(integral_tiles, own, blocks).reshape(slots, chunk + piece, row_block)
    arrived = lax.all_to_all(sent, EVERY, 0, 0, tiled=True)

    lists = lax.all_gather(task_list * NRB + block_offsets, TASK, axis=1, tiled=True)
    mine = lax.dynamic_index_in_dim(lists, worker, 2, keepdims=False)
    is_busy = busy[:, None, None] == jnp.arange(tasks, dtype=jnp.int32)
    second_row = jnp.sum(jnp.where(is_busy, lists[..., 1] % NRB, 0), axis=-1)
    meta = jnp.concatenate([(mine[..., 0] % NRB).reshape(-1), second_row.reshape(-1), core[None]])

    virt = jnp.arange(span, dtype=jnp.int32)
    owner = (busy == worker)[:, None, None]
    hot = ((mine[..., 1] // NRB)[..., None] == virt) & owner
    held = jnp.einsum("nd,cdp->cnp", hot.reshape(slots, span).astype(amplitudes.dtype), amplitudes)
    held = held.reshape(row_tasks, 2, piece, slots, pair_total)
    here = lax.dynamic_index_in_dim(held, core, 1, keepdims=False)
    there = lax.dynamic_index_in_dim(held, 1 - core, 1, keepdims=False)
    merged = here + lax.ppermute(there, "core", [(0, 1), (1, 0)])
    extras = lax.dynamic_index_in_dim(merged, ty, 0, keepdims=False)
    for hop in range(1, row_tasks):
        away = lax.dynamic_index_in_dim(merged, lax.rem(ty + hop, row_tasks), 0, keepdims=False)
        extras += lax.ppermute(away, "ty", [(i, (i + hop) % row_tasks) for i in range(row_tasks)])
    extras = jnp.transpose(extras, (1, 2, 0))

    hot = (mine[..., 0] // NRB)[..., None] == virt
    columns = jnp.einsum("nd,cdp->npc", hot.reshape(slots, span).astype(amplitudes.dtype), amplitudes)

    part = jax.ShapeDtypeStruct((blocks, row_tasks, rows, pairs, row_block), jnp.float32)
    in_vmem = pl.BlockSpec(memory_space=pltpu.VMEM)
    keep, send = pl.pallas_call(
        functools.partial(ladder_kernel, row_tasks=row_tasks, pair_blocks=blocks),
        out_shape=(part, part),
        in_specs=[pl.BlockSpec(memory_space=pltpu.SMEM), in_vmem, in_vmem, in_vmem],
        out_specs=(in_vmem, in_vmem),
        scratch_shapes=[pltpu.VMEM((NRB, pair_total, row_block), jnp.float32)],
        compiler_params=pltpu.CompilerParams(vmem_limit_bytes=16 << 20),
        cost_estimate=pl.CostEstimate(
            flops=2 * slots * (chunk + piece) * pair_total * row_block,
            bytes_accessed=2 * slots * (chunk + piece) * (pair_total + row_block) + 4 * NRB * pair_total * row_block,
            transcendentals=0,
        ),
        name="ladder",
    )(meta, columns, extras, arrived)

    other = lax.ppermute(send, "core", [(0, 1), (1, 0)])
    half = (keep + other).reshape(blocks * row_tasks, rows, pairs, row_block)
    parts = lax.all_to_all(half, ("blk", "ty"), 0, 0, tiled=True)
    out = jnp.sum(parts, axis=0)
    return jnp.transpose(out, (1, 0, 2)).reshape(pairs, rows * row_block)


def solution(mesh):
    blocks, tasks = mesh.shape["blk"], mesh.shape["task"]
    fine = Mesh(mesh.devices.reshape(blocks, tasks // 2, 2), EVERY)
    placed = (
        P("blk", TASK, None),
        P("blk", TASK, None, None, None, None),
        P(None, TASK, None, None),
        P(None, TASK, None, None),
        P(None, TASK, None),
    )
    return jax.shard_map(
        functools.partial(body, shape=(blocks, tasks // 2)),
        mesh=fine, in_specs=placed, out_specs=P("blk", TASK), check_vma=False,
    )
```

time: 93.3 us -> 76.5 us (0.82)
  waiting for transfers between devices: 25.5 us -> 9.49 us
  local copies, waits for them, and re-layouts: 23.3 us -> 9.98 us
  matrix products: 0 us -> 10.9 us
  other arithmetic: 0.23 us -> 4.26 us
  Pallas kernels: 8.45 us -> 4.77 us
  starting transfers between devices: 7.37 us -> 9.26 us
    all_to_all x1, waiting for transfers between devices: 23.6 us -> 0.01 us  [body(): arrived = lax.all_to_all(sent, EVERY, 0, 0, tiled=True)]
    unnamed x9 -> x4, local copies, waits for them, and re-layouts: 13.6 us -> 2.27 us
    dot_general x0 -> x2, matrix products: none -> 10.9 us  [the longest x1 5.94 us: body(): jnp.einsum('nd,cdp->npc', hot.reshape(slots, span).astype(amplitudes.dtyp...]
    ppermute x0 -> x2, waiting for transfers between devices: none -> 7.6 us  [the longest x1 7.59 us: body(): lax.ppermute(away, 'ty', [(i, (i + hop) % row_tasks) for i in range(row_t...]
    gather x1 -> x0, local copies, waits for them, and re-layouts: 5.53 us -> none  [body(): jnp.take(jnp.transpose(amplitudes, (1, 0, 2)), column, axis=0, mode='clip')]
    pallas_call x1 -> x2, Pallas kernels: 8.45 us -> 4.77 us  [the longest x1 2.43 us: body(): pl.pallas_call(functools.partial(ladder_kernel, row_tasks=row_tasks, pair...]
    transpose x1 -> x0, local copies, waits for them, and re-layouts: 3.2 us -> none  [body(): jnp.transpose(cut, (2, 0, 1, 3, 4))]
    dot_general x0 -> x1, local copies, waits for them, and re-layouts: none -> 1.95 us  [body(): jnp.einsum('nd,cdp->npc', hot.reshape(slots, span).astype(amplitudes.dtyp...]
  transfers between devices with their start and end apart: 2 -> 4, of which waited for: 2 -> 2; matrix products, arithmetic and copies ran while one was open for 19% -> 28% of each run, Pallas kernels for 0% -> 0%
where the time goes in v2:
time: 76.5 us; the launch traced here: 76 us
  blocking collectives  27.3 us (36%)
  matrix products  10.9 us (14%)
  local copies, waits for them, and re-layouts  9.98 us (13%)
  waiting for transfers between devices  9.49 us (12%)
  starting transfers between devices  9.26 us (12%)
  Pallas kernels  4.77 us (6%)
  other arithmetic  4.26 us (6%)
    all_to_all x1, blocking collectives, body(): parts = lax.all_to_all(half, ('blk', 'ty'), 0, 0, tiled=True)  21.8 us
    ppermute x1, waiting for transfers between devices, body(): lax.ppermute(away, 'ty', [(i, (i + hop) % row_tasks) for i in range(row_t...  7.59 us
    all_to_all x1, starting transfers between devices, body(): arrived = lax.all_to_all(sent, EVERY, 0, 0, tiled=True)  7.3 us
    dot_general x1, matrix products, body(): jnp.einsum('nd,cdp->npc', hot.reshape(slots, span).astype(amplitudes.dtyp...  5.94 us
    all_gather x1, blocking collectives, body(): lax.all_gather(task_list * NRB + block_offsets, TASK, axis=1, tiled=True)  5.46 us
    dot_general x1, matrix products, body(): jnp.einsum('nd,cdp->cnp', hot.reshape(slots, span).astype(amplitudes.dtyp...  4.94 us
    pallas_call x1, Pallas kernels, body(): pl.pallas_call(functools.partial(ladder_kernel, row_tasks=row_tasks, pair...  2.43 us
    pallas_call x1, Pallas kernels, pack(): pl.pallas_call(pack_kernel, out_shape=jax.ShapeDtypeStruct((blocks, tasks...  2.34 us
  transfers between devices with their start and end apart: 4, of which 2 were waited for; matrix products, arithmetic and copies ran while one was open for 28% of the time, Pallas kernels for 0%

profile of v2, /device:TPU:0, one launch (start us, length us, event | category | flops | bytes accessed | tf_op | source)
XLA Modules:
  0.0 76.0 jit_solution(969189681240910257)
XLA Ops:
  0.0 0.0 copy-start
  0.0 0.7 copy-done
  0.7 0.5 bitcast_reduce_fusion
  1.2 0.6 dynamic_slice.26.busy
  1.8 0.0 copy-start.1
  1.8 1.6 %copy-done.1 = bf16[1,1,4,2,1024,128]{5,4,3,2,1,0:T(8,128)(2,1)S(1)} copy-done((bf16[1,1,4,2,1024,128]{5,4,3,2,1,0:T(8,128)(2,1)S(1)}, bf16[1,1,4,2,1024,128]{5,4,3,2,1,0:T(8,128)(2,1)}, u32[]{:S(2)}) %copy-start.1) | copy-done | bytes 2097176
  3.4 2.3 %pack.1 = bf16[8,4,160,128]{3,2,1,0:T(8,128)(2,1)} custom-call(s32[1]{0:T(128)} %dynamic_slice.26.busy, bf16[8,8,128,128]{3,2,1,0:T(8,128)(2,1)S(1)} %bitcast.52, bf16[8,8,4,32,128]{4,3,2,1,0:T(8,128)(2,1)S(1)} %bitcast.53), custom_call_target="tpu_custom_call" | custom-call | tf_op jit(solution)/shard_map/pack/pallas_call | solution.py:27
  5.7 7.3 %all-to-all-start = ((bf16[32,160,128]{2,1,0:T(8,128)(2,1)}), bf16[32,160,128]{2,1,0:T(8,128)(2,1)S(1)}, u32[]{:S(2)}, u32[]{:S(2)}) async-start(bf16[32,160,128]{2,1,0:T(8,128)(2,1)} %bitcast.17), calls=%async_computation | async-start | bytes 2621440 | tf_op jit(solution)/shard_map/all_to_all | solution.py:83
  13.0 0.7 copy_add_fusion
  13.8 5.5 %all_gather.3 = s32[8,4,4,2]{0,2,3,1:T(4,128)S(1)} all-gather(s32[8,1,4,2]{0,2,3,1:T(4,128)S(1)} %copy_add_fusion), channel_id=1, replica_groups=mesh['blk'=8,'ty'=2,'core'=2] {'ty','core'}, dimensions={1}, use_global_device_ids=true | all-gather | bytes 1280 | tf_op jit(solution)/shard_map/all_gather | solution.py:85
  19.3 0.1 and.47
  19.3 0.1 and.48
  19.4 0.1 copy.37
  19.5 0.1 eq.69
  19.6 4.9 %fusion.6 = bf16[32,128,128]{2,0,1:T(8,128)(2,1)S(1)} fusion(bf16[128,256,128]{2,1,0:T(8,128)(2,1)} %param.5, s32[32]{0:T(128)S(1)} %eq.69, pred[32]{0:T(512)(128)(4,1)S(1)} %and.48), kind=kOutput, calls=%fused_computation.12 | convolution fusion | flops 268451840 | bytes 9437344 | tf_op jit(solution)/shard_map/nd,cdp->cnp/dot_general | solution.py:94
  24.5 0.8 %dynamic-slice_bitcast_fusion = bf16[2,32,32,128]{3,2,1,0:T(8,128)(2,1)} fusion(bf16[2,2,32,32,128]{4,3,2,1,0:T(8,128)(2,1)S(1)} %bitcast.55, s32[]{:T(128)S(6)} %select_n.60), kind=kLoop, calls=%fused_computation.3 | loop fusion | bytes 1048580 | tf_op jit(solution)/shard_map/jit(dynamic_index_in_dim)/squeeze | solution.py:97
  25.4 0.3 collective-permute-start
  25.7 0.1 copy.34
  25.8 0.1 reshape.52
  25.9 0.1 copy.35
  26.0 0.1 eq.65
  26.1 0.1 copy.33
  26.1 0.1 squeeze.30
  26.2 5.9 %fusion.2 = bf16[32,128,128]{2,0,1:T(8,128)(2,1)} fusion(bf16[128,256,128]{2,1,0:T(8,128)(2,1)} %param.5, s32[32]{0:T(128)S(1)} %eq.65), kind=kOutput, calls=%fused_computation.9 | convolution fusion | flops 268443648 | bytes 9437312 | tf_op jit(solution)/shard_map/nd,cdp->npc/dot_general | solution.py:106
  32.2 1.9 %copy.36 = bf16[32,128,128]{1,2,0:T(8,128)(2,1)S(1)} copy(bf16[32,128,128]{2,0,1:T(8,128)(2,1)} %fusion.2) | data formatting | bytes 2097152 | tf_op jit(solution)/shard_map/nd,cdp->npc/dot_general | solution.py:106
  34.1 0.0 collective-permute-done
  34.1 1.1 %bitcast_add_fusion.1 = bf16[2,32,32,128]{3,2,1,0:T(8,128)(2,1)S(1)} fusion(bf16[2,32,32,128]{3,2,1,0:T(8,128)(2,1)} %collective-permute-done, bf16[2,2,32,32,128]{4,3,2,1,0:T(8,128)(2,1)S(1)} %bitcast.56, s32[]{:T(128)S(6)} %select_n.59), kind=kLoop, calls=%fused_computation.2 | loop fusion | flops 262144 | bytes 1572868 | tf_op jit(solution)/shard_map/add | solution.py:98
  35.3 1.6 %collective-permute-start.1 = (bf16[32,32,128]{2,1,0:T(8,128)(2,1)S(1)}, bf16[32,32,128]{2,1,0:T(8,128)(2,1)S(1)}, u32[]{:S(2)}, u32[]{:S(2)}) collective-permute-start(bf16[32,32,128]{2,1,0:T(8,128)(2,1)S(1)} %get-tuple-element.12), channel_id=1, source_target_pairs={{0,2},{2,0},{1,3},{3,1},{4,6},{6,4},{5,7},{7,5},{8,10},{10,8},{9,1... | collective-permute-start | bytes 786440 | tf_op jit(solution)/shard_map/ppermute | solution.py:102
  36.9 0.1 pad_add_fusion.meta
  37.0 1.4 %copy.38 = bf16[1,32,32,128]{1,3,2,0:T(8,128)(2,1)} copy(bf16[1,32,32,128]{3,2,1,0:T(8,128)(2,1)S(1)} %get-tuple-element.11) | data formatting | bytes 524288 | tf_op jit(solution)/shard_map/jit(dynamic_index_in_dim)/dynamic_slice | solution.py:99
  38.4 7.6 %collective-permute-done.1 = bf16[32,32,128]{2,1,0:T(8,128)(2,1)S(1)} collective-permute-done((bf16[32,32,128]{2,1,0:T(8,128)(2,1)S(1)}, bf16[32,32,128]{2,1,0:T(8,128)(2,1)S(1)}, u32[]{:S(2)}, u32[]{:S(2)}) %collective-permute-start.1) | collective-permute-done | bytes 262176 | tf_op jit(solution)/shard_map/ppermute | solution.py:102
  46.0 1.4 %copy.39 = bf16[32,32,128]{0,2,1:T(8,128)(2,1)} copy(bf16[32,32,128]{2,1,0:T(8,128)(2,1)S(1)} %collective-permute-done.1) | data formatting | bytes 524288 | tf_op jit(solution)/shard_map/ppermute | solution.py:102
  47.4 1.6 %fusion.extras = bf16[32,128,32]{2,1,0:T(8,128)(2,1)S(1)} fusion(bf16[32,32,128]{0,2,1:T(8,128)(2,1)} %copy.39, bf16[1,32,32,128]{1,3,2,0:T(8,128)(2,1)} %copy.38), kind=kLoop, calls=%fused_computation.1 | loop fusion | flops 131072 | bytes 786432 | tf_op jit(solution)/shard_map/transpose | solution.py:103
  49.0 0.0 all-to-all-done.tiles
  49.1 2.4 %ladder.1 = (f32[8,2,4,16,128]{4,3,2,1,0:T(8,128)S(1)}, f32[8,2,4,16,128]{4,3,2,1,0:T(8,128)S(1)}) custom-call(s32[65]{0:T(128)S(1)} %pad_add_fusion.meta, bf16[32,128,128]{2,1,0:T(8,128)(2,1)S(1)} %bitcast.54, bf16[32,128,32]{2,1,0:T(8,128)(2,1)S(1)} %fusion.extras, bf16[32,160,128]{2,1,0:T(8,128)(2,1)S(1)} %all-to-all-done.tiles), custom_call_target="tpu_custom_call" | custom-call | flops 167772160 | bytes 3670016 | tf_op jit(solution)/shard_map/ladder/pallas_call | solution.py:110
  51.5 0.1 collective-permute-start.2
  51.6 1.9 %collective-permute-done.2 = f32[8,2,4,16,128]{4,3,2,1,0:T(8,128)S(1)} collective-permute-done((f32[8,2,4,16,128]{4,3,2,1,0:T(8,128)S(1)}, f32[8,2,4,16,128]{4,3,2,1,0:T(8,128)S(1)}, u32[]{:S(2)}, u32[]{:S(2)}) %collective-permute-start.2) | collective-permute-done | bytes 524320 | tf_op jit(solution)/shard_map/ppermute | solution.py:125
  53.5 0.1 add.70
  53.6 21.8 %all_to_all.10 = f32[16,4,16,128]{3,2,1,0:T(8,128)S(1)} all-to-all(f32[16,4,16,128]{3,2,1,0:T(8,128)S(1)} %bitcast.57), channel_id=1, replica_groups=mesh['blk'=8,'ty'=2,'core'=2] {'blk','ty'}, dimensions={0} | all-to-all | bytes 1048576 | tf_op jit(solution)/shard_map/all_to_all | solution.py:127
  75.4 0.6 copy_bitcast_fusion
  (9 shorter events, 0.2 us)
Async XLA Ops:
  0.0 0.7 copy-start
  1.8 1.6 %copy-start.1 = (bf16[1,1,4,2,1024,128]{5,4,3,2,1,0:T(8,128)(2,1)S(1)}, bf16[1,1,4,2,1024,128]{5,4,3,2,1,0:T(8,128)(2,1)}, u32[]{:S(2)}) copy-start(bf16[1,1,4,2,1024,128]{5,4,3,2,1,0:T(8,128)(2,1)} %param.6) | copy-start | bytes 6291460
  5.7 43.3 %all-to-all-start = ((bf16[32,160,128]{2,1,0:T(8,128)(2,1)}), bf16[32,160,128]{2,1,0:T(8,128)(2,1)S(1)}, u32[]{:S(2)}, u32[]{:S(2)}) async-start(bf16[32,160,128]{2,1,0:T(8,128)(2,1)} %bitcast.17), calls=%async_computation | async-start | bytes 2621440 | tf_op jit(solution)/shard_map/all_to_all | solution.py:83
  25.4 8.7 %collective-permute-start = (bf16[2,32,32,128]{3,2,1,0:T(8,128)(2,1)}, bf16[2,32,32,128]{3,2,1,0:T(8,128)(2,1)}, u32[]{:S(2)}, u32[]{:S(2)}) collective-permute-start(bf16[2,32,32,128]{3,2,1,0:T(8,128)(2,1)} %dynamic-slice_bitcast_fusion), channel_id=1, source_target_pairs={{0,1},{1,0},{2,3},{3,2},{4,5},{5,4},{6,7},{7,6},{8,9},{9,8},{10,11... | collective-permute-start | bytes 1572872 | tf_op jit(solution)/shard_map/ppermute | solution.py:98
  35.3 10.7 %collective-permute-start.1 = (bf16[32,32,128]{2,1,0:T(8,128)(2,1)S(1)}, bf16[32,32,128]{2,1,0:T(8,128)(2,1)S(1)}, u32[]{:S(2)}, u32[]{:S(2)}) collective-permute-start(bf16[32,32,128]{2,1,0:T(8,128)(2,1)S(1)} %get-tuple-element.12), channel_id=1, source_target_pairs={{0,2},{2,0},{1,3},{3,1},{4,6},{6,4},{5,7},{7,5},{8,10},{10,8},{9,1... | collective-permute-start | bytes 786440 | tf_op jit(solution)/shard_map/ppermute | solution.py:102
  51.5 2.0 %collective-permute-start.2 = (f32[8,2,4,16,128]{4,3,2,1,0:T(8,128)S(1)}, f32[8,2,4,16,128]{4,3,2,1,0:T(8,128)S(1)}, u32[]{:S(2)}, u32[]{:S(2)}) collective-permute-start(f32[8,2,4,16,128]{4,3,2,1,0:T(8,128)S(1)} %get-tuple-element.10), channel_id=1, source_target_pairs={{0,1},{1,0},{2,3},{3,2},{4,5},{5,4},{6,7},{7,6},{8,9},{9,8},{10,11... | collective-permute-start | bytes 1572872 | tf_op jit(solution)/shard_map/ppermute | solution.py:125

commit v3 on v2

--- a/solution.py
+++ b/solution.py
@@ -12,33 +12,55 @@
 EVERY = ("blk", "ty", "core")
 
 
-def pack_kernel(busy, first, second, out):
-    chunk = first.shape[1]
-    out[:, :chunk] = first[...]
-    out[:, chunk:] = second[...]
+def pack_kernel(counts, tiles, pieces, out, first_sem, second_sem):
+    blocks, tasks, _, _ = out.shape
+    chunk = tiles.shape[2]
+    copies = [
+        pltpu.make_async_copy(tiles.at[2 * w], out.at[:, w, pl.ds(0, chunk)], first_sem.at[w])
+        for w in range(tasks)
+    ]
+    for copy in copies:
+        copy.start()
+    group = lax.axis_index("blk")
+    second = 1
+    for w in range(1, tasks):
+        second = jnp.where(counts[w, group] == 2, 2 * w + 1, second)
+    more = [
+        pltpu.make_async_copy(
+            pieces.at[second, :, w], out.at[:, w, pl.ds(chunk, pieces.shape[3])], second_sem.at[w]
+        )
+        for w in range(tasks)
+    ]
+    for copy in more:
+        copy.start()
+    for copy in copies + more:
+        copy.wait()
 
 
-def pack(integral_tiles, busy, blocks):
+def pack(integral_tiles, tile_counts, blocks):
     tasks, _, virt_total, row_block = integral_tiles.shape[2:]
     chunk = virt_total // blocks
     piece = chunk // tasks
-    flat = integral_tiles.reshape(tasks * 2, blocks, chunk, row_block)
+    tiles = integral_tiles.reshape(tasks * 2, blocks, chunk, row_block)
     pieces = integral_tiles.reshape(tasks * 2, blocks, tasks, piece, row_block)
+    counts = jnp.transpose(tile_counts[:, 0])
+    if piece % 16:
+        own = lax.dynamic_index_in_dim(counts, lax.axis_index("blk"), 1, keepdims=False)
+        second = lax.dynamic_index_in_dim(pieces, 2 * jnp.argmax(own) + 1, 0, keepdims=False)
+        return jnp.concatenate([jnp.swapaxes(tiles[::2], 0, 1), second], axis=2)
     return pl.pallas_call(
         pack_kernel,
-        out_shape=jax.ShapeDtypeStruct((blocks, tasks, chunk + piece, row_block), flat.dtype),
-        grid_spec=pltpu.PrefetchScalarGridSpec(
-            num_scalar_prefetch=1,
-            grid=(tasks,),
-            in_specs=[
-                pl.BlockSpec((None, blocks, chunk, row_block), lambda w, m: (2 * w, 0, 0, 0)),
-                pl.BlockSpec((None, blocks, None, piece, row_block), lambda w, m: (2 * m[0] + 1, 0, w, 0, 0)),
-            ],
-            out_specs=pl.BlockSpec((blocks, None, chunk + piece, row_block), lambda w, m: (0, w, 0, 0)),
-        ),
+        out_shape=jax.ShapeDtypeStruct((blocks, tasks, chunk + piece, row_block), tiles.dtype),
+        in_specs=[
+            pl.BlockSpec(memory_space=pltpu.SMEM),
+            pl.BlockSpec(memory_space=pl.ANY),
+            pl.BlockSpec(memory_space=pl.ANY),
+        ],
+        out_specs=pl.BlockSpec(memory_space=pltpu.VMEM),
+        scratch_shapes=[pltpu.SemaphoreType.DMA((tasks,)), pltpu.SemaphoreType.DMA((tasks,))],
         compiler_params=pltpu.CompilerParams(vmem_limit_bytes=8 << 20),
         name="pack",
-    )(busy, flat, pieces)
+    )(counts, tiles, pieces)
 
 
 def ladder_kernel(meta, columns, extras, tiles, keep, send, total, *, row_tasks, pair_blocks):
@@ -78,8 +100,7 @@
     worker = ty * 2 + core
 
     busy = jnp.argmax(tile_counts[:, 0], axis=-1).astype(jnp.int32)
-    own = lax.dynamic_slice_in_dim(busy, lax.axis_index("blk"), 1)
-    sent = pack(integral_tiles, own, blocks).reshape(slots, chunk + piece, row_block)
+    sent = pack(integral_tiles, tile_counts, blocks).reshape(slots, chunk + piece, row_block)
     arrived = lax.all_to_all(sent, EVERY, 0, 0, tiled=True)
 
     lists = lax.all_gather(task_list * NRB + block_offsets, TASK, axis=1, tiled=True)
@@ -102,7 +123,9 @@
         extras += lax.ppermute(away, "ty", [(i, (i + hop) % row_tasks) for i in range(row_tasks)])
     extras = jnp.transpose(extras, (1, 2, 0))
 
-    hot = (mine[..., 0] // NRB)[..., None] == virt
+    first = mine[..., 0] // NRB
+    first, _ = lax.optimization_barrier((first, merged))
+    hot = first[..., None] == virt
     columns = jnp.einsum("nd,cdp->npc", hot.reshape(slots, span).astype(amplitudes.dtype), amplitudes)
 
     part = jax.ShapeDtypeStruct((blocks, row_tasks, rows, pairs, row_block), jnp.float32)

time: 76.5 us -> 70.9 us (0.927)
  waiting for transfers between devices: 9.49 us -> 6.7 us
  starting transfers between devices: 9.26 us -> 7.75 us
  blocking collectives: 27.3 us -> 28.6 us
  matrix products: 10.9 us -> 9.87 us
    all_gather x1, blocking collectives: 5.46 us -> 9.92 us  [body(): lax.all_gather(task_list * NRB + block_offsets, TASK, axis=1, tiled=True)]
    ppermute x1, waiting for transfers between devices: 7.59 us -> 3.67 us  [body(): lax.ppermute(away, 'ty', [(i, (i + hop) % row_tasks) for i in range(row_t...]
    all_to_all x1, blocking collectives: 21.8 us -> 18.6 us  [body(): parts = lax.all_to_all(half, ('blk', 'ty'), 0, 0, tiled=True)]
    ppermute x1, starting transfers between devices: 1.58 us -> 0.01 us  [body(): lax.ppermute(away, 'ty', [(i, (i + hop) % row_tasks) for i in range(row_t...]
    ppermute x1, waiting for transfers between devices: 0.01 us -> 1.13 us  [body(): merged = here + lax.ppermute(there, 'core', [(0, 1), (1, 0)])]
    add x1, other arithmetic: 1.12 us -> 0.06 us  [body(): merged = here + lax.ppermute(there, 'core', [(0, 1), (1, 0)])]
    dot_general x1, matrix products: 5.94 us -> 4.93 us  [body(): jnp.einsum('nd,cdp->npc', hot.reshape(slots, span).astype(amplitudes.dtyp...]
    dot_general x1, local copies, waits for them, and re-layouts: 1.95 us -> 0.98 us  [body(): jnp.einsum('nd,cdp->npc', hot.reshape(slots, span).astype(amplitudes.dtyp...]
  transfers between devices with their start and end apart: 4 -> 4, of which waited for: 2 -> 3; matrix products, arithmetic and copies ran while one was open for 28% -> 28% of each run, Pallas kernels for 0% -> 0%
where the time goes in v3:
time: 70.9 us; the launch traced here: 70.4 us
  blocking collectives  28.6 us (40%)
  matrix products  9.87 us (14%)
  local copies, waits for them, and re-layouts  9.26 us (13%)
  starting transfers between devices  7.75 us (11%)
  waiting for transfers between devices  6.7 us (9%)
  Pallas kernels  4.3 us (6%)
  other arithmetic  3.89 us (5%)
    all_to_all x1, blocking collectives, body(): parts = lax.all_to_all(half, ('blk', 'ty'), 0, 0, tiled=True)  18.6 us
    all_gather x1, blocking collectives, body(): lax.all_gather(task_list * NRB + block_offsets, TASK, axis=1, tiled=True)  9.92 us
    all_to_all x1, starting transfers between devices, body(): arrived = lax.all_to_all(sent, EVERY, 0, 0, tiled=True)  7.3 us
    dot_general x1, matrix products, body(): jnp.einsum('nd,cdp->cnp', hot.reshape(slots, span).astype(amplitudes.dtyp...  4.94 us
    dot_general x1, matrix products, body(): jnp.einsum('nd,cdp->npc', hot.reshape(slots, span).astype(amplitudes.dtyp...  4.93 us
    ppermute x1, waiting for transfers between devices, body(): lax.ppermute(away, 'ty', [(i, (i + hop) % row_tasks) for i in range(row_t...  3.67 us
    pallas_call x1, Pallas kernels, body(): pl.pallas_call(functools.partial(ladder_kernel, row_tasks=row_tasks, pair...  2.45 us
    ppermute x1, local copies, waits for them, and re-layouts, body(): lax.ppermute(away, 'ty', [(i, (i + hop) % row_tasks) for i in range(row_t...  2.34 us
  transfers between devices with their start and end apart: 4, of which 3 were waited for; matrix products, arithmetic and copies ran while one was open for 28% of the time, Pallas kernels for 0%

profile of v3, /device:TPU:0, one launch (start us, length us, event | category | flops | bytes accessed | tf_op | source)
XLA Modules:
  0.0 70.4 jit_solution(6085113365602217245)
XLA Ops:
  0.0 0.0 copy-start
  0.0 1.6 %copy-done = bf16[1,1,4,2,1024,128]{5,4,3,2,1,0:T(8,128)(2,1)S(1)} copy-done((bf16[1,1,4,2,1024,128]{5,4,3,2,1,0:T(8,128)(2,1)S(1)}, bf16[1,1,4,2,1024,128]{5,4,3,2,1,0:T(8,128)(2,1)}, u32[]{:S(2)}) %copy-start) | copy-done | bytes 2097176
  1.6 0.0 copy-start.1
  1.6 0.7 copy-done.1
  2.3 1.8 %pack.1 = bf16[8,4,160,128]{3,2,1,0:T(8,128)(2,1)} custom-call(s32[4,8]{1,0:T(4,128)S(1)} %bitcast.71, bf16[8,8,128,128]{3,2,1,0:T(8,128)(2,1)S(1)} %bitcast.68, bf16[8,8,4,32,128]{4,3,2,1,0:T(8,128)(2,1)S(1)} %bitcast.69), custom_call_target="tpu_custom_call" | custom-call | tf_op jit(solution)/shard_map/pack/pallas_call | solution.py:51
  4.1 7.3 %all-to-all-start = ((bf16[32,160,128]{2,1,0:T(8,128)(2,1)}), bf16[32,160,128]{2,1,0:T(8,128)(2,1)S(1)}, u32[]{:S(2)}, u32[]{:S(2)}) async-start(bf16[32,160,128]{2,1,0:T(8,128)(2,1)} %bitcast.19), calls=%async_computation | async-start | bytes 2621440 | tf_op jit(solution)/shard_map/all_to_all | solution.py:104
  11.4 1.2 %bitcast_reduce_fusion = (s32[8]{0:T(128)}, s32[8]{0:T(128)S(1)}) fusion(s32[8,1,4]{0,2,1:T(4,128)} %param.9), kind=kLoop, calls=%fused_computation.41 | loop fusion | flops 168 | bytes 192 | tf_op jit(solution)/shard_map/body/reduce | solution.py:102
  12.7 0.1 and.44
  12.7 0.1 and.45
  12.8 0.7 %copy_add_fusion = s32[8,1,4,2]{0,2,3,1:T(4,128)S(1)} fusion(s32[8,1,4,2]{0,3,2,1:T(2,128)} %param.8, s32[8,1,4,2]{0,3,2,1:T(2,128)} %param.7), kind=kLoop, calls=%fused_computation.24 | loop fusion | flops 128 | bytes 768 | tf_op jit(solution)/shard_map/add | solution.py:106
  13.6 9.9 %all_gather.3 = s32[8,4,4,2]{0,2,3,1:T(4,128)S(1)} all-gather(s32[8,1,4,2]{0,2,3,1:T(4,128)S(1)} %copy_add_fusion), channel_id=1, replica_groups=mesh['blk'=8,'ty'=2,'core'=2] {'ty','core'}, dimensions={1}, use_global_device_ids=true | all-gather | bytes 1280 | tf_op jit(solution)/shard_map/all_gather | solution.py:106
  23.5 0.1 copy.35
  23.6 0.1 eq.65
  23.7 4.9 %fusion.3 = bf16[32,128,128]{2,0,1:T(8,128)(2,1)S(1)} fusion(bf16[128,256,128]{2,1,0:T(8,128)(2,1)} %param.5, s32[32]{0:T(128)S(1)} %eq.65, pred[32]{0:T(512)(128)(4,1)S(1)} %and.45), kind=kOutput, calls=%fused_computation.10 | convolution fusion | flops 268451840 | bytes 9437344 | tf_op jit(solution)/shard_map/nd,cdp->cnp/dot_general | solution.py:115
  28.7 0.4 collective-permute-start
  29.1 0.1 copy.34
  29.1 0.1 reshape.53
  29.2 0.1 copy.33
  29.3 0.1 squeeze.33
  29.4 0.1 pad_add_fusion.meta
  29.5 1.1 %collective-permute-done = bf16[2,32,32,128]{3,2,1,0:T(8,128)(2,1)S(1)} collective-permute-done((bf16[2,32,32,128]{3,2,1,0:T(8,128)(2,1)S(1)}, bf16[2,32,32,128]{3,2,1,0:T(8,128)(2,1)S(1)}, u32[]{:S(2)}, u32[]{:S(2)}) %collective-permute-start) | collective-permute-done | bytes 524320 | tf_op jit(solution)/shard_map/ppermute | solution.py:119
  30.6 0.1 bitcast_add_fusion.1
  30.7 0.1 copy.36
  30.8 0.1 eq.71
  30.9 0.7 %constant_dynamic-slice_fusion = (bf16[1,32,32,128]{3,2,1,0:T(8,128)(2,1)S(1)}, bf16[32,32,128]{2,1,0:T(8,128)(2,1)}) fusion(bf16[2,32,32,128]{3,2,1,0:T(8,128)(2,1)S(1)} %bitcast_add_fusion.1, s32[]{:T(128)S(6)} %select_n.57, s32[]{:T(128)S(6)} %select_n.58), kind=kLoop, calls=%fused_computation.47 | loop fusion | bytes 1048584 | tf_op jit(solution)/shard_map/jit(dynamic_index_in_dim)/dynamic_slice | solution.py:120
  31.6 0.0 collective-permute-start.1
  31.6 4.9 %fusion.6 = bf16[32,128,128]{2,0,1:T(8,128)(2,1)S(1)} fusion(bf16[128,256,128]{2,1,0:T(8,128)(2,1)} %param.5, s32[32]{0:T(128)S(1)} %eq.71), kind=kOutput, calls=%fused_computation.12 | convolution fusion | flops 268443648 | bytes 9437312 | tf_op jit(solution)/shard_map/nd,cdp->npc/dot_general | solution.py:129
  36.5 1.4 %copy.38 = bf16[1,32,32,128]{1,3,2,0:T(8,128)(2,1)} copy(bf16[1,32,32,128]{3,2,1,0:T(8,128)(2,1)S(1)} %get-tuple-element.13) | data formatting | bytes 524288 | tf_op jit(solution)/shard_map/jit(dynamic_index_in_dim)/dynamic_slice | solution.py:120
  38.0 1.0 %copy.37 = bf16[32,128,128]{1,2,0:T(8,128)(2,1)S(1)} copy(bf16[32,128,128]{2,0,1:T(8,128)(2,1)S(1)} %fusion.6) | data formatting | bytes 2097152 | tf_op jit(solution)/shard_map/nd,cdp->npc/dot_general | solution.py:129
  39.0 3.7 %collective-permute-done.1 = bf16[32,32,128]{2,1,0:T(8,128)(2,1)} collective-permute-done((bf16[32,32,128]{2,1,0:T(8,128)(2,1)}, bf16[32,32,128]{2,1,0:T(8,128)(2,1)}, u32[]{:S(2)}, u32[]{:S(2)}) %collective-permute-start.1) | collective-permute-done | bytes 262176 | tf_op jit(solution)/shard_map/ppermute | solution.py:123
  42.6 2.3 %copy.39 = bf16[32,32,128]{0,2,1:T(8,128)(2,1)} copy(bf16[32,32,128]{2,1,0:T(8,128)(2,1)} %collective-permute-done.1) | data formatting | bytes 524288 | tf_op jit(solution)/shard_map/ppermute | solution.py:123
  45.0 1.6 %fusion.extras = bf16[32,128,32]{2,1,0:T(8,128)(2,1)S(1)} fusion(bf16[32,32,128]{0,2,1:T(8,128)(2,1)} %copy.39, bf16[1,32,32,128]{1,3,2,0:T(8,128)(2,1)} %copy.38), kind=kLoop, calls=%fused_computation.1 | loop fusion | flops 131072 | bytes 786432 | tf_op jit(solution)/shard_map/transpose | solution.py:124
  46.6 0.0 all-to-all-done.tiles
  46.6 2.5 %ladder.1 = (f32[8,2,4,16,128]{4,3,2,1,0:T(8,128)S(1)}, f32[8,2,4,16,128]{4,3,2,1,0:T(8,128)S(1)}) custom-call(s32[65]{0:T(128)S(1)} %pad_add_fusion.meta, bf16[32,128,128]{2,1,0:T(8,128)(2,1)S(1)} %bitcast.70, bf16[32,128,32]{2,1,0:T(8,128)(2,1)S(1)} %fusion.extras, bf16[32,160,128]{2,1,0:T(8,128)(2,1)S(1)} %all-to-all-done.tiles), custom_call_target="tpu_custom_call" | custom-call | flops 167772160 | bytes 3670016 | tf_op jit(solution)/shard_map/ladder/pallas_call | solution.py:133
  49.1 0.1 collective-permute-start.2
  49.2 1.9 %collective-permute-done.2 = f32[8,2,4,16,128]{4,3,2,1,0:T(8,128)S(1)} collective-permute-done((f32[8,2,4,16,128]{4,3,2,1,0:T(8,128)S(1)}, f32[8,2,4,16,128]{4,3,2,1,0:T(8,128)S(1)}, u32[]{:S(2)}, u32[]{:S(2)}) %collective-permute-start.2) | collective-permute-done | bytes 524320 | tf_op jit(solution)/shard_map/ppermute | solution.py:148
  51.1 0.1 add.65
  51.1 18.6 %all_to_all.10 = f32[16,4,16,128]{3,2,1,0:T(8,128)S(1)} all-to-all(f32[16,4,16,128]{3,2,1,0:T(8,128)S(1)} %bitcast.74), channel_id=1, replica_groups=mesh['blk'=8,'ty'=2,'core'=2] {'blk','ty'}, dimensions={0} | all-to-all | bytes 1048576 | tf_op jit(solution)/shard_map/all_to_all | solution.py:150
  69.8 0.6 copy_bitcast_fusion
  (10 shorter events, 0.2 us)
Async XLA Ops:
  0.0 1.6 %copy-start = (bf16[1,1,4,2,1024,128]{5,4,3,2,1,0:T(8,128)(2,1)S(1)}, bf16[1,1,4,2,1024,128]{5,4,3,2,1,0:T(8,128)(2,1)}, u32[]{:S(2)}) copy-start(bf16[1,1,4,2,1024,128]{5,4,3,2,1,0:T(8,128)(2,1)} %param.6) | copy-start | bytes 6291460
  1.6 0.7 copy-start.1
  4.1 42.5 %all-to-all-start = ((bf16[32,160,128]{2,1,0:T(8,128)(2,1)}), bf16[32,160,128]{2,1,0:T(8,128)(2,1)S(1)}, u32[]{:S(2)}, u32[]{:S(2)}) async-start(bf16[32,160,128]{2,1,0:T(8,128)(2,1)} %bitcast.19), calls=%async_computation | async-start | bytes 2621440 | tf_op jit(solution)/shard_map/all_to_all | solution.py:104
  28.7 2.0 %collective-permute-start = (bf16[2,32,32,128]{3,2,1,0:T(8,128)(2,1)S(1)}, bf16[2,32,32,128]{3,2,1,0:T(8,128)(2,1)S(1)}, u32[]{:S(2)}, u32[]{:S(2)}) collective-permute-start(bf16[2,32,32,128]{3,2,1,0:T(8,128)(2,1)S(1)} %dynamic-slice_bitcast_fusion), channel_id=1, source_target_pairs={{0,1},{1,0},{2,3},{3,2},{4,5},{5,4},{6,7},{7,6},{8,9},{9,8},{10,11... | collective-permute-start | bytes 1572872 | tf_op jit(solution)/shard_map/ppermute | solution.py:119
  31.6 11.0 %collective-permute-start.1 = (bf16[32,32,128]{2,1,0:T(8,128)(2,1)}, bf16[32,32,128]{2,1,0:T(8,128)(2,1)}, u32[]{:S(2)}, u32[]{:S(2)}) collective-permute-start(bf16[32,32,128]{2,1,0:T(8,128)(2,1)} %get-tuple-element.14), channel_id=1, source_target_pairs={{0,2},{2,0},{1,3},{3,1},{4,6},{6,4},{5,7},{7,5},{8,10},{10,8},{9,1... | collective-permute-start | bytes 786440 | tf_op jit(solution)/shard_map/ppermute | solution.py:123
  49.1 2.0 %collective-permute-start.2 = (f32[8,2,4,16,128]{4,3,2,1,0:T(8,128)S(1)}, f32[8,2,4,16,128]{4,3,2,1,0:T(8,128)S(1)}, u32[]{:S(2)}, u32[]{:S(2)}) collective-permute-start(f32[8,2,4,16,128]{4,3,2,1,0:T(8,128)S(1)} %get-tuple-element.12), channel_id=1, source_target_pairs={{0,1},{1,0},{2,3},{3,2},{4,5},{5,4},{6,7},{7,6},{8,9},{9,8},{10,11... | collective-permute-start | bytes 1572872 | tf_op jit(solution)/shard_map/ppermute | solution.py:148

commit v4 on v3

--- a/solution.py
+++ b/solution.py
@@ -12,28 +12,34 @@
 EVERY = ("blk", "ty", "core")
 
 
-def pack_kernel(counts, tiles, pieces, out, first_sem, second_sem):
-    blocks, tasks, _, _ = out.shape
+def pack_kernel(counts, tiles, pieces, out, held, busy, first_sem, second_sem, out_sem, count_sem):
+    tasks, _, rows, _ = held.shape
     chunk = tiles.shape[2]
-    copies = [
-        pltpu.make_async_copy(tiles.at[2 * w], out.at[:, w, pl.ds(0, chunk)], first_sem.at[w])
+    count_copy = pltpu.make_async_copy(counts, busy, count_sem)
+    count_copy.start()
+    first = [
+        pltpu.make_async_copy(tiles.at[2 * w], held.at[w, :, pl.ds(0, chunk)], first_sem.at[w])
         for w in range(tasks)
     ]
-    for copy in copies:
+    for copy in first:
         copy.start()
+    count_copy.wait()
     group = lax.axis_index("blk")
-    second = 1
+    tile = 1
     for w in range(1, tasks):
-        second = jnp.where(counts[w, group] == 2, 2 * w + 1, second)
-    more = [
-        pltpu.make_async_copy(
-            pieces.at[second, :, w], out.at[:, w, pl.ds(chunk, pieces.shape[3])], second_sem.at[w]
-        )
+        tile = jnp.where(busy[w, group] == 2, 2 * w + 1, tile)
+    second = [
+        pltpu.make_async_copy(pieces.at[tile, :, w], held.at[w, :, pl.ds(chunk, rows - chunk)], second_sem.at[w])
         for w in range(tasks)
     ]
-    for copy in more:
+    for copy in second:
         copy.start()
-    for copy in copies + more:
+    leave = [pltpu.make_async_copy(held.at[w], out.at[:, w], out_sem.at[w]) for w in range(tasks)]
+    for w in range(tasks):
+        first[w].wait()
+        second[w].wait()
+        leave[w].start()
+    for copy in leave:
         copy.wait()
 
 
@@ -51,19 +57,89 @@
     return pl.pallas_call(
         pack_kernel,
         out_shape=jax.ShapeDtypeStruct((blocks, tasks, chunk + piece, row_block), tiles.dtype),
-        in_specs=[
-            pl.BlockSpec(memory_space=pltpu.SMEM),
-            pl.BlockSpec(memory_space=pl.ANY),
-            pl.BlockSpec(memory_space=pl.ANY),
-        ],
-        out_specs=pl.BlockSpec(memory_space=pltpu.VMEM),
-        scratch_shapes=[pltpu.SemaphoreType.DMA((tasks,)), pltpu.SemaphoreType.DMA((tasks,))],
-        compiler_params=pltpu.CompilerParams(vmem_limit_bytes=8 << 20),
+        in_specs=[pl.BlockSpec(memory_space=pl.ANY)] * 3,
+        out_specs=pl.BlockSpec(memory_space=pl.ANY),
+        scratch_shapes=[
+            pltpu.VMEM((tasks, blocks, chunk + piece, row_block), tiles.dtype),
+            pltpu.SMEM(counts.shape, counts.dtype),
+        ]
+        + [pltpu.SemaphoreType.DMA((tasks,))] * 3
+        + [pltpu.SemaphoreType.DMA],
+        compiler_params=pltpu.CompilerParams(vmem_limit_bytes=58 << 20),
         name="pack",
     )(counts, tiles, pieces)
 
 
-def ladder_kernel(meta, columns, extras, tiles, keep, send, total, *, row_tasks, pair_blocks):
+def pick_kernel(column, amplitudes, here, there, held, hot, picked, sems):
+    row_tasks, slots, piece, _ = here.shape
+    span = hot.shape[1]
+    parts = sems.shape[1]
+    core = lax.axis_index("core")
+
+    def task_of(step):
+        return 2 * lax.rem(step, row_tasks) + lax.rem(core + 1 + step // row_tasks, 2)
+
+    def copy_of(step, part):
+        rows = pl.ds(task_of(step) * piece + part * (piece // parts), piece // parts)
+        return pltpu.make_async_copy(amplitudes.at[rows], held.at[rows], sems.at[step, part])
+
+    for step in range(2 * row_tasks):
+        for part in range(parts):
+            copy_of(step, part).start()
+
+    lane = lax.broadcasted_iota(jnp.int32, (1, span), 1)
+    for n in range(slots):
+        hot[pl.ds(n, 1), :] = jnp.where(lane == column[n], 1.0, 0.0)
+    chosen = hot[...].astype(held.dtype)
+
+    def one_task(step, out, row_task):
+        for part in range(parts):
+            copy_of(step, part).wait()
+        base = task_of(step) * piece
+        for c in range(piece):
+            picked[c] = jnp.dot(chosen, held[base + c], preferred_element_type=jnp.float32)
+        for n in range(slots):
+            out[row_task, n] = picked[:, n, :].astype(out.dtype)
+
+    @pl.loop(0, row_tasks)
+    def _(step):
+        one_task(step, there, step)
+
+    @pl.loop(0, row_tasks)
+    def _(step):
+        one_task(row_tasks + step, here, step)
+
+
+def pick(column, amplitudes, row_tasks):
+    chunk, span, pair_total = amplitudes.shape
+    slots = column.shape[0]
+    piece = chunk // (2 * row_tasks)
+    parts = 4
+    part = jax.ShapeDtypeStruct((row_tasks, slots, piece, pair_total), amplitudes.dtype)
+    in_vmem = pl.BlockSpec(memory_space=pltpu.VMEM)
+    return pl.pallas_call(
+        pick_kernel,
+        out_shape=(part, part),
+        in_specs=[pl.BlockSpec(memory_space=pltpu.SMEM), pl.BlockSpec(memory_space=pl.ANY)],
+        out_specs=(in_vmem, in_vmem),
+        scratch_shapes=[
+            pltpu.VMEM(amplitudes.shape, amplitudes.dtype),
+            pltpu.VMEM((slots, span), jnp.float32),
+            pltpu.VMEM((piece, slots, pair_total), jnp.float32),
+            pltpu.SemaphoreType.DMA((2 * row_tasks, parts)),
+        ],
+        compiler_params=pltpu.CompilerParams(vmem_limit_bytes=58 << 20),
+        cost_estimate=pl.CostEstimate(
+            flops=2 * slots * chunk * span * pair_total,
+            bytes_accessed=2 * chunk * (span + slots) * pair_total,
+            transcendentals=0,
+        ),
+        name="pick",
+    )(column, amplitudes)
+
+
+def ladder_kernel(meta, columns, here, other_core, other_row, tiles, keep, send, total, *, row_tasks, pair_blocks):
+    mine = meta[2 * columns.shape[0] + 1]
     slots, _, chunk = columns.shape
     total[...] = jnp.zeros_like(total)
 
@@ -71,7 +147,10 @@
         for part in range(4):
             n = step * 4 + part
             total[meta[n]] += jnp.dot(columns[n], tiles[n, :chunk], preferred_element_type=jnp.float32)
-            total[meta[slots + n]] += jnp.dot(extras[n], tiles[n, chunk:], preferred_element_type=jnp.float32)
+            second = here[mine, n] + other_core[mine, n] + other_row[n]
+            total[meta[slots + n]] += lax.dot_general(
+                second, tiles[n, chunk:], (((0,), (0,)), ((), ())), preferred_element_type=jnp.float32
+            )
         return carry
 
     lax.fori_loop(0, slots // 4, add_slots, 0)
@@ -99,32 +178,30 @@
     ty = lax.axis_index("ty").astype(jnp.int32)
     worker = ty * 2 + core
 
-    busy = jnp.argmax(tile_counts[:, 0], axis=-1).astype(jnp.int32)
     sent = pack(integral_tiles, tile_counts, blocks).reshape(slots, chunk + piece, row_block)
     arrived = lax.all_to_all(sent, EVERY, 0, 0, tiled=True)
 
     lists = lax.all_gather(task_list * NRB + block_offsets, TASK, axis=1, tiled=True)
+    counts, lists = lax.optimization_barrier((tile_counts, lists))
+    busy = jnp.argmax(counts[:, 0], axis=-1).astype(jnp.int32)
     mine = lax.dynamic_index_in_dim(lists, worker, 2, keepdims=False)
     is_busy = busy[:, None, None] == jnp.arange(tasks, dtype=jnp.int32)
     second_row = jnp.sum(jnp.where(is_busy, lists[..., 1] % NRB, 0), axis=-1)
-    meta = jnp.concatenate([(mine[..., 0] % NRB).reshape(-1), second_row.reshape(-1), core[None]])
+    meta = jnp.concatenate([(mine[..., 0] % NRB).reshape(-1), second_row.reshape(-1), core[None], ty[None]])
 
     virt = jnp.arange(span, dtype=jnp.int32)
-    owner = (busy == worker)[:, None, None]
-    hot = ((mine[..., 1] // NRB)[..., None] == virt) & owner
-    held = jnp.einsum("nd,cdp->cnp", hot.reshape(slots, span).astype(amplitudes.dtype), amplitudes)
-    held = held.reshape(row_tasks, 2, piece, slots, pair_total)
-    here = lax.dynamic_index_in_dim(held, core, 1, keepdims=False)
-    there = lax.dynamic_index_in_dim(held, 1 - core, 1, keepdims=False)
-    merged = here + lax.ppermute(there, "core", [(0, 1), (1, 0)])
-    extras = lax.dynamic_index_in_dim(merged, ty, 0, keepdims=False)
+    owner = (busy == worker)[:, None]
+    column = jnp.where(owner, mine[..., 1] // NRB, span).reshape(-1)
+    here, there = pick(column, amplitudes, row_tasks)
+    other_core = lax.ppermute(there, "core", [(0, 1), (1, 0)])
+    other_row = 0
     for hop in range(1, row_tasks):
-        away = lax.dynamic_index_in_dim(merged, lax.rem(ty + hop, row_tasks), 0, keepdims=False)
-        extras += lax.ppermute(away, "ty", [(i, (i + hop) % row_tasks) for i in range(row_tasks)])
-    extras = jnp.transpose(extras, (1, 2, 0))
+        to = lax.rem(ty + hop, row_tasks)
+        away = lax.dynamic_index_in_dim(here, to, 0, False) + lax.dynamic_index_in_dim(other_core, to, 0, False)
+        other_row += lax.ppermute(away, "ty", [(i, (i + hop) % row_tasks) for i in range(row_tasks)])
 
     first = mine[..., 0] // NRB
-    first, _ = lax.optimization_barrier((first, merged))
+    first, _ = lax.optimization_barrier((first, other_core))
     hot = first[..., None] == virt
     columns = jnp.einsum("nd,cdp->npc", hot.reshape(slots, span).astype(amplitudes.dtype), amplitudes)
 
@@ -133,7 +210,7 @@
     keep, send = pl.pallas_call(
         functools.partial(ladder_kernel, row_tasks=row_tasks, pair_blocks=blocks),
         out_shape=(part, part),
-        in_specs=[pl.BlockSpec(memory_space=pltpu.SMEM), in_vmem, in_vmem, in_vmem],
+        in_specs=[pl.BlockSpec(memory_space=pltpu.SMEM)] + [in_vmem] * 5,
         out_specs=(in_vmem, in_vmem),
         scratch_shapes=[pltpu.VMEM((NRB, pair_total, row_block), jnp.float32)],
         compiler_params=pltpu.CompilerParams(vmem_limit_bytes=16 << 20),
@@ -143,7 +220,7 @@
             transcendentals=0,
         ),
         name="ladder",
-    )(meta, columns, extras, arrived)
+    )(meta, columns, here, other_core, other_row, arrived)
 
     other = lax.ppermute(send, "core", [(0, 1), (1, 0)])
     half = (keep + other).reshape(blocks * row_tasks, rows, pairs, row_block)

time: 70.9 us -> 69.6 us (0.982)
  Pallas kernels: 4.3 us -> 12.5 us
  local copies, waits for them, and re-layouts: 9.26 us -> 3.4 us
  matrix products: 9.87 us -> 5.93 us
  blocking collectives: 28.6 us -> 26.5 us
  starting transfers between devices: 7.75 us -> 9.26 us
    pallas_call x0 -> x1, Pallas kernels: none -> 6.36 us  [pick(): pl.pallas_call(pick_kernel, out_shape=(part, part), in_specs=[pl.BlockSpe...]
    dot_general x1 -> x0, matrix products: 4.94 us -> none  [body(): jnp.einsum('nd,cdp->cnp', hot.reshape(slots, span).astype(amplitudes.dtyp...]
    all_gather x1, blocking collectives: 9.92 us -> 5.46 us  [body(): lax.all_gather(task_list * NRB + block_offsets, TASK, axis=1, tiled=True)]
    ppermute x1, waiting for transfers between devices: 3.67 us -> 1.05 us  [body(): lax.ppermute(away, 'ty', [(i, (i + hop) % row_tasks) for i in range(row_t...]
    all_to_all x1, waiting for transfers between devices: 0.01 us -> 2.62 us  [body(): arrived = lax.all_to_all(sent, EVERY, 0, 0, tiled=True)]
    all_to_all x1, blocking collectives: 18.6 us -> 21 us  [body(): parts = lax.all_to_all(half, ('blk', 'ty'), 0, 0, tiled=True)]
    ppermute x1 -> x0, local copies, waits for them, and re-layouts: 2.34 us -> none  [body(): lax.ppermute(away, 'ty', [(i, (i + hop) % row_tasks) for i in range(row_t...]
    unnamed x4 -> x2, local copies, waits for them, and re-layouts: 2.27 us -> 0.01 us
  transfers between devices with their start and end apart: 4 -> 4, of which waited for: 3 -> 4; matrix products, arithmetic and copies ran while one was open for 28% -> 19% of each run, Pallas kernels for 0% -> 9%
where the time goes in v4:
time: 69.6 us; the launch traced here: 69.2 us
  blocking collectives  26.5 us (38%)
  Pallas kernels  12.5 us (18%)
  starting transfers between devices  9.26 us (13%)
  waiting for transfers between devices  6.91 us (10%)
  matrix products  5.93 us (9%)
  other arithmetic  4.51 us (6%)
  local copies, waits for them, and re-layouts  3.4 us (5%)
    all_to_all x1, blocking collectives, body(): parts = lax.all_to_all(half, ('blk', 'ty'), 0, 0, tiled=True)  21 us
    all_to_all x1, starting transfers between devices, body(): arrived = lax.all_to_all(sent, EVERY, 0, 0, tiled=True)  7.3 us
    pallas_call x1, Pallas kernels, pick(): pl.pallas_call(pick_kernel, out_shape=(part, part), in_specs=[pl.BlockSpe...  6.36 us
    dot_general x1, matrix products, body(): jnp.einsum('nd,cdp->npc', hot.reshape(slots, span).astype(amplitudes.dtyp...  5.93 us
    all_gather x1, blocking collectives, body(): lax.all_gather(task_list * NRB + block_offsets, TASK, axis=1, tiled=True)  5.46 us
    pallas_call x1, Pallas kernels, body(): pl.pallas_call(functools.partial(ladder_kernel, row_tasks=row_tasks, pair...  3.25 us
    pallas_call x1, Pallas kernels, pack(): pl.pallas_call(pack_kernel, out_shape=jax.ShapeDtypeStruct((blocks, tasks...  2.93 us
    all_to_all x1, waiting for transfers between devices, body(): arrived = lax.all_to_all(sent, EVERY, 0, 0, tiled=True)  2.62 us
  transfers between devices with their start and end apart: 4, of which 4 were waited for; matrix products, arithmetic and copies ran while one was open for 19% of the time, Pallas kernels for 9%

profile of v4, /device:TPU:0, one launch (start us, length us, event | category | flops | bytes accessed | tf_op | source)
XLA Modules:
  0.0 69.2 jit_solution(7155814027820811634)
XLA Ops:
  0.0 2.9 %pack.1 = bf16[8,4,160,128]{3,2,1,0:T(8,128)(2,1)} custom-call(s32[4,8]{1,0:T(4,128)} %bitcast.58, bf16[8,8,128,128]{3,2,1,0:T(8,128)(2,1)} %bitcast.52, bf16[8,8,4,32,128]{4,3,2,1,0:T(8,128)(2,1)} %bitcast.53), custom_call_target="tpu_custom_call" | custom-call | tf_op jit(solution)/shard_map/pack/pallas_call | solution.py:57
  2.9 7.3 %all-to-all-start = ((bf16[32,160,128]{2,1,0:T(8,128)(2,1)}), bf16[32,160,128]{2,1,0:T(8,128)(2,1)S(1)}, u32[]{:S(2)}, u32[]{:S(2)}) async-start(bf16[32,160,128]{2,1,0:T(8,128)(2,1)} %bitcast.54), calls=%async_computation | async-start | bytes 2621440 | tf_op jit(solution)/shard_map/all_to_all | solution.py:182
  10.3 0.7 %copy_add_fusion = s32[8,1,4,2]{0,2,3,1:T(4,128)S(1)} fusion(s32[8,1,4,2]{0,3,2,1:T(2,128)} %param.8, s32[8,1,4,2]{0,3,2,1:T(2,128)} %param.7), kind=kLoop, calls=%fused_computation.13 | loop fusion | flops 128 | bytes 768 | tf_op jit(solution)/shard_map/add | solution.py:184
  11.0 5.5 %all_gather.3 = s32[8,4,4,2]{0,2,3,1:T(4,128)S(1)} all-gather(s32[8,1,4,2]{0,2,3,1:T(4,128)S(1)} %copy_add_fusion), channel_id=1, replica_groups=mesh['blk'=8,'ty'=2,'core'=2] {'ty','core'}, dimensions={1}, use_global_device_ids=true | all-gather | bytes 1280 | tf_op jit(solution)/shard_map/all_gather | solution.py:184
  16.4 1.2 %bitcast_reduce_fusion = (s32[8]{0:T(128)}, s32[8]{0:T(128)S(1)}) fusion(s32[8,1,4]{0,2,1:T(4,128)} %param.9), kind=kLoop, calls=%fused_computation.25 | loop fusion | flops 168 | bytes 192 | tf_op jit(solution)/shard_map/body/reduce | solution.py:186
  17.7 0.1 broadcast_in_dim.38
  17.8 0.1 broadcast_in_dim.39
  17.9 0.1 copy.29
  18.0 0.1 squeeze.30
  18.1 0.6 fusion.11.column
  18.7 6.4 %pick.1 = (bf16[2,32,32,128]{3,2,1,0:T(8,128)(2,1)}, bf16[2,32,32,128]{3,2,1,0:T(8,128)(2,1)}) custom-call(s32[32]{0:T(128)} %fusion.11.column, bf16[128,256,128]{2,1,0:T(8,128)(2,1)} %amplitudes.1), custom_call_target="tpu_custom_call" | custom-call | flops 268435456 | bytes 9437184 | tf_op jit(solution)/shard_map/pick/pallas_call | solution.py:120
  25.0 0.0 copy-start
  25.0 0.4 collective-permute-start
  25.4 0.1 copy.28
  25.5 0.1 reshape.50
  25.6 0.1 copy.27
  25.7 0.1 squeeze.26
  25.8 0.1 pad_add_fusion.meta
  25.9 1.3 %collective-permute-done.other_core = bf16[2,32,32,128]{3,2,1,0:T(8,128)(2,1)S(1)} collective-permute-done((bf16[2,32,32,128]{3,2,1,0:T(8,128)(2,1)}, bf16[2,32,32,128]{3,2,1,0:T(8,128)(2,1)S(1)}, u32[]{:S(2)}, u32[]{:S(2)}) %collective-permute-start) | collective-permute-done | bytes 524320 | tf_op jit(solution)/shard_map/ppermute | solution.py:196
  27.2 0.1 copy.30
  27.3 0.1 eq.51
  27.4 1.7 %add_bitcast_fusion = bf16[32,32,128]{2,1,0:T(8,128)(2,1)} fusion(bf16[2,32,32,128]{3,2,1,0:T(8,128)(2,1)S(1)} %collective-permute-done.other_core, s32[]{:T(128)S(6)} %select_n.52, bf16[2,32,32,128]{3,2,1,0:T(8,128)(2,1)} %get-tuple-element.18.here), kind=kLoop, calls=%fused_computation | loop fusion | flops 131072 | bytes 786436 | tf_op jit(solution)/shard_map/add | solution.py:200
  29.1 1.5 %collective-permute-start.1 = (bf16[32,32,128]{2,1,0:T(8,128)(2,1)}, bf16[32,32,128]{2,1,0:T(8,128)(2,1)}, u32[]{:S(2)}, u32[]{:S(2)}) collective-permute-start(bf16[32,32,128]{2,1,0:T(8,128)(2,1)} %add_bitcast_fusion), channel_id=1, source_target_pairs={{0,2},{2,0},{1,3},{3,1},{4,6},{6,4},{5,7},{7,5},{8,10},{10,8},{9,1... | collective-permute-start | bytes 786440 | tf_op jit(solution)/shard_map/ppermute | solution.py:201
  30.6 5.9 %fusion.1 = bf16[32,128,128]{2,0,1:T(8,128)(2,1)} fusion(bf16[128,256,128]{2,1,0:T(8,128)(2,1)} %amplitudes.1, s32[32]{0:T(128)S(1)} %eq.51), kind=kOutput, calls=%fused_computation.4 | convolution fusion | flops 268443648 | bytes 9437312 | tf_op jit(solution)/shard_map/nd,cdp->npc/dot_general | solution.py:206
  36.5 1.9 %copy.31 = bf16[32,128,128]{1,2,0:T(8,128)(2,1)S(1)} copy(bf16[32,128,128]{2,0,1:T(8,128)(2,1)} %fusion.1) | data formatting | bytes 2097152 | tf_op jit(solution)/shard_map/nd,cdp->npc/dot_general | solution.py:206
  38.5 1.0 %collective-permute-done.1.other_row = bf16[32,32,128]{2,1,0:T(8,128)(2,1)} collective-permute-done((bf16[32,32,128]{2,1,0:T(8,128)(2,1)}, bf16[32,32,128]{2,1,0:T(8,128)(2,1)}, u32[]{:S(2)}, u32[]{:S(2)}) %collective-permute-start.1) | collective-permute-done | bytes 262176 | tf_op jit(solution)/shard_map/ppermute | solution.py:201
  39.5 2.6 %all-to-all-done.tiles = bf16[32,160,128]{2,1,0:T(8,128)(2,1)S(1)} async-done(((bf16[32,160,128]{2,1,0:T(8,128)(2,1)}), bf16[32,160,128]{2,1,0:T(8,128)(2,1)S(1)}, u32[]{:S(2)}, u32[]{:S(2)}) %all-to-all-start) | async-done | bytes 1310752 | tf_op jit(solution)/shard_map/all_to_all | solution.py:182
  42.2 0.0 copy-done
  42.2 3.2 %ladder.1 = (f32[8,2,4,16,128]{4,3,2,1,0:T(8,128)S(1)}, f32[8,2,4,16,128]{4,3,2,1,0:T(8,128)S(1)}) custom-call(s32[66]{0:T(128)S(1)} %pad_add_fusion.meta, bf16[32,128,128]{2,1,0:T(8,128)(2,1)S(1)} %bitcast.51, bf16[2,32,32,128]{3,2,1,0:T(8,128)(2,1)S(1)} %copy-done, bf16[2,32,32,128]{3,2,1,0:T(8,128)(2,1)S(1)} %collective-permute-done.other_core, ...), custom_call_target="tpu_custom_call" | custom-call | flops 167772160 | bytes 3670016 | tf_op jit(solution)/shard_map/ladder/pallas_call | solution.py:210
  45.4 0.1 collective-permute-start.2
  45.5 1.9 %collective-permute-done.2 = f32[8,2,4,16,128]{4,3,2,1,0:T(8,128)S(1)} collective-permute-done((f32[8,2,4,16,128]{4,3,2,1,0:T(8,128)S(1)}, f32[8,2,4,16,128]{4,3,2,1,0:T(8,128)S(1)}, u32[]{:S(2)}, u32[]{:S(2)}) %collective-permute-start.2) | collective-permute-done | bytes 524320 | tf_op jit(solution)/shard_map/ppermute | solution.py:225
  47.4 0.1 add.52
  47.5 21.0 %all_to_all.10 = f32[16,4,16,128]{3,2,1,0:T(8,128)S(1)} all-to-all(f32[16,4,16,128]{3,2,1,0:T(8,128)S(1)} %bitcast.55), channel_id=1, replica_groups=mesh['blk'=8,'ty'=2,'core'=2] {'blk','ty'}, dimensions={0} | all-to-all | bytes 1048576 | tf_op jit(solution)/shard_map/all_to_all | solution.py:227
  68.5 0.6 copy_bitcast_fusion
  (9 shorter events, 0.1 us)
Async XLA Ops:
  2.9 39.2 %all-to-all-start = ((bf16[32,160,128]{2,1,0:T(8,128)(2,1)}), bf16[32,160,128]{2,1,0:T(8,128)(2,1)S(1)}, u32[]{:S(2)}, u32[]{:S(2)}) async-start(bf16[32,160,128]{2,1,0:T(8,128)(2,1)} %bitcast.54), calls=%async_computation | async-start | bytes 2621440 | tf_op jit(solution)/shard_map/all_to_all | solution.py:182
  25.0 17.1 %copy-start = (bf16[2,32,32,128]{3,2,1,0:T(8,128)(2,1)S(1)}, bf16[2,32,32,128]{3,2,1,0:T(8,128)(2,1)}, u32[]{:S(2)}) copy-start(bf16[2,32,32,128]{3,2,1,0:T(8,128)(2,1)} %get-tuple-element.18.here) | copy-start | bytes 1572868
  25.0 2.2 %collective-permute-start = (bf16[2,32,32,128]{3,2,1,0:T(8,128)(2,1)}, bf16[2,32,32,128]{3,2,1,0:T(8,128)(2,1)S(1)}, u32[]{:S(2)}, u32[]{:S(2)}) collective-permute-start(bf16[2,32,32,128]{3,2,1,0:T(8,128)(2,1)} %get-tuple-element.16), channel_id=1, source_target_pairs={{0,1},{1,0},{2,3},{3,2},{4,5},{5,4},{6,7},{7,6},{8,9},{9,8},{10,11... | collective-permute-start | bytes 1572872 | tf_op jit(solution)/shard_map/ppermute | solution.py:196
  29.1 10.4 %collective-permute-start.1 = (bf16[32,32,128]{2,1,0:T(8,128)(2,1)}, bf16[32,32,128]{2,1,0:T(8,128)(2,1)}, u32[]{:S(2)}, u32[]{:S(2)}) collective-permute-start(bf16[32,32,128]{2,1,0:T(8,128)(2,1)} %add_bitcast_fusion), channel_id=1, source_target_pairs={{0,2},{2,0},{1,3},{3,1},{4,6},{6,4},{5,7},{7,5},{8,10},{10,8},{9,1... | collective-permute-start | bytes 786440 | tf_op jit(solution)/shard_map/ppermute | solution.py:201
  45.4 2.0 %collective-permute-start.2 = (f32[8,2,4,16,128]{4,3,2,1,0:T(8,128)S(1)}, f32[8,2,4,16,128]{4,3,2,1,0:T(8,128)S(1)}, u32[]{:S(2)}, u32[]{:S(2)}) collective-permute-start(f32[8,2,4,16,128]{4,3,2,1,0:T(8,128)S(1)} %get-tuple-element.20), channel_id=1, source_target_pairs={{0,1},{1,0},{2,3},{3,2},{4,5},{5,4},{6,7},{7,6},{8,9},{9,8},{10,11... | collective-permute-start | bytes 1572872 | tf_op jit(solution)/shard_map/ppermute | solution.py:225

commit v5 on v3

v5 whole, which is shorter than its diff:
```python
import functools

import jax
import jax.numpy as jnp
from jax import lax
from jax.experimental import pallas as pl
from jax.experimental.pallas import tpu as pltpu
from jax.sharding import Mesh, PartitionSpec as P

NRB = 16
TASK = ("ty", "core")
EVERY = ("blk", "ty", "core")


def pack_kernel(counts, tiles, pieces, out, held, busy, first_sem, second_sem, out_sem, count_sem):
    tasks, blocks, rows, _ = held.shape
    chunk = tiles.shape[2]
    parts = first_sem.shape[1]
    count_copy = pltpu.make_async_copy(counts, busy, count_sem)
    count_copy.start()
    spans = [(w, part, pl.ds(part * (blocks // parts), blocks // parts)) for w in range(tasks) for part in range(parts)]
    first = [
        pltpu.make_async_copy(tiles.at[2 * w, span], held.at[w, span, pl.ds(0, chunk)], first_sem.at[w, part])
        for w, part, span in spans
    ]
    for copy in first:
        copy.start()
    count_copy.wait()
    group = lax.axis_index("blk")
    tile = 1
    for w in range(1, tasks):
        tile = jnp.where(busy[w, group] == 2, 2 * w + 1, tile)
    second = [
        pltpu.make_async_copy(
            pieces.at[tile, span, w], held.at[w, span, pl.ds(chunk, rows - chunk)], second_sem.at[w, part]
        )
        for w, part, span in spans
    ]
    for copy in second:
        copy.start()
    leave = [pltpu.make_async_copy(held.at[w, span], out.at[span, w], out_sem.at[w, part]) for w, part, span in spans]
    for n in range(len(spans)):
        first[n].wait()
        second[n].wait()
        leave[n].start()
    for copy in leave:
        copy.wait()


def pack(integral_tiles, tile_counts, blocks):
    tasks, _, virt_total, row_block = integral_tiles.shape[2:]
    chunk = virt_total // blocks
    piece = chunk // tasks
    tiles = integral_tiles.reshape(tasks * 2, blocks, chunk, row_block)
    pieces = integral_tiles.reshape(tasks * 2, blocks, tasks, piece, row_block)
    counts = jnp.transpose(tile_counts[:, 0])
    if piece % 16:
        own = lax.dynamic_index_in_dim(counts, lax.axis_index("blk"), 1, keepdims=False)
        second = lax.dynamic_index_in_dim(pieces, 2 * jnp.argmax(own) + 1, 0, keepdims=False)
        return jnp.concatenate([jnp.swapaxes(tiles[::2], 0, 1), second], axis=2)
    return pl.pallas_call(
        pack_kernel,
        out_shape=jax.ShapeDtypeStruct((blocks, tasks, chunk + piece, row_block), tiles.dtype),
        in_specs=[pl.BlockSpec(memory_space=pl.ANY)] * 3,
        out_specs=pl.BlockSpec(memory_space=pl.ANY),
        scratch_shapes=[
            pltpu.VMEM((tasks, blocks, chunk + piece, row_block), tiles.dtype),
            pltpu.SMEM(counts.shape, counts.dtype),
        ]
        + [pltpu.SemaphoreType.DMA((tasks, 4))] * 3
        + [pltpu.SemaphoreType.DMA],
        compiler_params=pltpu.CompilerParams(vmem_limit_bytes=58 << 20),
        name="pack",
    )(counts, tiles, pieces)


def pick_kernel(lists, amplitudes, there, here, *refs, hop, row_tasks):
    columns = refs[0] if len(refs) == 5 else None
    held, hot, picked, sems = refs[-4:]
    slots, piece, _ = here.shape
    sides, parts = sems.shape
    rows = piece // parts
    core, row_task = lax.axis_index("core"), lax.axis_index("ty") + hop

    def base_of(side):
        task = 2 * lax.rem(row_task + side // 2, row_tasks) + lax.rem(core + 1 + side, 2)
        return pl.multiple_of(task * piece, piece)

    def copy_of(side, part):
        return pltpu.make_async_copy(
            amplitudes.at[pl.ds(base_of(side) + part * rows, rows)],
            held.at[side, pl.ds(part * rows, rows)],
            sems.at[side, part],
        )

    for side in range(sides):
        for part in range(parts):
            copy_of(side, part).start()

    lane = lax.broadcasted_iota(jnp.int32, (1, hot.shape[1]), 1)
    for n in range(hot.shape[0]):
        hot[pl.ds(n, 1), :] = jnp.where(lane == lists[n], 1.0, 0.0)
    chosen = hot[...].astype(held.dtype)

    for side in range(sides):
        for part in range(parts):
            copy_of(side, part).wait()
            for c in range(part * rows, (part + 1) * rows):
                picked[c] = jnp.dot(chosen, held[side, c], preferred_element_type=jnp.float32)
        if side < 2:
            for n in range(slots):
                (there, here)[side][n] = picked[:, n, :].astype(here.dtype)
        if columns is not None:
            for n in range(slots):
                columns[n, pl.ds(base_of(side), piece), :] = picked[:, slots + n, :].astype(columns.dtype)


def pick(lists, amplitudes, hop, row_tasks, slots):
    chunk, span, pair_total = amplitudes.shape
    tasks = 2 * row_tasks
    piece = chunk // tasks
    listed = lists.shape[0]
    sides = tasks if listed > slots else 2
    part = jax.ShapeDtypeStruct((slots, piece, pair_total), amplitudes.dtype)
    whole = jax.ShapeDtypeStruct((slots, chunk, pair_total), amplitudes.dtype)
    outs = (part, part, whole) if listed > slots else (part, part)
    return pl.pallas_call(
        functools.partial(pick_kernel, hop=hop, row_tasks=row_tasks),
        out_shape=outs,
        in_specs=[pl.BlockSpec(memory_space=pltpu.SMEM), pl.BlockSpec(memory_space=pl.ANY)],
        out_specs=(pl.BlockSpec(memory_space=pltpu.VMEM),) * len(outs),
        scratch_shapes=[
            pltpu.VMEM((sides, piece, span, pair_total), amplitudes.dtype),
            pltpu.VMEM((listed, span), jnp.float32),
            pltpu.VMEM((piece, listed, pair_total), jnp.float32),
            pltpu.SemaphoreType.DMA((sides, 4)),
        ],
        compiler_params=pltpu.CompilerParams(vmem_limit_bytes=48 << 20),
        cost_estimate=pl.CostEstimate(
            flops=2 * listed * sides * piece * span * pair_total,
            bytes_accessed=2 * sides * piece * (span + listed) * pair_total,
            transcendentals=0,
        ),
        name="pick",
    )(lists, amplitudes)


def dot_rows(left, right):
    return lax.dot_general(left, right, (((0,), (0,)), ((), ())), preferred_element_type=jnp.float32)


def ladder_kernel(meta, columns, tiles, here, *refs, row_tasks, pair_blocks):
    others, (keep, send, total) = refs[:-3], refs[-3:]
    slots, chunk, _ = columns.shape
    total[...] = jnp.zeros_like(total)

    def add_slots(step, carry):
        for part in range(4):
            n = step * 4 + part
            total[meta[n]] += dot_rows(columns[n], tiles[n, :chunk])
            second = sum((other[n] for other in others), here[n])
            total[meta[slots + n]] += dot_rows(second, tiles[n, chunk:])
        return carry

    lax.fori_loop(0, slots // 4, add_slots, 0)

    core = meta[2 * slots]
    rows = NRB // (2 * row_tasks)
    pairs = total.shape[1] // pair_blocks
    for task in range(row_tasks):
        for block in range(pair_blocks):
            span = pl.ds(block * pairs, pairs)
            for row in range(rows):
                keep[block, task, row] = total[(2 * task + core) * rows + row, span, :]
                send[block, task, row] = total[(2 * task + 1 - core) * rows + row, span, :]


def body(amplitudes, integral_tiles, task_list, block_offsets, tile_counts, *, shape):
    blocks, row_tasks = shape
    tasks = 2 * row_tasks
    chunk, span, pair_total = amplitudes.shape
    row_block = integral_tiles.shape[5]
    slots = blocks * tasks
    piece = chunk // tasks
    rows, pairs = NRB // tasks, pair_total // blocks
    core = lax.axis_index("core").astype(jnp.int32)
    ty = lax.axis_index("ty").astype(jnp.int32)
    worker = ty * 2 + core

    sent = pack(integral_tiles, tile_counts, blocks).reshape(slots, chunk + piece, row_block)
    arrived = lax.all_to_all(sent, EVERY, 0, 0, tiled=True)

    lists = lax.all_gather(task_list * NRB + block_offsets, TASK, axis=1, tiled=True)
    counts, lists = lax.optimization_barrier((tile_counts[:, 0], lists))
    mine = lax.dynamic_index_in_dim(lists, worker, 2, keepdims=False)
    second_row = jnp.sum(jnp.where(counts[:, None] == 2, lists[..., 1] % NRB, 0), axis=-1)
    meta = jnp.concatenate([(mine[..., 0] % NRB).reshape(-1), second_row.reshape(-1), core[None]])

    owner = lax.dynamic_index_in_dim(counts, worker, 1) == 2
    column = jnp.where(owner, mine[..., 1] // NRB, span).reshape(-1)
    first = (mine[..., 0] // NRB).reshape(-1)
    others = []
    for hop in range(1, row_tasks):
        there, here = pick(column, amplitudes, hop, row_tasks, slots)
        away = here + lax.ppermute(there, "core", [(0, 1), (1, 0)])
        others.append(lax.ppermute(away, "ty", [(i, (i + hop) % row_tasks) for i in range(row_tasks)]))
        column, first, _ = lax.optimization_barrier((column, first, away))
    if piece % 16:
        there, here = pick(column, amplitudes, 0, row_tasks, slots)
        hot = (first[:, None] == jnp.arange(span, dtype=jnp.int32)).astype(amplitudes.dtype)
        columns = jnp.einsum("nd,cdp->ncp", hot, amplitudes)
    else:
        there, here, columns = pick(jnp.concatenate([column, first]), amplitudes, 0, row_tasks, slots)
    others.append(lax.ppermute(there, "core", [(0, 1), (1, 0)]))

    part = jax.ShapeDtypeStruct((blocks, row_tasks, rows, pairs, row_block), jnp.float32)
    in_vmem = pl.BlockSpec(memory_space=pltpu.VMEM)
    keep, send = pl.pallas_call(
        functools.partial(ladder_kernel, row_tasks=row_tasks, pair_blocks=blocks),
        out_shape=(part, part),
        in_specs=[pl.BlockSpec(memory_space=pltpu.SMEM)] + [in_vmem] * (3 + len(others)),
        out_specs=(in_vmem, in_vmem),
        scratch_shapes=[pltpu.VMEM((NRB, pair_total, row_block), jnp.float32)],
        compiler_params=pltpu.CompilerParams(vmem_limit_bytes=16 << 20),
        cost_estimate=pl.CostEstimate(
            flops=2 * slots * (chunk + piece) * pair_total * row_block,
            bytes_accessed=2 * slots * (chunk + piece) * (pair_total + row_block) + 4 * NRB * pair_total * row_block,
            transcendentals=0,
        ),
        name="ladder",
    )(meta, columns, arrived, here, *others)

    other = lax.ppermute(send, "core", [(0, 1), (1, 0)])
    half = (keep + other).reshape(blocks * row_tasks, rows, pairs, row_block)
    parts = lax.all_to_all(half, ("blk", "ty"), 0, 0, tiled=True)
    out = jnp.sum(parts, axis=0)
    return jnp.transpose(out, (1, 0, 2)).reshape(pairs, rows * row_block)


def solution(mesh):
    blocks, tasks = mesh.shape["blk"], mesh.shape["task"]
    fine = Mesh(mesh.devices.reshape(blocks, tasks // 2, 2), EVERY)
    placed = (
        P("blk", TASK, None),
        P("blk", TASK, None, None, None, None),
        P(None, TASK, None, None),
        P(None, TASK, None, None),
        P(None, TASK, None),
    )
    return jax.shard_map(
        functools.partial(body, shape=(blocks, tasks // 2)),
        mesh=fine, in_specs=placed, out_specs=P("blk", TASK), check_vma=False,
    )
```

time: 70.9 us -> 68.2 us (0.962)
  Pallas kernels: 4.3 us -> 17.9 us
  matrix products: 9.87 us -> 0 us
  local copies, waits for them, and re-layouts: 9.26 us -> 1.31 us
  waiting for transfers between devices: 6.7 us -> 12.8 us
  other arithmetic: 3.89 us -> 1.11 us
  blocking collectives: 28.6 us -> 25.9 us
  starting transfers between devices: 7.75 us -> 8.67 us
    pallas_call x0 -> x2, Pallas kernels: none -> 11.8 us  [pick(): pl.pallas_call(functools.partial(pick_kernel, hop=hop, row_tasks=row_task...]
    dot_general x2 -> x0, matrix products: 9.87 us -> none  [the longest x1 4.94 us: body(): jnp.einsum('nd,cdp->cnp', hot.reshape(slots, span).astype(amplitudes.dtyp...]
    all_to_all x1, waiting for transfers between devices: 0.01 us -> 8.01 us  [body(): arrived = lax.all_to_all(sent, EVERY, 0, 0, tiled=True)]
    all_gather x1, blocking collectives: 9.92 us -> 6.14 us  [body(): lax.all_gather(task_list * NRB + block_offsets, TASK, axis=1, tiled=True)]
    ppermute x1 -> x0, local copies, waits for them, and re-layouts: 2.34 us -> none  [body(): lax.ppermute(away, 'ty', [(i, (i + hop) % row_tasks) for i in range(row_t...]
    unnamed x4 -> x6, local copies, waits for them, and re-layouts: 2.27 us -> 0.02 us
    dynamic_slice x2 -> x0, local copies, waits for them, and re-layouts: 2.17 us -> none  [body(): extras = lax.dynamic_index_in_dim(merged, ty, 0, keepdims=False)]
    ppermute x1, waiting for transfers between devices: 3.67 us -> 1.8 us  [body(): lax.ppermute(away, 'ty', [(i, (i + hop) % row_tasks) for i in range(row_t...]
  transfers between devices with their start and end apart: 4 -> 5, of which waited for: 3 -> 4; matrix products, arithmetic and copies ran while one was open for 28% -> 2% of each run, Pallas kernels for 0% -> 17%
where the time goes in v5:
time: 68.2 us; the launch traced here: 67.8 us
  blocking collectives  25.9 us (38%)
  Pallas kernels  17.9 us (26%)
  waiting for transfers between devices  12.8 us (19%)
  starting transfers between devices  8.67 us (13%)
  local copies, waits for them, and re-layouts  1.31 us (2%)
  other arithmetic  1.11 us (2%)
    all_to_all x1, blocking collectives, body(): parts = lax.all_to_all(half, ('blk', 'ty'), 0, 0, tiled=True)  19.8 us
    pallas_call x2, Pallas kernels, pick(): pl.pallas_call(functools.partial(pick_kernel, hop=hop, row_tasks=row_task...  11.8 us
    all_to_all x1, waiting for transfers between devices, body(): arrived = lax.all_to_all(sent, EVERY, 0, 0, tiled=True)  8.01 us
    all_to_all x1, starting transfers between devices, body(): arrived = lax.all_to_all(sent, EVERY, 0, 0, tiled=True)  7.3 us
    all_gather x1, blocking collectives, body(): lax.all_gather(task_list * NRB + block_offsets, TASK, axis=1, tiled=True)  6.14 us
    pallas_call x1, Pallas kernels, pack(): pl.pallas_call(pack_kernel, out_shape=jax.ShapeDtypeStruct((blocks, tasks...  3.17 us
    pallas_call x1, Pallas kernels, body(): pl.pallas_call(functools.partial(ladder_kernel, row_tasks=row_tasks, pair...  2.9 us
    ppermute x1, waiting for transfers between devices, body(): other = lax.ppermute(send, 'core', [(0, 1), (1, 0)])  1.9 us
  transfers between devices with their start and end apart: 5, of which 4 were waited for; matrix products, arithmetic and copies ran while one was open for 2% of the time, Pallas kernels for 17%

profile of v5, /device:TPU:0, one launch (start us, length us, event | category | flops | bytes accessed | tf_op | source)
XLA Modules:
  0.0 67.8 jit_solution(10631337293722168456)
XLA Ops:
  0.0 3.2 %pack.1 = bf16[8,4,160,128]{3,2,1,0:T(8,128)(2,1)} custom-call(s32[4,8]{1,0:T(4,128)} %bitcast.32, bf16[8,8,128,128]{3,2,1,0:T(8,128)(2,1)} %bitcast.27, bf16[8,8,4,32,128]{4,3,2,1,0:T(8,128)(2,1)} %bitcast.28), custom_call_target="tpu_custom_call" | custom-call | tf_op jit(solution)/shard_map/pack/pallas_call | solution.py:61
  3.2 0.0 copy-start.1
  3.2 0.0 copy-start.2
  3.2 0.0 copy-start
  3.2 7.3 %all-to-all-start = ((bf16[32,160,128]{2,1,0:T(8,128)(2,1)}), bf16[32,160,128]{2,1,0:T(8,128)(2,1)S(1)}, u32[]{:S(2)}, u32[]{:S(2)}) async-start(bf16[32,160,128]{2,1,0:T(8,128)(2,1)} %bitcast.29), calls=%async_computation | async-start | bytes 2621440 | tf_op jit(solution)/shard_map/all_to_all | solution.py:191
  10.5 0.0 copy-done.1
  10.5 0.0 copy-done.2
  10.6 6.1 %all_gather.3 = s32[8,4,4,2]{0,2,3,1:T(4,128)S(1)} all-gather(s32[8,1,4,2]{0,2,3,1:T(4,128)S(1)} %copy_add_fusion), channel_id=1, replica_groups=mesh['blk'=8,'ty'=2,'core'=2] {'ty','core'}, dimensions={1}, use_global_device_ids=true | all-gather | bytes 1280 | tf_op jit(solution)/shard_map/all_gather | solution.py:193
  16.7 0.0 copy-done
  16.7 0.1 broadcast_in_dim.33
  16.8 0.1 broadcast_in_dim.34
  16.9 0.1 copy.23
  17.0 0.1 squeeze.22
  17.1 4.1 %pick.2 = (bf16[32,32,128]{2,1,0:T(8,128)(2,1)S(1)}, bf16[32,32,128]{2,1,0:T(8,128)(2,1)S(1)}) custom-call(s32[32]{0:T(128)S(1)} %fusion.3.lists, bf16[128,256,128]{2,1,0:T(8,128)(2,1)} %amplitudes.3), custom_call_target="tpu_custom_call" | custom-call | flops 134217728 | bytes 4718592 | tf_op jit(solution)/shard_map/pick/pallas_call | solution.py:127
  21.2 0.4 collective-permute-start
  21.5 0.1 copy.21
  21.6 0.1 squeeze.20
  21.7 1.1 %collective-permute-done = bf16[32,32,128]{2,1,0:T(8,128)(2,1)S(1)} collective-permute-done((bf16[32,32,128]{2,1,0:T(8,128)(2,1)S(1)}, bf16[32,32,128]{2,1,0:T(8,128)(2,1)S(1)}, u32[]{:S(2)}, u32[]{:S(2)}) %collective-permute-start) | collective-permute-done | bytes 262176 | tf_op jit(solution)/shard_map/ppermute | solution.py:205
  22.8 0.8 %add.40 = bf16[32,32,128]{2,1,0:T(8,128)(2,1)} add(bf16[32,32,128]{2,1,0:T(8,128)(2,1)S(1)} %get-tuple-element.18, bf16[32,32,128]{2,1,0:T(8,128)(2,1)S(1)} %collective-permute-done) | non-fusion elementwise | flops 131072 | bytes 786432 | tf_op jit(solution)/shard_map/add | solution.py:205
  23.5 0.8 %collective-permute-start.1 = (bf16[32,32,128]{2,1,0:T(8,128)(2,1)}, bf16[32,32,128]{2,1,0:T(8,128)(2,1)S(1)}, u32[]{:S(2)}, u32[]{:S(2)}) collective-permute-start(bf16[32,32,128]{2,1,0:T(8,128)(2,1)} %add.40), channel_id=1, source_target_pairs={{0,2},{2,0},{1,3},{3,1},{4,6},{6,4},{5,7},{7,5},{8,10},{10,8},{9,1... | collective-permute-start | bytes 786440 | tf_op jit(solution)/shard_map/ppermute | solution.py:206
  24.4 0.1 pad_add_fusion.1.lists
  24.4 7.8 %pick.3 = (bf16[32,32,128]{2,1,0:T(8,128)(2,1)S(1)}, bf16[32,32,128]{2,1,0:T(8,128)(2,1)S(1)}, bf16[32,128,128]{2,1,0:T(8,128)(2,1)S(1)}) custom-call(s32[64]{0:T(128)S(1)} %pad_add_fusion.1.lists, bf16[128,256,128]{2,1,0:T(8,128)(2,1)} %amplitudes.3), custom_call_target="tpu_custom_call" | custom-call | flops 536870912 | bytes 10485760 | tf_op jit(solution)/shard_map/pick/pallas_call | solution.py:127
  32.2 0.1 collective-permute-start.2
  32.4 0.1 copy.22
  32.4 0.1 reshape.27
  32.5 0.1 pad_add_fusion.meta
  32.6 1.8 %collective-permute-done.1.refs_0_ = bf16[32,32,128]{2,1,0:T(8,128)(2,1)S(1)} collective-permute-done((bf16[32,32,128]{2,1,0:T(8,128)(2,1)}, bf16[32,32,128]{2,1,0:T(8,128)(2,1)S(1)}, u32[]{:S(2)}, u32[]{:S(2)}) %collective-permute-start.1) | collective-permute-done | bytes 262176 | tf_op jit(solution)/shard_map/ppermute | solution.py:206
  34.4 0.0 collective-permute-done.2.refs_1_
  34.4 8.0 %all-to-all-done.tiles = bf16[32,160,128]{2,1,0:T(8,128)(2,1)S(1)} async-done(((bf16[32,160,128]{2,1,0:T(8,128)(2,1)}), bf16[32,160,128]{2,1,0:T(8,128)(2,1)S(1)}, u32[]{:S(2)}, u32[]{:S(2)}) %all-to-all-start) | async-done | bytes 1310752 | tf_op jit(solution)/shard_map/all_to_all | solution.py:191
  42.4 2.9 %ladder.1 = (f32[8,2,4,16,128]{4,3,2,1,0:T(8,128)S(1)}, f32[8,2,4,16,128]{4,3,2,1,0:T(8,128)S(1)}) custom-call(s32[65]{0:T(128)S(1)} %pad_add_fusion.meta, bf16[32,128,128]{2,1,0:T(8,128)(2,1)S(1)} %get-tuple-element.22.columns, bf16[32,160,128]{2,1,0:T(8,128)(2,1)S(1)} %all-to-all-done.tiles, bf16[32,32,128]{2,1,0:T(8,128)(2,1)S(1)} %get-tuple-element.23.here, ...), custom_call_target="tpu_custom_call" | custom-call | flops 167772160 | bytes 3670016 | tf_op jit(solution)/shard_map/ladder/pallas_call | solution.py:218
  45.3 0.1 collective-permute-start.3
  45.4 1.9 %collective-permute-done.3 = f32[8,2,4,16,128]{4,3,2,1,0:T(8,128)S(1)} collective-permute-done((f32[8,2,4,16,128]{4,3,2,1,0:T(8,128)S(1)}, f32[8,2,4,16,128]{4,3,2,1,0:T(8,128)S(1)}, u32[]{:S(2)}, u32[]{:S(2)}) %collective-permute-start.3) | collective-permute-done | bytes 524320 | tf_op jit(solution)/shard_map/ppermute | solution.py:233
  47.3 0.1 add.41
  47.4 19.8 %all_to_all.10 = f32[16,4,16,128]{3,2,1,0:T(8,128)S(1)} all-to-all(f32[16,4,16,128]{3,2,1,0:T(8,128)S(1)} %bitcast.30), channel_id=1, replica_groups=mesh['blk'=8,'ty'=2,'core'=2] {'blk','ty'}, dimensions={0} | all-to-all | bytes 1048576 | tf_op jit(solution)/shard_map/all_to_all | solution.py:235
  67.2 0.6 copy_bitcast_fusion
  (10 shorter events, 0.1 us)
Async XLA Ops:
  3.2 7.4 %copy-start.1 = (s32[8,1,4,2]{0,3,2,1:T(2,128)S(1)}, s32[8,1,4,2]{0,3,2,1:T(2,128)}, u32[]{:S(2)}) copy-start(s32[8,1,4,2]{0,3,2,1:T(2,128)} %param.8) | copy-start | bytes 772
  3.2 7.4 %copy-start.2 = (s32[8,1,4,2]{0,3,2,1:T(2,128)S(1)}, s32[8,1,4,2]{0,3,2,1:T(2,128)}, u32[]{:S(2)}) copy-start(s32[8,1,4,2]{0,3,2,1:T(2,128)} %param.7) | copy-start | bytes 772
  3.2 13.5 %copy-start = (s32[8,1,4]{0,2,1:T(4,128)S(1)}, s32[8,1,4]{0,2,1:T(4,128)}, u32[]{:S(2)}) copy-start(s32[8,1,4]{0,2,1:T(4,128)} %param.9) | copy-start | bytes 388
  3.2 39.2 %all-to-all-start = ((bf16[32,160,128]{2,1,0:T(8,128)(2,1)}), bf16[32,160,128]{2,1,0:T(8,128)(2,1)S(1)}, u32[]{:S(2)}, u32[]{:S(2)}) async-start(bf16[32,160,128]{2,1,0:T(8,128)(2,1)} %bitcast.29), calls=%async_computation | async-start | bytes 2621440 | tf_op jit(solution)/shard_map/all_to_all | solution.py:191
  21.2 1.6 %collective-permute-start = (bf16[32,32,128]{2,1,0:T(8,128)(2,1)S(1)}, bf16[32,32,128]{2,1,0:T(8,128)(2,1)S(1)}, u32[]{:S(2)}, u32[]{:S(2)}) collective-permute-start(bf16[32,32,128]{2,1,0:T(8,128)(2,1)S(1)} %get-tuple-element.19), channel_id=1, source_target_pairs={{0,1},{1,0},{2,3},{3,2},{4,5},{5,4},{6,7},{7,6},{8,9},{9,8},{10,11... | collective-permute-start | bytes 786440 | tf_op jit(solution)/shard_map/ppermute | solution.py:205
  23.5 10.9 %collective-permute-start.1 = (bf16[32,32,128]{2,1,0:T(8,128)(2,1)}, bf16[32,32,128]{2,1,0:T(8,128)(2,1)S(1)}, u32[]{:S(2)}, u32[]{:S(2)}) collective-permute-start(bf16[32,32,128]{2,1,0:T(8,128)(2,1)} %add.40), channel_id=1, source_target_pairs={{0,2},{2,0},{1,3},{3,1},{4,6},{6,4},{5,7},{7,5},{8,10},{10,8},{9,1... | collective-permute-start | bytes 786440 | tf_op jit(solution)/shard_map/ppermute | solution.py:206
  32.2 2.2 %collective-permute-start.2 = (bf16[32,32,128]{2,1,0:T(8,128)(2,1)S(1)}, bf16[32,32,128]{2,1,0:T(8,128)(2,1)S(1)}, u32[]{:S(2)}, u32[]{:S(2)}) collective-permute-start(bf16[32,32,128]{2,1,0:T(8,128)(2,1)S(1)} %get-tuple-element.24), channel_id=1, source_target_pairs={{0,1},{1,0},{2,3},{3,2},{4,5},{5,4},{6,7},{7,6},{8,9},{9,8},{10,11... | collective-permute-start | bytes 786440 | tf_op jit(solution)/shard_map/ppermute | solution.py:214
  45.3 2.0 %collective-permute-start.3 = (f32[8,2,4,16,128]{4,3,2,1,0:T(8,128)S(1)}, f32[8,2,4,16,128]{4,3,2,1,0:T(8,128)S(1)}, u32[]{:S(2)}, u32[]{:S(2)}) collective-permute-start(f32[8,2,4,16,128]{4,3,2,1,0:T(8,128)S(1)} %get-tuple-element.26), channel_id=1, source_target_pairs={{0,1},{1,0},{2,3},{3,2},{4,5},{5,4},{6,7},{7,6},{8,9},{9,8},{10,11... | collective-permute-start | bytes 1572872 | tf_op jit(solution)/shard_map/ppermute | solution.py:233

commit v6 on v5

--- a/solution.py
+++ b/solution.py
@@ -12,17 +12,13 @@
 EVERY = ("blk", "ty", "core")
 
 
-def pack_kernel(counts, tiles, pieces, out, held, busy, first_sem, second_sem, out_sem, count_sem):
-    tasks, blocks, rows, _ = held.shape
+def pack_kernel(counts, tiles, pieces, out, held, busy, in_sem, out_sem, count_sem):
+    tasks, _, rows, _ = held.shape
     chunk = tiles.shape[2]
-    parts = first_sem.shape[1]
+    upper, lower = pl.ds(0, chunk), pl.ds(chunk, rows - chunk)
     count_copy = pltpu.make_async_copy(counts, busy, count_sem)
     count_copy.start()
-    spans = [(w, part, pl.ds(part * (blocks // parts), blocks // parts)) for w in range(tasks) for part in range(parts)]
-    first = [
-        pltpu.make_async_copy(tiles.at[2 * w, span], held.at[w, span, pl.ds(0, chunk)], first_sem.at[w, part])
-        for w, part, span in spans
-    ]
+    first = [pltpu.make_async_copy(tiles.at[2 * w], held.at[w, :, upper], in_sem.at[0, w]) for w in range(tasks)]
     for copy in first:
         copy.start()
     count_copy.wait()
@@ -31,18 +27,18 @@
     for w in range(1, tasks):
         tile = jnp.where(busy[w, group] == 2, 2 * w + 1, tile)
     second = [
-        pltpu.make_async_copy(
-            pieces.at[tile, span, w], held.at[w, span, pl.ds(chunk, rows - chunk)], second_sem.at[w, part]
-        )
-        for w, part, span in spans
+        pltpu.make_async_copy(pieces.at[tile, :, w], held.at[w, :, lower], in_sem.at[1, w]) for w in range(tasks)
     ]
     for copy in second:
         copy.start()
-    leave = [pltpu.make_async_copy(held.at[w, span], out.at[span, w], out_sem.at[w, part]) for w, part, span in spans]
-    for n in range(len(spans)):
-        first[n].wait()
-        second[n].wait()
-        leave[n].start()
+    leave = [
+        pltpu.make_async_copy(held.at[w, :, span], out.at[:, w, span], out_sem.at[half, w])
+        for half, span in enumerate((upper, lower))
+        for w in range(tasks)
+    ]
+    for arrive, go in zip(first + second, leave):
+        arrive.wait()
+        go.start()
     for copy in leave:
         copy.wait()
 
@@ -67,7 +63,7 @@
             pltpu.VMEM((tasks, blocks, chunk + piece, row_block), tiles.dtype),
             pltpu.SMEM(counts.shape, counts.dtype),
         ]
-        + [pltpu.SemaphoreType.DMA((tasks, 4))] * 3
+        + [pltpu.SemaphoreType.DMA((2, tasks))] * 2
         + [pltpu.SemaphoreType.DMA],
         compiler_params=pltpu.CompilerParams(vmem_limit_bytes=58 << 20),
         name="pack",
@@ -149,20 +145,20 @@
     return lax.dot_general(left, right, (((0,), (0,)), ((), ())), preferred_element_type=jnp.float32)
 
 
-def ladder_kernel(meta, columns, tiles, here, *refs, row_tasks, pair_blocks):
-    others, (keep, send, total) = refs[:-3], refs[-3:]
+def ladder_kernel(meta, columns, tiles, extras, keep, send, total, *, row_tasks, pair_blocks):
     slots, chunk, _ = columns.shape
     total[...] = jnp.zeros_like(total)
 
+    group = min(slots, 32)
+
     def add_slots(step, carry):
-        for part in range(4):
-            n = step * 4 + part
+        for part in range(group):
+            n = step * group + part
             total[meta[n]] += dot_rows(columns[n], tiles[n, :chunk])
-            second = sum((other[n] for other in others), here[n])
-            total[meta[slots + n]] += dot_rows(second, tiles[n, chunk:])
+            total[meta[slots + n]] += dot_rows(extras[n], tiles[n, chunk:])
         return carry
 
-    lax.fori_loop(0, slots // 4, add_slots, 0)
+    lax.fori_loop(0, slots // group, add_slots, 0)
 
     core = meta[2 * slots]
     rows = NRB // (2 * row_tasks)
@@ -212,13 +208,14 @@
     else:
         there, here, columns = pick(jnp.concatenate([column, first]), amplitudes, 0, row_tasks, slots)
     others.append(lax.ppermute(there, "core", [(0, 1), (1, 0)]))
+    extras = sum(others, here)
 
     part = jax.ShapeDtypeStruct((blocks, row_tasks, rows, pairs, row_block), jnp.float32)
     in_vmem = pl.BlockSpec(memory_space=pltpu.VMEM)
     keep, send = pl.pallas_call(
         functools.partial(ladder_kernel, row_tasks=row_tasks, pair_blocks=blocks),
         out_shape=(part, part),
-        in_specs=[pl.BlockSpec(memory_space=pltpu.SMEM)] + [in_vmem] * (3 + len(others)),
+        in_specs=[pl.BlockSpec(memory_space=pltpu.SMEM)] + [in_vmem] * 3,
         out_specs=(in_vmem, in_vmem),
         scratch_shapes=[pltpu.VMEM((NRB, pair_total, row_block), jnp.float32)],
         compiler_params=pltpu.CompilerParams(vmem_limit_bytes=16 << 20),
@@ -228,7 +225,7 @@
             transcendentals=0,
         ),
         name="ladder",
-    )(meta, columns, arrived, here, *others)
+    )(meta, columns, arrived, extras)
 
     other = lax.ppermute(send, "core", [(0, 1), (1, 0)])
     half = (keep + other).reshape(blocks * row_tasks, rows, pairs, row_block)

time: 68.2 us -> 66.1 us (0.969)
  Pallas kernels: 17.9 us -> 15.9 us
    pallas_call x1, Pallas kernels: 2.9 us -> 1.43 us  [body(): pl.pallas_call(functools.partial(ladder_kernel, row_tasks=row_tasks, pair...]
    add x0 -> x1, other arithmetic: none -> 1 us  [body(): extras = sum(others, here)]
    all_to_all x1, waiting for transfers between devices: 8.01 us -> 7.24 us  [body(): arrived = lax.all_to_all(sent, EVERY, 0, 0, tiled=True)]
    add x1, other arithmetic: 0.77 us -> 0.07 us  [body(): away = here + lax.ppermute(there, 'core', [(0, 1), (1, 0)])]
  transfers between devices with their start and end apart: 5 -> 5, of which waited for: 4 -> 4; matrix products, arithmetic and copies ran while one was open for 2% -> 3% of each run, Pallas kernels for 17% -> 18%
where the time goes in v6:
time: 66.1 us; the launch traced here: 65.8 us
  blocking collectives  25.9 us (39%)
  Pallas kernels  15.9 us (24%)
  waiting for transfers between devices  12.4 us (19%)
  starting transfers between devices  8.73 us (13%)
  other arithmetic  1.4 us (2%)
  local copies, waits for them, and re-layouts  1.31 us (2%)
    all_to_all x1, blocking collectives, body(): parts = lax.all_to_all(half, ('blk', 'ty'), 0, 0, tiled=True)  19.8 us
    pallas_call x2, Pallas kernels, pick(): pl.pallas_call(functools.partial(pick_kernel, hop=hop, row_tasks=row_task...  11.8 us
    all_to_all x1, starting transfers between devices, body(): arrived = lax.all_to_all(sent, EVERY, 0, 0, tiled=True)  7.3 us
    all_to_all x1, waiting for transfers between devices, body(): arrived = lax.all_to_all(sent, EVERY, 0, 0, tiled=True)  7.24 us
    all_gather x1, blocking collectives, body(): lax.all_gather(task_list * NRB + block_offsets, TASK, axis=1, tiled=True)  6.14 us
    pallas_call x1, Pallas kernels, pack(): pl.pallas_call(pack_kernel, out_shape=jax.ShapeDtypeStruct((blocks, tasks...  2.62 us
    ppermute x1, waiting for transfers between devices, body(): lax.ppermute(away, 'ty', [(i, (i + hop) % row_tasks) for i in range(row_t...  2.21 us
    ppermute x1, waiting for transfers between devices, body(): other = lax.ppermute(send, 'core', [(0, 1), (1, 0)])  1.9 us
  transfers between devices with their start and end apart: 5, of which 4 were waited for; matrix products, arithmetic and copies ran while one was open for 3% of the time, Pallas kernels for 18%

profile of v6, /device:TPU:0, one launch (start us, length us, event | category | flops | bytes accessed | tf_op | source)
XLA Modules:
  0.0 65.8 jit_solution(4542175836239750026)
XLA Ops:
  0.0 2.6 %pack.1 = bf16[8,4,160,128]{3,2,1,0:T(8,128)(2,1)} custom-call(s32[4,8]{1,0:T(4,128)} %bitcast.32, bf16[8,8,128,128]{3,2,1,0:T(8,128)(2,1)} %bitcast.27, bf16[8,8,4,32,128]{4,3,2,1,0:T(8,128)(2,1)} %bitcast.28), custom_call_target="tpu_custom_call" | custom-call | tf_op jit(solution)/shard_map/pack/pallas_call | solution.py:57
  2.6 0.0 copy-start.1
  2.6 0.0 copy-start.2
  2.7 0.0 copy-start
  2.7 7.3 %all-to-all-start = ((bf16[32,160,128]{2,1,0:T(8,128)(2,1)}), bf16[32,160,128]{2,1,0:T(8,128)(2,1)S(1)}, u32[]{:S(2)}, u32[]{:S(2)}) async-start(bf16[32,160,128]{2,1,0:T(8,128)(2,1)} %bitcast.29), calls=%async_computation | async-start | bytes 2621440 | tf_op jit(solution)/shard_map/all_to_all | solution.py:187
  10.0 0.0 copy-done.1
  10.0 0.0 copy-done.2
  10.0 6.1 %all_gather.3 = s32[8,4,4,2]{0,2,3,1:T(4,128)S(1)} all-gather(s32[8,1,4,2]{0,2,3,1:T(4,128)S(1)} %copy_add_fusion), channel_id=1, replica_groups=mesh['blk'=8,'ty'=2,'core'=2] {'ty','core'}, dimensions={1}, use_global_device_ids=true | all-gather | bytes 1280 | tf_op jit(solution)/shard_map/all_gather | solution.py:189
  16.2 0.0 copy-done
  16.2 0.1 broadcast_in_dim.33
  16.2 0.1 broadcast_in_dim.34
  16.4 0.1 copy.23
  16.4 0.1 squeeze.22
  16.5 4.1 %pick.2 = (bf16[32,32,128]{2,1,0:T(8,128)(2,1)S(1)}, bf16[32,32,128]{2,1,0:T(8,128)(2,1)S(1)}) custom-call(s32[32]{0:T(128)S(1)} %fusion.3.lists, bf16[128,256,128]{2,1,0:T(8,128)(2,1)} %amplitudes.3), custom_call_target="tpu_custom_call" | custom-call | flops 134217728 | bytes 4718592 | tf_op jit(solution)/shard_map/pick/pallas_call | solution.py:123
  20.6 0.4 collective-permute-start
  21.0 0.1 copy.21
  21.1 0.1 squeeze.20
  21.2 1.1 %collective-permute-done = bf16[32,32,128]{2,1,0:T(8,128)(2,1)S(1)} collective-permute-done((bf16[32,32,128]{2,1,0:T(8,128)(2,1)S(1)}, bf16[32,32,128]{2,1,0:T(8,128)(2,1)S(1)}, u32[]{:S(2)}, u32[]{:S(2)}) %collective-permute-start) | collective-permute-done | bytes 262176 | tf_op jit(solution)/shard_map/ppermute | solution.py:201
  22.2 0.1 add.46
  22.3 0.9 %collective-permute-start.1 = (bf16[32,32,128]{2,1,0:T(8,128)(2,1)S(1)}, bf16[32,32,128]{2,1,0:T(8,128)(2,1)S(1)}, u32[]{:S(2)}, u32[]{:S(2)}) collective-permute-start(bf16[32,32,128]{2,1,0:T(8,128)(2,1)S(1)} %add.46), channel_id=1, source_target_pairs={{0,2},{2,0},{1,3},{3,1},{4,6},{6,4},{5,7},{7,5},{8,10},{10,8},{9,1... | collective-permute-start | bytes 786440 | tf_op jit(solution)/shard_map/ppermute | solution.py:202
  23.2 0.1 pad_add_fusion.1.lists
  23.3 7.8 %pick.3 = (bf16[32,32,128]{2,1,0:T(8,128)(2,1)S(1)}, bf16[32,32,128]{2,1,0:T(8,128)(2,1)S(1)}, bf16[32,128,128]{2,1,0:T(8,128)(2,1)S(1)}) custom-call(s32[64]{0:T(128)S(1)} %pad_add_fusion.1.lists, bf16[128,256,128]{2,1,0:T(8,128)(2,1)} %amplitudes.3), custom_call_target="tpu_custom_call" | custom-call | flops 536870912 | bytes 10485760 | tf_op jit(solution)/shard_map/pick/pallas_call | solution.py:123
  31.1 0.1 collective-permute-start.2
  31.2 0.1 copy.22
  31.3 0.1 reshape.27
  31.3 0.1 pad_add_fusion.meta
  31.4 2.2 %collective-permute-done.1 = bf16[32,32,128]{2,1,0:T(8,128)(2,1)S(1)} collective-permute-done((bf16[32,32,128]{2,1,0:T(8,128)(2,1)S(1)}, bf16[32,32,128]{2,1,0:T(8,128)(2,1)S(1)}, u32[]{:S(2)}, u32[]{:S(2)}) %collective-permute-start.1) | collective-permute-done | bytes 262176 | tf_op jit(solution)/shard_map/ppermute | solution.py:202
  33.6 0.0 collective-permute-done.2
  33.6 1.0 %add_add_fusion.extras = bf16[32,32,128]{2,1,0:T(8,128)(2,1)S(1)} fusion(bf16[32,32,128]{2,1,0:T(8,128)(2,1)} %collective-permute-done.2, bf16[32,32,128]{2,1,0:T(8,128)(2,1)S(1)} %get-tuple-element.23, bf16[32,32,128]{2,1,0:T(8,128)(2,1)S(1)} %collective-permute-done.1), kind=kLoop, calls=%fused_computation | loop fusion | flops 262144 | bytes 1048576 | tf_op jit(solution)/shard_map/add | solution.py:211
  34.6 7.2 %all-to-all-done.tiles = bf16[32,160,128]{2,1,0:T(8,128)(2,1)S(1)} async-done(((bf16[32,160,128]{2,1,0:T(8,128)(2,1)}), bf16[32,160,128]{2,1,0:T(8,128)(2,1)S(1)}, u32[]{:S(2)}, u32[]{:S(2)}) %all-to-all-start) | async-done | bytes 1310752 | tf_op jit(solution)/shard_map/all_to_all | solution.py:187
  41.9 1.4 %ladder.1 = (f32[8,2,4,16,128]{4,3,2,1,0:T(8,128)S(1)}, f32[8,2,4,16,128]{4,3,2,1,0:T(8,128)S(1)}) custom-call(s32[65]{0:T(128)S(1)} %pad_add_fusion.meta, bf16[32,128,128]{2,1,0:T(8,128)(2,1)S(1)} %get-tuple-element.22.columns, bf16[32,160,128]{2,1,0:T(8,128)(2,1)S(1)} %all-to-all-done.tiles, bf16[32,32,128]{2,1,0:T(8,128)(2,1)S(1)} %add_add_fusion.extras), custom_call_target="tpu_custom_call" | custom-call | flops 167772160 | bytes 3670016 | tf_op jit(solution)/shard_map/ladder/pallas_call | solution.py:215
  43.3 0.1 collective-permute-start.3
  43.4 1.9 %collective-permute-done.3 = f32[8,2,4,16,128]{4,3,2,1,0:T(8,128)S(1)} collective-permute-done((f32[8,2,4,16,128]{4,3,2,1,0:T(8,128)S(1)}, f32[8,2,4,16,128]{4,3,2,1,0:T(8,128)S(1)}, u32[]{:S(2)}, u32[]{:S(2)}) %collective-permute-start.3) | collective-permute-done | bytes 524320 | tf_op jit(solution)/shard_map/ppermute | solution.py:230
  45.3 0.1 add.49
  45.4 19.8 %all_to_all.10 = f32[16,4,16,128]{3,2,1,0:T(8,128)S(1)} all-to-all(f32[16,4,16,128]{3,2,1,0:T(8,128)S(1)} %bitcast.30), channel_id=1, replica_groups=mesh['blk'=8,'ty'=2,'core'=2] {'blk','ty'}, dimensions={0} | all-to-all | bytes 1048576 | tf_op jit(solution)/shard_map/all_to_all | solution.py:232
  65.2 0.6 copy_bitcast_fusion
  (10 shorter events, 0.1 us)
Async XLA Ops:
  2.6 7.4 %copy-start.1 = (s32[8,1,4,2]{0,3,2,1:T(2,128)S(1)}, s32[8,1,4,2]{0,3,2,1:T(2,128)}, u32[]{:S(2)}) copy-start(s32[8,1,4,2]{0,3,2,1:T(2,128)} %param.8) | copy-start | bytes 772
  2.6 7.4 %copy-start.2 = (s32[8,1,4,2]{0,3,2,1:T(2,128)S(1)}, s32[8,1,4,2]{0,3,2,1:T(2,128)}, u32[]{:S(2)}) copy-start(s32[8,1,4,2]{0,3,2,1:T(2,128)} %param.7) | copy-start | bytes 772
  2.7 13.5 %copy-start = (s32[8,1,4]{0,2,1:T(4,128)S(1)}, s32[8,1,4]{0,2,1:T(4,128)}, u32[]{:S(2)}) copy-start(s32[8,1,4]{0,2,1:T(4,128)} %param.9) | copy-start | bytes 388
  2.7 39.2 %all-to-all-start = ((bf16[32,160,128]{2,1,0:T(8,128)(2,1)}), bf16[32,160,128]{2,1,0:T(8,128)(2,1)S(1)}, u32[]{:S(2)}, u32[]{:S(2)}) async-start(bf16[32,160,128]{2,1,0:T(8,128)(2,1)} %bitcast.29), calls=%async_computation | async-start | bytes 2621440 | tf_op jit(solution)/shard_map/all_to_all | solution.py:187
  20.6 1.6 %collective-permute-start = (bf16[32,32,128]{2,1,0:T(8,128)(2,1)S(1)}, bf16[32,32,128]{2,1,0:T(8,128)(2,1)S(1)}, u32[]{:S(2)}, u32[]{:S(2)}) collective-permute-start(bf16[32,32,128]{2,1,0:T(8,128)(2,1)S(1)} %get-tuple-element.19), channel_id=1, source_target_pairs={{0,1},{1,0},{2,3},{3,2},{4,5},{5,4},{6,7},{7,6},{8,9},{9,8},{10,11... | collective-permute-start | bytes 786440 | tf_op jit(solution)/shard_map/ppermute | solution.py:201
  22.3 11.3 %collective-permute-start.1 = (bf16[32,32,128]{2,1,0:T(8,128)(2,1)S(1)}, bf16[32,32,128]{2,1,0:T(8,128)(2,1)S(1)}, u32[]{:S(2)}, u32[]{:S(2)}) collective-permute-start(bf16[32,32,128]{2,1,0:T(8,128)(2,1)S(1)} %add.46), channel_id=1, source_target_pairs={{0,2},{2,0},{1,3},{3,1},{4,6},{6,4},{5,7},{7,5},{8,10},{10,8},{9,1... | collective-permute-start | bytes 786440 | tf_op jit(solution)/shard_map/ppermute | solution.py:202
  31.1 2.6 %collective-permute-start.2 = (bf16[32,32,128]{2,1,0:T(8,128)(2,1)S(1)}, bf16[32,32,128]{2,1,0:T(8,128)(2,1)}, u32[]{:S(2)}, u32[]{:S(2)}) collective-permute-start(bf16[32,32,128]{2,1,0:T(8,128)(2,1)S(1)} %get-tuple-element.24), channel_id=1, source_target_pairs={{0,1},{1,0},{2,3},{3,2},{4,5},{5,4},{6,7},{7,6},{8,9},{9,8},{10,11... | collective-permute-start | bytes 786440 | tf_op jit(solution)/shard_map/ppermute | solution.py:210
  43.3 2.0 %collective-permute-start.3 = (f32[8,2,4,16,128]{4,3,2,1,0:T(8,128)S(1)}, f32[8,2,4,16,128]{4,3,2,1,0:T(8,128)S(1)}, u32[]{:S(2)}, u32[]{:S(2)}) collective-permute-start(f32[8,2,4,16,128]{4,3,2,1,0:T(8,128)S(1)} %get-tuple-element.26), channel_id=1, source_target_pairs={{0,1},{1,0},{2,3},{3,2},{4,5},{5,4},{6,7},{7,6},{8,9},{9,8},{10,11... | collective-permute-start | bytes 1572872 | tf_op jit(solution)/shard_map/ppermute | solution.py:230

commit v7 on v6

--- a/solution.py
+++ b/solution.py
@@ -171,6 +171,37 @@
                 send[block, task, row] = total[(2 * task + 1 - core) * rows + row, span, :]
 
 
+STEPS, TOP, FLOOR = 64.0, 32752.0, 2.0**-111
+
+
+def code_kernel(keep, other, out):
+    rows = out.shape[1] - 8
+    lane = lax.broadcasted_iota(jnp.int32, (8, out.shape[2]), 1)
+    for to in range(out.shape[0]):
+        value = (keep[to] + other[to]).reshape(rows, out.shape[2])
+        largest = jnp.maximum(jnp.max(jnp.abs(value), axis=1, keepdims=True), FLOOR)
+        level = jnp.floor(jnp.log2(largest) * STEPS) + 2.0
+        out[to, :rows] = jnp.round(value * (jnp.exp2(level * (-1.0 / STEPS)) * TOP)).astype(jnp.int32).astype(jnp.int16)
+        scales = jnp.zeros(lane.shape, jnp.float32)
+        for group in range(rows // 8):
+            scales = jnp.where(lane == group, level[8 * group : 8 * group + 8], scales)
+        out[to, rows:] = scales.astype(jnp.int32).astype(jnp.int16)
+
+
+def decode_kernel(parts, out):
+    pairs, width = out.shape[0], parts.shape[2]
+    rows = parts.shape[1] - 8
+    total = [jnp.zeros((8, width), jnp.float32)] * (rows // 8)
+    for source in range(parts.shape[0]):
+        scales = jnp.exp2(parts[source, rows:].astype(jnp.int32).astype(jnp.float32) * (1.0 / STEPS)) * (1.0 / TOP)
+        value = parts[source, :rows].astype(jnp.int32).astype(jnp.float32)
+        for group in range(rows // 8):
+            total[group] += value[8 * group : 8 * group + 8] * scales[:, group : group + 1]
+    for group in range(rows // 8):
+        first = 8 * group
+        out[first % pairs : first % pairs + 8, first // pairs * width : (first // pairs + 1) * width] = total[group]
+
+
 def body(amplitudes, integral_tiles, task_list, block_offsets, tile_counts, *, shape):
     blocks, row_tasks = shape
     tasks = 2 * row_tasks
@@ -228,10 +259,25 @@
     )(meta, columns, arrived, extras)
 
     other = lax.ppermute(send, "core", [(0, 1), (1, 0)])
-    half = (keep + other).reshape(blocks * row_tasks, rows, pairs, row_block)
-    parts = lax.all_to_all(half, ("blk", "ty"), 0, 0, tiled=True)
-    out = jnp.sum(parts, axis=0)
-    return jnp.transpose(out, (1, 0, 2)).reshape(pairs, rows * row_block)
+    peers = blocks * row_tasks
+    cut = (peers, rows, pairs, row_block)
+    coded = pl.pallas_call(
+        code_kernel,
+        out_shape=jax.ShapeDtypeStruct((peers, rows * pairs + 8, row_block), jnp.int16),
+        in_specs=[in_vmem, in_vmem],
+        out_specs=in_vmem,
+        compiler_params=pltpu.CompilerParams(vmem_limit_bytes=16 << 20),
+        name="code",
+    )(keep.reshape(cut), other.reshape(cut))
+    parts = lax.all_to_all(coded, ("blk", "ty"), 0, 0, tiled=True)
+    return pl.pallas_call(
+        decode_kernel,
+        out_shape=jax.ShapeDtypeStruct((pairs, rows * row_block), jnp.float32),
+        in_specs=[in_vmem],
+        out_specs=in_vmem,
+        compiler_params=pltpu.CompilerParams(vmem_limit_bytes=16 << 20),
+        name="decode",
+    )(parts)
 
 
 def solution(mesh):

time: 66.1 us -> 62.3 us (0.943)
  blocking collectives: 25.9 us -> 21.5 us
  Pallas kernels: 15.9 us -> 17.2 us
    all_to_all x1, blocking collectives: 19.8 us -> 15.4 us  [body(): parts = lax.all_to_all(coded, ('blk', 'ty'), 0, 0, tiled=True)]
    pallas_call x0 -> x2, Pallas kernels: none -> 1.23 us  [the longest x1 0.92 us: body(): pl.pallas_call(decode_kernel, out_shape=jax.ShapeDtypeStruct((pairs, rows...]
  transfers between devices with their start and end apart: 5 -> 5, of which waited for: 4 -> 4; matrix products, arithmetic and copies ran while one was open for 3% -> 3% of each run, Pallas kernels for 18% -> 19%
where the time goes in v7:
time: 62.3 us; the launch traced here: 62 us
  blocking collectives  21.5 us (35%)
  Pallas kernels  17.2 us (28%)
  waiting for transfers between devices  12.4 us (20%)
  starting transfers between devices  8.73 us (14%)
  other arithmetic  1.3 us (2%)
  local copies, waits for them, and re-layouts  0.69 us (1%)
    all_to_all x1, blocking collectives, body(): parts = lax.all_to_all(coded, ('blk', 'ty'), 0, 0, tiled=True)  15.4 us
    pallas_call x2, Pallas kernels, pick(): pl.pallas_call(functools.partial(pick_kernel, hop=hop, row_tasks=row_task...  11.8 us
    all_to_all x1, starting transfers between devices, body(): arrived = lax.all_to_all(sent, EVERY, 0, 0, tiled=True)  7.3 us
    all_to_all x1, waiting for transfers between devices, body(): arrived = lax.all_to_all(sent, EVERY, 0, 0, tiled=True)  7.24 us
    all_gather x1, blocking collectives, body(): lax.all_gather(task_list * NRB + block_offsets, TASK, axis=1, tiled=True)  6.14 us
    pallas_call x1, Pallas kernels, pack(): pl.pallas_call(pack_kernel, out_shape=jax.ShapeDtypeStruct((blocks, tasks...  2.67 us
    ppermute x1, waiting for transfers between devices, body(): lax.ppermute(away, 'ty', [(i, (i + hop) % row_tasks) for i in range(row_t...  2.21 us
    ppermute x1, waiting for transfers between devices, body(): other = lax.ppermute(send, 'core', [(0, 1), (1, 0)])  1.9 us
  transfers between devices with their start and end apart: 5, of which 4 were waited for; matrix products, arithmetic and copies ran while one was open for 3% of the time, Pallas kernels for 19%

profile of v7, /device:TPU:0, one launch (start us, length us, event | category | flops | bytes accessed | tf_op | source)
XLA Modules:
  0.0 62.0 jit_solution(8830023194682532166)
XLA Ops:
  0.0 2.7 %pack.1 = bf16[8,4,160,128]{3,2,1,0:T(8,128)(2,1)} custom-call(s32[4,8]{1,0:T(4,128)} %bitcast.28, bf16[8,8,128,128]{3,2,1,0:T(8,128)(2,1)} %bitcast.24, bf16[8,8,4,32,128]{4,3,2,1,0:T(8,128)(2,1)} %bitcast.25), custom_call_target="tpu_custom_call" | custom-call | tf_op jit(solution)/shard_map/pack/pallas_call | solution.py:57
  2.7 0.0 copy-start.1
  2.7 0.0 copy-start.2
  2.7 0.0 copy-start
  2.7 7.3 %all-to-all-start = ((bf16[32,160,128]{2,1,0:T(8,128)(2,1)}), bf16[32,160,128]{2,1,0:T(8,128)(2,1)S(1)}, u32[]{:S(2)}, u32[]{:S(2)}) async-start(bf16[32,160,128]{2,1,0:T(8,128)(2,1)} %bitcast.26), calls=%async_computation | async-start | bytes 2621440 | tf_op jit(solution)/shard_map/all_to_all | solution.py:218
  10.0 0.0 copy-done.1
  10.0 0.0 copy-done.2
  10.1 6.1 %all_gather.3 = s32[8,4,4,2]{0,2,3,1:T(4,128)S(1)} all-gather(s32[8,1,4,2]{0,2,3,1:T(4,128)S(1)} %copy_add_fusion), channel_id=1, replica_groups=mesh['blk'=8,'ty'=2,'core'=2] {'ty','core'}, dimensions={1}, use_global_device_ids=true | all-gather | bytes 1280 | tf_op jit(solution)/shard_map/all_gather | solution.py:220
  16.2 0.0 copy-done
  16.2 0.1 broadcast_in_dim.33
  16.3 0.1 broadcast_in_dim.34
  16.4 0.1 copy.17
  16.5 0.1 squeeze.22
  16.6 4.1 %pick.2 = (bf16[32,32,128]{2,1,0:T(8,128)(2,1)S(1)}, bf16[32,32,128]{2,1,0:T(8,128)(2,1)S(1)}) custom-call(s32[32]{0:T(128)S(1)} %fusion.3.lists, bf16[128,256,128]{2,1,0:T(8,128)(2,1)} %amplitudes.3), custom_call_target="tpu_custom_call" | custom-call | flops 134217728 | bytes 4718592 | tf_op jit(solution)/shard_map/pick/pallas_call | solution.py:123
  20.7 0.4 collective-permute-start
  21.0 0.1 copy.15
  21.1 0.1 squeeze.20
  21.2 1.1 %collective-permute-done = bf16[32,32,128]{2,1,0:T(8,128)(2,1)S(1)} collective-permute-done((bf16[32,32,128]{2,1,0:T(8,128)(2,1)S(1)}, bf16[32,32,128]{2,1,0:T(8,128)(2,1)S(1)}, u32[]{:S(2)}, u32[]{:S(2)}) %collective-permute-start) | collective-permute-done | bytes 262176 | tf_op jit(solution)/shard_map/ppermute | solution.py:232
  22.3 0.1 add.43
  22.3 0.9 %collective-permute-start.1 = (bf16[32,32,128]{2,1,0:T(8,128)(2,1)S(1)}, bf16[32,32,128]{2,1,0:T(8,128)(2,1)S(1)}, u32[]{:S(2)}, u32[]{:S(2)}) collective-permute-start(bf16[32,32,128]{2,1,0:T(8,128)(2,1)S(1)} %add.43), channel_id=1, source_target_pairs={{0,2},{2,0},{1,3},{3,1},{4,6},{6,4},{5,7},{7,5},{8,10},{10,8},{9,1... | collective-permute-start | bytes 786440 | tf_op jit(solution)/shard_map/ppermute | solution.py:233
  23.2 0.1 pad_add_fusion.1.lists
  23.3 7.8 %pick.3 = (bf16[32,32,128]{2,1,0:T(8,128)(2,1)S(1)}, bf16[32,32,128]{2,1,0:T(8,128)(2,1)S(1)}, bf16[32,128,128]{2,1,0:T(8,128)(2,1)S(1)}) custom-call(s32[64]{0:T(128)S(1)} %pad_add_fusion.1.lists, bf16[128,256,128]{2,1,0:T(8,128)(2,1)} %amplitudes.3), custom_call_target="tpu_custom_call" | custom-call | flops 536870912 | bytes 10485760 | tf_op jit(solution)/shard_map/pick/pallas_call | solution.py:123
  31.1 0.1 collective-permute-start.2
  31.2 0.1 copy.16
  31.3 0.1 reshape.27
  31.4 0.1 pad_add_fusion.meta
  31.5 2.2 %collective-permute-done.1 = bf16[32,32,128]{2,1,0:T(8,128)(2,1)S(1)} collective-permute-done((bf16[32,32,128]{2,1,0:T(8,128)(2,1)S(1)}, bf16[32,32,128]{2,1,0:T(8,128)(2,1)S(1)}, u32[]{:S(2)}, u32[]{:S(2)}) %collective-permute-start.1) | collective-permute-done | bytes 262176 | tf_op jit(solution)/shard_map/ppermute | solution.py:233
  33.7 0.0 collective-permute-done.2
  33.7 1.0 %add_add_fusion.extras = bf16[32,32,128]{2,1,0:T(8,128)(2,1)S(1)} fusion(bf16[32,32,128]{2,1,0:T(8,128)(2,1)} %collective-permute-done.2, bf16[32,32,128]{2,1,0:T(8,128)(2,1)S(1)} %get-tuple-element.23, bf16[32,32,128]{2,1,0:T(8,128)(2,1)S(1)} %collective-permute-done.1), kind=kLoop, calls=%fused_computation | loop fusion | flops 262144 | bytes 1048576 | tf_op jit(solution)/shard_map/add | solution.py:242
  34.7 7.2 %all-to-all-done.tiles = bf16[32,160,128]{2,1,0:T(8,128)(2,1)S(1)} async-done(((bf16[32,160,128]{2,1,0:T(8,128)(2,1)}), bf16[32,160,128]{2,1,0:T(8,128)(2,1)S(1)}, u32[]{:S(2)}, u32[]{:S(2)}) %all-to-all-start) | async-done | bytes 1310752 | tf_op jit(solution)/shard_map/all_to_all | solution.py:218
  41.9 1.4 %ladder.1 = (f32[8,2,4,16,128]{4,3,2,1,0:T(8,128)S(1)}, f32[8,2,4,16,128]{4,3,2,1,0:T(8,128)S(1)}) custom-call(s32[65]{0:T(128)S(1)} %pad_add_fusion.meta, bf16[32,128,128]{2,1,0:T(8,128)(2,1)S(1)} %get-tuple-element.22.columns, bf16[32,160,128]{2,1,0:T(8,128)(2,1)S(1)} %all-to-all-done.tiles, bf16[32,32,128]{2,1,0:T(8,128)(2,1)S(1)} %add_add_fusion.extras), custom_call_target="tpu_custom_call" | custom-call | flops 167772160 | bytes 3670016 | tf_op jit(solution)/shard_map/ladder/pallas_call | solution.py:246
  43.4 0.1 collective-permute-start.3
  43.5 1.9 %collective-permute-done.3 = f32[8,2,4,16,128]{4,3,2,1,0:T(8,128)S(1)} collective-permute-done((f32[8,2,4,16,128]{4,3,2,1,0:T(8,128)S(1)}, f32[8,2,4,16,128]{4,3,2,1,0:T(8,128)S(1)}, u32[]{:S(2)}, u32[]{:S(2)}) %collective-permute-start.3) | collective-permute-done | bytes 524320 | tf_op jit(solution)/shard_map/ppermute | solution.py:261
  45.3 0.3 code.1
  45.7 15.4 %all_to_all.10.parts = s16[16,72,128]{2,1,0:T(8,128)(2,1)S(1)} all-to-all(s16[16,72,128]{2,1,0:T(8,128)(2,1)S(1)} %code.1), channel_id=1, replica_groups=mesh['blk'=8,'ty'=2,'core'=2] {'blk','ty'}, dimensions={0} | all-to-all | bytes 589824 | tf_op jit(solution)/shard_map/all_to_all | solution.py:272
  61.0 0.9 %decode.1 = f32[16,512]{1,0:T(8,128)} custom-call(s16[16,72,128]{2,1,0:T(8,128)(2,1)S(1)} %all_to_all.10.parts), custom_call_target="tpu_custom_call" | custom-call | tf_op jit(solution)/shard_map/decode/pallas_call | solution.py:273
  (9 shorter events, 0.1 us)
Async XLA Ops:
  2.7 7.4 %copy-start.1 = (s32[8,1,4,2]{0,3,2,1:T(2,128)S(1)}, s32[8,1,4,2]{0,3,2,1:T(2,128)}, u32[]{:S(2)}) copy-start(s32[8,1,4,2]{0,3,2,1:T(2,128)} %param.8) | copy-start | bytes 772
  2.7 7.4 %copy-start.2 = (s32[8,1,4,2]{0,3,2,1:T(2,128)S(1)}, s32[8,1,4,2]{0,3,2,1:T(2,128)}, u32[]{:S(2)}) copy-start(s32[8,1,4,2]{0,3,2,1:T(2,128)} %param.7) | copy-start | bytes 772
  2.7 13.5 %copy-start = (s32[8,1,4]{0,2,1:T(4,128)S(1)}, s32[8,1,4]{0,2,1:T(4,128)}, u32[]{:S(2)}) copy-start(s32[8,1,4]{0,2,1:T(4,128)} %param.9) | copy-start | bytes 388
  2.7 39.2 %all-to-all-start = ((bf16[32,160,128]{2,1,0:T(8,128)(2,1)}), bf16[32,160,128]{2,1,0:T(8,128)(2,1)S(1)}, u32[]{:S(2)}, u32[]{:S(2)}) async-start(bf16[32,160,128]{2,1,0:T(8,128)(2,1)} %bitcast.26), calls=%async_computation | async-start | bytes 2621440 | tf_op jit(solution)/shard_map/all_to_all | solution.py:218
  20.7 1.6 %collective-permute-start = (bf16[32,32,128]{2,1,0:T(8,128)(2,1)S(1)}, bf16[32,32,128]{2,1,0:T(8,128)(2,1)S(1)}, u32[]{:S(2)}, u32[]{:S(2)}) collective-permute-start(bf16[32,32,128]{2,1,0:T(8,128)(2,1)S(1)} %get-tuple-element.19), channel_id=1, source_target_pairs={{0,1},{1,0},{2,3},{3,2},{4,5},{5,4},{6,7},{7,6},{8,9},{9,8},{10,11... | collective-permute-start | bytes 786440 | tf_op jit(solution)/shard_map/ppermute | solution.py:232
  22.3 11.3 %collective-permute-start.1 = (bf16[32,32,128]{2,1,0:T(8,128)(2,1)S(1)}, bf16[32,32,128]{2,1,0:T(8,128)(2,1)S(1)}, u32[]{:S(2)}, u32[]{:S(2)}) collective-permute-start(bf16[32,32,128]{2,1,0:T(8,128)(2,1)S(1)} %add.43), channel_id=1, source_target_pairs={{0,2},{2,0},{1,3},{3,1},{4,6},{6,4},{5,7},{7,5},{8,10},{10,8},{9,1... | collective-permute-start | bytes 786440 | tf_op jit(solution)/shard_map/ppermute | solution.py:233
  31.1 2.6 %collective-permute-start.2 = (bf16[32,32,128]{2,1,0:T(8,128)(2,1)S(1)}, bf16[32,32,128]{2,1,0:T(8,128)(2,1)}, u32[]{:S(2)}, u32[]{:S(2)}) collective-permute-start(bf16[32,32,128]{2,1,0:T(8,128)(2,1)S(1)} %get-tuple-element.24), channel_id=1, source_target_pairs={{0,1},{1,0},{2,3},{3,2},{4,5},{5,4},{6,7},{7,6},{8,9},{9,8},{10,11... | collective-permute-start | bytes 786440 | tf_op jit(solution)/shard_map/ppermute | solution.py:241
  43.4 2.0 %collective-permute-start.3 = (f32[8,2,4,16,128]{4,3,2,1,0:T(8,128)S(1)}, f32[8,2,4,16,128]{4,3,2,1,0:T(8,128)S(1)}, u32[]{:S(2)}, u32[]{:S(2)}) collective-permute-start(f32[8,2,4,16,128]{4,3,2,1,0:T(8,128)S(1)} %get-tuple-element.26), channel_id=1, source_target_pairs={{0,1},{1,0},{2,3},{3,2},{4,5},{5,4},{6,7},{7,6},{8,9},{9,8},{10,11... | collective-permute-start | bytes 1572872 | tf_op jit(solution)/shard_map/ppermute | solution.py:261

commit v8 on v7

--- a/solution.py
+++ b/solution.py
@@ -145,7 +145,7 @@
     return lax.dot_general(left, right, (((0,), (0,)), ((), ())), preferred_element_type=jnp.float32)
 
 
-def ladder_kernel(meta, columns, tiles, extras, keep, send, total, *, row_tasks, pair_blocks):
+def ladder_kernel(meta, columns, tiles, extras, send, total, *, row_tasks, pair_blocks):
     slots, chunk, _ = columns.shape
     total[...] = jnp.zeros_like(total)
 
@@ -167,18 +167,21 @@
         for block in range(pair_blocks):
             span = pl.ds(block * pairs, pairs)
             for row in range(rows):
-                keep[block, task, row] = total[(2 * task + core) * rows + row, span, :]
                 send[block, task, row] = total[(2 * task + 1 - core) * rows + row, span, :]
 
 
 STEPS, TOP, FLOOR = 64.0, 32752.0, 2.0**-111
 
 
-def code_kernel(keep, other, out):
-    rows = out.shape[1] - 8
-    lane = lax.broadcasted_iota(jnp.int32, (8, out.shape[2]), 1)
-    for to in range(out.shape[0]):
-        value = (keep[to] + other[to]).reshape(rows, out.shape[2])
+def code_kernel(total, other, out, *, row_tasks):
+    peers, blocks, pairs, width = other.shape
+    rows = blocks * pairs
+    core = lax.axis_index("core")
+    lane = lax.broadcasted_iota(jnp.int32, (8, width), 1)
+    for to in range(peers):
+        first = (2 * (to % row_tasks) + core) * blocks
+        own = total[pl.ds(first, blocks), pl.ds(to // row_tasks * pairs, pairs), :]
+        value = (own + other[to]).reshape(rows, width)
         largest = jnp.maximum(jnp.max(jnp.abs(value), axis=1, keepdims=True), FLOOR)
         level = jnp.floor(jnp.log2(largest) * STEPS) + 2.0
         out[to, :rows] = jnp.round(value * (jnp.exp2(level * (-1.0 / STEPS)) * TOP)).astype(jnp.int32).astype(jnp.int16)
@@ -191,15 +194,17 @@
 def decode_kernel(parts, out):
     pairs, width = out.shape[0], parts.shape[2]
     rows = parts.shape[1] - 8
-    total = [jnp.zeros((8, width), jnp.float32)] * (rows // 8)
-    for source in range(parts.shape[0]):
-        scales = jnp.exp2(parts[source, rows:].astype(jnp.int32).astype(jnp.float32) * (1.0 / STEPS)) * (1.0 / TOP)
-        value = parts[source, :rows].astype(jnp.int32).astype(jnp.float32)
-        for group in range(rows // 8):
-            total[group] += value[8 * group : 8 * group + 8] * scales[:, group : group + 1]
+    scales = [
+        jnp.exp2(parts[source, rows:].astype(jnp.int32).astype(jnp.float32) * (1.0 / STEPS)) * (1.0 / TOP)
+        for source in range(parts.shape[0])
+    ]
     for group in range(rows // 8):
         first = 8 * group
-        out[first % pairs : first % pairs + 8, first // pairs * width : (first // pairs + 1) * width] = total[group]
+        total = jnp.zeros((8, width), jnp.float32)
+        for source, scale in enumerate(scales):
+            value = parts[source, first : first + 8].astype(jnp.int32).astype(jnp.float32)
+            total += value * scale[:, group : group + 1]
+        out[first % pairs : first % pairs + 8, first // pairs * width : (first // pairs + 1) * width] = total
 
 
 def body(amplitudes, integral_tiles, task_list, block_offsets, tile_counts, *, shape):
@@ -243,12 +248,11 @@
 
     part = jax.ShapeDtypeStruct((blocks, row_tasks, rows, pairs, row_block), jnp.float32)
     in_vmem = pl.BlockSpec(memory_space=pltpu.VMEM)
-    keep, send = pl.pallas_call(
+    send, total = pl.pallas_call(
         functools.partial(ladder_kernel, row_tasks=row_tasks, pair_blocks=blocks),
-        out_shape=(part, part),
+        out_shape=(part, jax.ShapeDtypeStruct((NRB, pair_total, row_block), jnp.float32)),
         in_specs=[pl.BlockSpec(memory_space=pltpu.SMEM)] + [in_vmem] * 3,
         out_specs=(in_vmem, in_vmem),
-        scratch_shapes=[pltpu.VMEM((NRB, pair_total, row_block), jnp.float32)],
         compiler_params=pltpu.CompilerParams(vmem_limit_bytes=16 << 20),
         cost_estimate=pl.CostEstimate(
             flops=2 * slots * (chunk + piece) * pair_total * row_block,
@@ -262,13 +266,13 @@
     peers = blocks * row_tasks
     cut = (peers, rows, pairs, row_block)
     coded = pl.pallas_call(
-        code_kernel,
+        functools.partial(code_kernel, row_tasks=row_tasks),
         out_shape=jax.ShapeDtypeStruct((peers, rows * pairs + 8, row_block), jnp.int16),
         in_specs=[in_vmem, in_vmem],
         out_specs=in_vmem,
         compiler_params=pltpu.CompilerParams(vmem_limit_bytes=16 << 20),
         name="code",
-    )(keep.reshape(cut), other.reshape(cut))
+    )(total, other.reshape(cut))
     parts = lax.all_to_all(coded, ("blk", "ty"), 0, 0, tiled=True)
     return pl.pallas_call(
         decode_kernel,

time: 62.3 us -> 62.2 us (level)
  no operation moved by 1% of the time
where the time goes in v8:
time: 62.2 us; the launch traced here: 61.8 us
  blocking collectives  21.5 us (35%)
  Pallas kernels  17.1 us (27%)
  waiting for transfers between devices  12.4 us (20%)
  starting transfers between devices  8.73 us (14%)
  other arithmetic  1.3 us (2%)
  local copies, waits for them, and re-layouts  0.69 us (1%)
    all_to_all x1, blocking collectives, body(): parts = lax.all_to_all(coded, ('blk', 'ty'), 0, 0, tiled=True)  15.4 us
    pallas_call x2, Pallas kernels, pick(): pl.pallas_call(functools.partial(pick_kernel, hop=hop, row_tasks=row_task...  11.8 us
    all_to_all x1, starting transfers between devices, body(): arrived = lax.all_to_all(sent, EVERY, 0, 0, tiled=True)  7.3 us
    all_to_all x1, waiting for transfers between devices, body(): arrived = lax.all_to_all(sent, EVERY, 0, 0, tiled=True)  7.24 us
    all_gather x1, blocking collectives, body(): lax.all_gather(task_list * NRB + block_offsets, TASK, axis=1, tiled=True)  6.14 us
    pallas_call x1, Pallas kernels, pack(): pl.pallas_call(pack_kernel, out_shape=jax.ShapeDtypeStruct((blocks, tasks...  2.67 us
    ppermute x1, waiting for transfers between devices, body(): lax.ppermute(away, 'ty', [(i, (i + hop) % row_tasks) for i in range(row_t...  2.21 us
    ppermute x1, waiting for transfers between devices, body(): other = lax.ppermute(send, 'core', [(0, 1), (1, 0)])  1.9 us
  transfers between devices with their start and end apart: 5, of which 4 were waited for; matrix products, arithmetic and copies ran while one was open for 3% of the time, Pallas kernels for 19%

profile of v8, /device:TPU:0, one launch (start us, length us, event | category | flops | bytes accessed | tf_op | source)
XLA Modules:
  0.0 61.8 jit_solution(15958662347808371011)
XLA Ops:
  0.0 2.7 %pack.1 = bf16[8,4,160,128]{3,2,1,0:T(8,128)(2,1)} custom-call(s32[4,8]{1,0:T(4,128)} %bitcast.26, bf16[8,8,128,128]{3,2,1,0:T(8,128)(2,1)} %bitcast.22, bf16[8,8,4,32,128]{4,3,2,1,0:T(8,128)(2,1)} %bitcast.23), custom_call_target="tpu_custom_call" | custom-call | tf_op jit(solution)/shard_map/pack/pallas_call | solution.py:57
  2.7 0.0 copy-start.1
  2.7 0.0 copy-start.2
  2.7 0.0 copy-start
  2.7 7.3 %all-to-all-start = ((bf16[32,160,128]{2,1,0:T(8,128)(2,1)}), bf16[32,160,128]{2,1,0:T(8,128)(2,1)S(1)}, u32[]{:S(2)}, u32[]{:S(2)}) async-start(bf16[32,160,128]{2,1,0:T(8,128)(2,1)} %bitcast.24), calls=%async_computation | async-start | bytes 2621440 | tf_op jit(solution)/shard_map/all_to_all | solution.py:223
  10.0 0.0 copy-done.1
  10.0 0.0 copy-done.2
  10.1 6.1 %all_gather.3 = s32[8,4,4,2]{0,2,3,1:T(4,128)S(1)} all-gather(s32[8,1,4,2]{0,2,3,1:T(4,128)S(1)} %copy_add_fusion), channel_id=1, replica_groups=mesh['blk'=8,'ty'=2,'core'=2] {'ty','core'}, dimensions={1}, use_global_device_ids=true | all-gather | bytes 1280 | tf_op jit(solution)/shard_map/all_gather | solution.py:225
  16.2 0.0 copy-done
  16.2 0.1 broadcast_in_dim.33
  16.3 0.1 broadcast_in_dim.34
  16.4 0.1 copy.17
  16.5 0.1 squeeze.22
  16.6 4.1 %pick.2 = (bf16[32,32,128]{2,1,0:T(8,128)(2,1)S(1)}, bf16[32,32,128]{2,1,0:T(8,128)(2,1)S(1)}) custom-call(s32[32]{0:T(128)S(1)} %fusion.3.lists, bf16[128,256,128]{2,1,0:T(8,128)(2,1)} %amplitudes.3), custom_call_target="tpu_custom_call" | custom-call | flops 134217728 | bytes 4718592 | tf_op jit(solution)/shard_map/pick/pallas_call | solution.py:123
  20.7 0.4 collective-permute-start
  21.0 0.1 copy.15
  21.1 0.1 squeeze.20
  21.2 1.1 %collective-permute-done = bf16[32,32,128]{2,1,0:T(8,128)(2,1)S(1)} collective-permute-done((bf16[32,32,128]{2,1,0:T(8,128)(2,1)S(1)}, bf16[32,32,128]{2,1,0:T(8,128)(2,1)S(1)}, u32[]{:S(2)}, u32[]{:S(2)}) %collective-permute-start) | collective-permute-done | bytes 262176 | tf_op jit(solution)/shard_map/ppermute | solution.py:237
  22.3 0.1 add.43
  22.3 0.9 %collective-permute-start.1 = (bf16[32,32,128]{2,1,0:T(8,128)(2,1)S(1)}, bf16[32,32,128]{2,1,0:T(8,128)(2,1)S(1)}, u32[]{:S(2)}, u32[]{:S(2)}) collective-permute-start(bf16[32,32,128]{2,1,0:T(8,128)(2,1)S(1)} %add.43), channel_id=1, source_target_pairs={{0,2},{2,0},{1,3},{3,1},{4,6},{6,4},{5,7},{7,5},{8,10},{10,8},{9,1... | collective-permute-start | bytes 786440 | tf_op jit(solution)/shard_map/ppermute | solution.py:238
  23.2 0.1 pad_add_fusion.1.lists
  23.3 7.8 %pick.3 = (bf16[32,32,128]{2,1,0:T(8,128)(2,1)S(1)}, bf16[32,32,128]{2,1,0:T(8,128)(2,1)S(1)}, bf16[32,128,128]{2,1,0:T(8,128)(2,1)S(1)}) custom-call(s32[64]{0:T(128)S(1)} %pad_add_fusion.1.lists, bf16[128,256,128]{2,1,0:T(8,128)(2,1)} %amplitudes.3), custom_call_target="tpu_custom_call" | custom-call | flops 536870912 | bytes 10485760 | tf_op jit(solution)/shard_map/pick/pallas_call | solution.py:123
  31.1 0.1 collective-permute-start.2
  31.2 0.1 copy.16
  31.3 0.1 reshape.24
  31.4 0.1 pad_add_fusion.meta
  31.5 2.2 %collective-permute-done.1 = bf16[32,32,128]{2,1,0:T(8,128)(2,1)S(1)} collective-permute-done((bf16[32,32,128]{2,1,0:T(8,128)(2,1)S(1)}, bf16[32,32,128]{2,1,0:T(8,128)(2,1)S(1)}, u32[]{:S(2)}, u32[]{:S(2)}) %collective-permute-start.1) | collective-permute-done | bytes 262176 | tf_op jit(solution)/shard_map/ppermute | solution.py:238
  33.7 0.0 collective-permute-done.2
  33.7 1.0 %add_add_fusion.extras = bf16[32,32,128]{2,1,0:T(8,128)(2,1)S(1)} fusion(bf16[32,32,128]{2,1,0:T(8,128)(2,1)} %collective-permute-done.2, bf16[32,32,128]{2,1,0:T(8,128)(2,1)S(1)} %get-tuple-element.23, bf16[32,32,128]{2,1,0:T(8,128)(2,1)S(1)} %collective-permute-done.1), kind=kLoop, calls=%fused_computation | loop fusion | flops 262144 | bytes 1048576 | tf_op jit(solution)/shard_map/add | solution.py:247
  34.7 7.2 %all-to-all-done.tiles = bf16[32,160,128]{2,1,0:T(8,128)(2,1)S(1)} async-done(((bf16[32,160,128]{2,1,0:T(8,128)(2,1)}), bf16[32,160,128]{2,1,0:T(8,128)(2,1)S(1)}, u32[]{:S(2)}, u32[]{:S(2)}) %all-to-all-start) | async-done | bytes 1310752 | tf_op jit(solution)/shard_map/all_to_all | solution.py:223
  41.9 1.4 %ladder.1 = (f32[8,2,4,16,128]{4,3,2,1,0:T(8,128)S(1)}, f32[16,128,128]{2,1,0:T(8,128)S(1)}) custom-call(s32[65]{0:T(128)S(1)} %pad_add_fusion.meta, bf16[32,128,128]{2,1,0:T(8,128)(2,1)S(1)} %get-tuple-element.22.columns, bf16[32,160,128]{2,1,0:T(8,128)(2,1)S(1)} %all-to-all-done.tiles, bf16[32,32,128]{2,1,0:T(8,128)(2,1)S(1)} %add_add_fusion.extras), custom_call_target="tpu_custom_call" | custom-call | flops 167772160 | bytes 3670016 | tf_op jit(solution)/shard_map/ladder/pallas_call | solution.py:251
  43.3 0.1 collective-permute-start.3
  43.4 1.9 %collective-permute-done.3 = f32[8,2,4,16,128]{4,3,2,1,0:T(8,128)S(1)} collective-permute-done((f32[8,2,4,16,128]{4,3,2,1,0:T(8,128)S(1)}, f32[8,2,4,16,128]{4,3,2,1,0:T(8,128)S(1)}, u32[]{:S(2)}, u32[]{:S(2)}) %collective-permute-start.3) | collective-permute-done | bytes 524320 | tf_op jit(solution)/shard_map/ppermute | solution.py:265
  45.3 0.3 code.1
  45.6 15.4 %all_to_all.10.parts = s16[16,72,128]{2,1,0:T(8,128)(2,1)S(1)} all-to-all(s16[16,72,128]{2,1,0:T(8,128)(2,1)S(1)} %code.1), channel_id=1, replica_groups=mesh['blk'=8,'ty'=2,'core'=2] {'blk','ty'}, dimensions={0} | all-to-all | bytes 589824 | tf_op jit(solution)/shard_map/all_to_all | solution.py:276
  61.0 0.8 %decode.1 = f32[16,512]{1,0:T(8,128)} custom-call(s16[16,72,128]{2,1,0:T(8,128)(2,1)S(1)} %all_to_all.10.parts), custom_call_target="tpu_custom_call" | custom-call | tf_op jit(solution)/shard_map/decode/pallas_call | solution.py:277
  (9 shorter events, 0.1 us)
Async XLA Ops:
  2.7 7.4 %copy-start.1 = (s32[8,1,4,2]{0,3,2,1:T(2,128)S(1)}, s32[8,1,4,2]{0,3,2,1:T(2,128)}, u32[]{:S(2)}) copy-start(s32[8,1,4,2]{0,3,2,1:T(2,128)} %param.8) | copy-start | bytes 772
  2.7 7.4 %copy-start.2 = (s32[8,1,4,2]{0,3,2,1:T(2,128)S(1)}, s32[8,1,4,2]{0,3,2,1:T(2,128)}, u32[]{:S(2)}) copy-start(s32[8,1,4,2]{0,3,2,1:T(2,128)} %param.7) | copy-start | bytes 772
  2.7 13.5 %copy-start = (s32[8,1,4]{0,2,1:T(4,128)S(1)}, s32[8,1,4]{0,2,1:T(4,128)}, u32[]{:S(2)}) copy-start(s32[8,1,4]{0,2,1:T(4,128)} %param.9) | copy-start | bytes 388
  2.7 39.2 %all-to-all-start = ((bf16[32,160,128]{2,1,0:T(8,128)(2,1)}), bf16[32,160,128]{2,1,0:T(8,128)(2,1)S(1)}, u32[]{:S(2)}, u32[]{:S(2)}) async-start(bf16[32,160,128]{2,1,0:T(8,128)(2,1)} %bitcast.24), calls=%async_computation | async-start | bytes 2621440 | tf_op jit(solution)/shard_map/all_to_all | solution.py:223
  20.7 1.6 %collective-permute-start = (bf16[32,32,128]{2,1,0:T(8,128)(2,1)S(1)}, bf16[32,32,128]{2,1,0:T(8,128)(2,1)S(1)}, u32[]{:S(2)}, u32[]{:S(2)}) collective-permute-start(bf16[32,32,128]{2,1,0:T(8,128)(2,1)S(1)} %get-tuple-element.19), channel_id=1, source_target_pairs={{0,1},{1,0},{2,3},{3,2},{4,5},{5,4},{6,7},{7,6},{8,9},{9,8},{10,11... | collective-permute-start | bytes 786440 | tf_op jit(solution)/shard_map/ppermute | solution.py:237
  22.3 11.3 %collective-permute-start.1 = (bf16[32,32,128]{2,1,0:T(8,128)(2,1)S(1)}, bf16[32,32,128]{2,1,0:T(8,128)(2,1)S(1)}, u32[]{:S(2)}, u32[]{:S(2)}) collective-permute-start(bf16[32,32,128]{2,1,0:T(8,128)(2,1)S(1)} %add.43), channel_id=1, source_target_pairs={{0,2},{2,0},{1,3},{3,1},{4,6},{6,4},{5,7},{7,5},{8,10},{10,8},{9,1... | collective-permute-start | bytes 786440 | tf_op jit(solution)/shard_map/ppermute | solution.py:238
  31.1 2.6 %collective-permute-start.2 = (bf16[32,32,128]{2,1,0:T(8,128)(2,1)S(1)}, bf16[32,32,128]{2,1,0:T(8,128)(2,1)}, u32[]{:S(2)}, u32[]{:S(2)}) collective-permute-start(bf16[32,32,128]{2,1,0:T(8,128)(2,1)S(1)} %get-tuple-element.24), channel_id=1, source_target_pairs={{0,1},{1,0},{2,3},{3,2},{4,5},{5,4},{6,7},{7,6},{8,9},{9,8},{10,11... | collective-permute-start | bytes 786440 | tf_op jit(solution)/shard_map/ppermute | solution.py:246
  43.3 2.0 %collective-permute-start.3 = (f32[8,2,4,16,128]{4,3,2,1,0:T(8,128)S(1)}, f32[8,2,4,16,128]{4,3,2,1,0:T(8,128)S(1)}, u32[]{:S(2)}, u32[]{:S(2)}) collective-permute-start(f32[8,2,4,16,128]{4,3,2,1,0:T(8,128)S(1)} %get-tuple-element.26), channel_id=1, source_target_pairs={{0,1},{1,0},{2,3},{3,2},{4,5},{5,4},{6,7},{7,6},{8,9},{9,8},{10,11... | collective-permute-start | bytes 1572872 | tf_op jit(solution)/shard_map/ppermute | solution.py:265

commit v9 on v8

--- a/solution.py
+++ b/solution.py
@@ -9,36 +9,43 @@
 
 NRB = 16
 TASK = ("ty", "core")
-EVERY = ("blk", "ty", "core")
+BLK = ("z", "x")
+AXES = BLK + TASK
+EVERY = ("x", "ty", "core", "z")
 
 
 def pack_kernel(counts, tiles, pieces, out, held, busy, in_sem, out_sem, count_sem):
-    tasks, _, rows, _ = held.shape
-    chunk = tiles.shape[2]
+    tasks, _, _, rows, _ = held.shape
+    chunk = tiles.shape[3]
     upper, lower = pl.ds(0, chunk), pl.ds(chunk, rows - chunk)
     count_copy = pltpu.make_async_copy(counts, busy, count_sem)
     count_copy.start()
-    first = [pltpu.make_async_copy(tiles.at[2 * w], held.at[w, :, upper], in_sem.at[0, w]) for w in range(tasks)]
+    first = [pltpu.make_async_copy(tiles.at[2 * w], held.at[w, :, :, upper], in_sem.at[0, w]) for w in range(tasks)]
     for copy in first:
         copy.start()
     count_copy.wait()
-    group = lax.axis_index("blk")
+    group = 2 * lax.axis_index("z") + lax.axis_index("x")
     tile = 1
     for w in range(1, tasks):
         tile = jnp.where(busy[w, group] == 2, 2 * w + 1, tile)
     second = [
-        pltpu.make_async_copy(pieces.at[tile, :, w], held.at[w, :, lower], in_sem.at[1, w]) for w in range(tasks)
+        pltpu.make_async_copy(pieces.at[tile, :, :, w], held.at[w, :, :, lower], in_sem.at[1, w]) for w in range(tasks)
     ]
     for copy in second:
         copy.start()
     leave = [
-        pltpu.make_async_copy(held.at[w, :, span], out.at[:, w, span], out_sem.at[half, w])
+        [
+            pltpu.make_async_copy(held.at[w, :, x, span], out.at[x, w, :, span], out_sem.at[half, w, x])
+            for x in range(2)
+        ]
         for half, span in enumerate((upper, lower))
         for w in range(tasks)
     ]
     for arrive, go in zip(first + second, leave):
         arrive.wait()
-        go.start()
+        for copy in go:
+            copy.start()
+    leave = sum(leave, [])
     for copy in leave:
         copy.wait()
 
@@ -47,23 +54,23 @@
     tasks, _, virt_total, row_block = integral_tiles.shape[2:]
     chunk = virt_total // blocks
     piece = chunk // tasks
-    tiles = integral_tiles.reshape(tasks * 2, blocks, chunk, row_block)
-    pieces = integral_tiles.reshape(tasks * 2, blocks, tasks, piece, row_block)
+    tiles = integral_tiles.reshape(tasks * 2, blocks // 2, 2, chunk, row_block)
+    pieces = integral_tiles.reshape(tasks * 2, blocks // 2, 2, tasks, piece, row_block)
     counts = jnp.transpose(tile_counts[:, 0])
     if piece % 16:
-        own = lax.dynamic_index_in_dim(counts, lax.axis_index("blk"), 1, keepdims=False)
+        own = lax.dynamic_index_in_dim(counts, lax.axis_index(BLK), 1, keepdims=False)
         second = lax.dynamic_index_in_dim(pieces, 2 * jnp.argmax(own) + 1, 0, keepdims=False)
-        return jnp.concatenate([jnp.swapaxes(tiles[::2], 0, 1), second], axis=2)
+        return jnp.concatenate([jnp.transpose(tiles[::2], (2, 0, 1, 3, 4)), jnp.transpose(second, (1, 2, 0, 3, 4))], axis=3)
     return pl.pallas_call(
         pack_kernel,
-        out_shape=jax.ShapeDtypeStruct((blocks, tasks, chunk + piece, row_block), tiles.dtype),
+        out_shape=jax.ShapeDtypeStruct((2, tasks, blocks // 2, chunk + piece, row_block), tiles.dtype),
         in_specs=[pl.BlockSpec(memory_space=pl.ANY)] * 3,
         out_specs=pl.BlockSpec(memory_space=pl.ANY),
         scratch_shapes=[
-            pltpu.VMEM((tasks, blocks, chunk + piece, row_block), tiles.dtype),
+            pltpu.VMEM((tasks, blocks // 2, 2, chunk + piece, row_block), tiles.dtype),
             pltpu.SMEM(counts.shape, counts.dtype),
         ]
-        + [pltpu.SemaphoreType.DMA((2, tasks))] * 2
+        + [pltpu.SemaphoreType.DMA((2, tasks)), pltpu.SemaphoreType.DMA((2, tasks, 2))]
         + [pltpu.SemaphoreType.DMA],
         compiler_params=pltpu.CompilerParams(vmem_limit_bytes=58 << 20),
         name="pack",
@@ -226,11 +233,16 @@
     counts, lists = lax.optimization_barrier((tile_counts[:, 0], lists))
     mine = lax.dynamic_index_in_dim(lists, worker, 2, keepdims=False)
     second_row = jnp.sum(jnp.where(counts[:, None] == 2, lists[..., 1] % NRB, 0), axis=-1)
-    meta = jnp.concatenate([(mine[..., 0] % NRB).reshape(-1), second_row.reshape(-1), core[None]])
+
+
+    def in_order(table):
+        return jnp.transpose(table.reshape(blocks // 2, 2, tasks), (1, 2, 0)).reshape(-1)
+
+    meta = jnp.concatenate([in_order(mine[..., 0] % NRB), in_order(second_row), core[None]])
 
     owner = lax.dynamic_index_in_dim(counts, worker, 1) == 2
-    column = jnp.where(owner, mine[..., 1] // NRB, span).reshape(-1)
-    first = (mine[..., 0] // NRB).reshape(-1)
+    column = in_order(jnp.where(owner, mine[..., 1] // NRB, span))
+    first = in_order(mine[..., 0] // NRB)
     others = []
     for hop in range(1, row_tasks):
         there, here = pick(column, amplitudes, hop, row_tasks, slots)
@@ -273,7 +285,7 @@
         compiler_params=pltpu.CompilerParams(vmem_limit_bytes=16 << 20),
         name="code",
     )(total, other.reshape(cut))
-    parts = lax.all_to_all(coded, ("blk", "ty"), 0, 0, tiled=True)
+    parts = lax.all_to_all(coded, BLK + ("ty",), 0, 0, tiled=True)
     return pl.pallas_call(
         decode_kernel,
         out_shape=jax.ShapeDtypeStruct((pairs, rows * row_block), jnp.float32),
@@ -286,15 +298,15 @@
 
 def solution(mesh):
     blocks, tasks = mesh.shape["blk"], mesh.shape["task"]
-    fine = Mesh(mesh.devices.reshape(blocks, tasks // 2, 2), EVERY)
+    fine = Mesh(mesh.devices.reshape(blocks // 2, 2, tasks // 2, 2), AXES)
     placed = (
-        P("blk", TASK, None),
-        P("blk", TASK, None, None, None, None),
+        P(BLK, TASK, None),
+        P(BLK, TASK, None, None, None, None),
         P(None, TASK, None, None),
         P(None, TASK, None, None),
         P(None, TASK, None),
     )
     return jax.shard_map(
         functools.partial(body, shape=(blocks, tasks // 2)),
-        mesh=fine, in_specs=placed, out_specs=P("blk", TASK), check_vma=False,
+        mesh=fine, in_specs=placed, out_specs=P(BLK, TASK), check_vma=False,
     )

time: 62.2 us -> 61.8 us (level)
  waiting for transfers between devices: 12.4 us -> 7.43 us
  starting transfers between devices: 8.73 us -> 11.2 us
  blocking collectives: 21.5 us -> 23.1 us
    all_to_all x1, waiting for transfers between devices: 7.24 us -> 3.88 us  [body(): arrived = lax.all_to_all(sent, EVERY, 0, 0, tiled=True)]
    all_gather x1, blocking collectives: 6.14 us -> 8.01 us  [body(): lax.all_gather(task_list * NRB + block_offsets, TASK, axis=1, tiled=True)]
    ppermute x1, waiting for transfers between devices: 2.21 us -> 0.36 us  [body(): lax.ppermute(away, 'ty', [(i, (i + hop) % row_tasks) for i in range(row_t...]
    ppermute x1, starting transfers between devices: 0.07 us -> 1.71 us  [body(): other = lax.ppermute(send, 'core', [(0, 1), (1, 0)])]
    ppermute x1, starting transfers between devices: 0.9 us -> 1.74 us  [body(): lax.ppermute(away, 'ty', [(i, (i + hop) % row_tasks) for i in range(row_t...]
    ppermute x1, waiting for transfers between devices: 0.01 us -> 0.72 us  [body(): others.append(lax.ppermute(there, 'core', [(0, 1), (1, 0)]))]
  transfers between devices with their start and end apart: 5 -> 5, of which waited for: 4 -> 5; matrix products, arithmetic and copies ran while one was open for 3% -> 4% of each run, Pallas kernels for 19% -> 19%
where the time goes in v9:
time: 61.8 us; the launch traced here: 61.4 us
  blocking collectives  23.1 us (37%)
  Pallas kernels  17.1 us (28%)
  starting transfers between devices  11.2 us (18%)
  waiting for transfers between devices  7.43 us (12%)
  other arithmetic  1.39 us (2%)
  local copies, waits for them, and re-layouts  1.11 us (2%)
    all_to_all x1, blocking collectives, body(): parts = lax.all_to_all(coded, BLK + ('ty',), 0, 0, tiled=True)  15.1 us
    pallas_call x2, Pallas kernels, pick(): pl.pallas_call(functools.partial(pick_kernel, hop=hop, row_tasks=row_task...  11.8 us
    all_gather x1, blocking collectives, body(): lax.all_gather(task_list * NRB + block_offsets, TASK, axis=1, tiled=True)  8.01 us
    all_to_all x1, starting transfers between devices, body(): arrived = lax.all_to_all(sent, EVERY, 0, 0, tiled=True)  7.3 us
    all_to_all x1, waiting for transfers between devices, body(): arrived = lax.all_to_all(sent, EVERY, 0, 0, tiled=True)  3.88 us
    pallas_call x1, Pallas kernels, pack(): pl.pallas_call(pack_kernel, out_shape=jax.ShapeDtypeStruct((2, tasks, blo...  2.71 us
    ppermute x1, starting transfers between devices, body(): lax.ppermute(away, 'ty', [(i, (i + hop) % row_tasks) for i in range(row_t...  1.74 us
    ppermute x1, starting transfers between devices, body(): other = lax.ppermute(send, 'core', [(0, 1), (1, 0)])  1.71 us
  transfers between devices with their start and end apart: 5, of which 5 were waited for; matrix products, arithmetic and copies ran while one was open for 4% of the time, Pallas kernels for 19%

profile of v9, /device:TPU:0, one launch (start us, length us, event | category | flops | bytes accessed | tf_op | source)
XLA Modules:
  0.0 61.4 jit_solution(15787550225938593393)
XLA Ops:
  0.0 2.7 %pack.1 = bf16[2,4,4,160,128]{4,3,2,1,0:T(8,128)(2,1)} custom-call(s32[4,8]{1,0:T(4,128)} %bitcast.34, bf16[8,4,2,128,128]{4,3,2,1,0:T(8,128)(2,1)} %bitcast.27, bf16[8,4,2,4,32,128]{5,4,3,2,1,0:T(8,128)(2,1)} %bitcast.28), custom_call_target="tpu_custom_call" | custom-call | tf_op jit(solution)/shard_map/pack/pallas_call | solution.py:64
  2.7 0.0 copy-start.1
  2.7 0.0 copy-start.2
  2.7 0.0 copy-start
  2.8 7.3 %all-to-all-start = ((bf16[32,160,128]{2,1,0:T(8,128)(2,1)}), bf16[32,160,128]{2,1,0:T(8,128)(2,1)S(1)}, u32[]{:S(2)}, u32[]{:S(2)}) async-start(bf16[32,160,128]{2,1,0:T(8,128)(2,1)} %bitcast.29), calls=%async_computation | async-start | bytes 2621440 | tf_op jit(solution)/shard_map/all_to_all | solution.py:230
  10.1 0.0 copy-done.1
  10.1 0.0 copy-done.2
  10.1 8.0 %all_gather.3 = s32[8,4,4,2]{0,2,3,1:T(4,128)S(1)} all-gather(s32[8,1,4,2]{0,2,3,1:T(4,128)S(1)} %copy_add_fusion), channel_id=1, replica_groups=mesh['z'=4,'x'=2,'ty'=2,'core'=2] {'ty','core'}, dimensions={1}, use_global_device_ids=true | all-gather | bytes 1280 | tf_op jit(solution)/shard_map/all_gather | solution.py:232
  18.1 0.0 copy-done
  18.1 0.1 broadcast_in_dim.30
  18.3 0.1 copy.20
  18.3 0.1 select_bitcast_fusion
  18.4 0.1 copy.21
  18.5 0.1 reshape.43.lists
  18.6 4.1 %pick.2 = (bf16[32,32,128]{2,1,0:T(8,128)(2,1)S(1)}, bf16[32,32,128]{2,1,0:T(8,128)(2,1)S(1)}) custom-call(s32[32]{0:T(128)S(1)} %reshape.43.lists, bf16[128,256,128]{2,1,0:T(8,128)(2,1)} %amplitudes.3), custom_call_target="tpu_custom_call" | custom-call | flops 134217728 | bytes 4718592 | tf_op jit(solution)/shard_map/pick/pallas_call | solution.py:130
  22.7 0.4 collective-permute-start
  23.0 0.1 copy.16
  23.2 0.1 copy.22
  23.3 0.1 reshape.44
  23.3 0.9 %collective-permute-done = bf16[32,32,128]{2,1,0:T(8,128)(2,1)S(1)} collective-permute-done((bf16[32,32,128]{2,1,0:T(8,128)(2,1)S(1)}, bf16[32,32,128]{2,1,0:T(8,128)(2,1)S(1)}, u32[]{:S(2)}, u32[]{:S(2)}) %collective-permute-start) | collective-permute-done | bytes 262176 | tf_op jit(solution)/shard_map/ppermute | solution.py:249
  24.3 0.1 add.43
  24.4 1.7 %collective-permute-start.1 = (bf16[32,32,128]{2,1,0:T(8,128)(2,1)S(1)}, bf16[32,32,128]{2,1,0:T(8,128)(2,1)S(1)}, u32[]{:S(2)}, u32[]{:S(2)}) collective-permute-start(bf16[32,32,128]{2,1,0:T(8,128)(2,1)S(1)} %add.43), channel_id=1, source_target_pairs={{0,2},{2,0},{1,3},{3,1},{4,6},{6,4},{5,7},{7,5},{8,10},{10,8},{9,1... | collective-permute-start | bytes 786440 | tf_op jit(solution)/shard_map/ppermute | solution.py:250
  26.1 0.1 pad_add_fusion.1.lists
  26.2 7.8 %pick.3 = (bf16[32,32,128]{2,1,0:T(8,128)(2,1)S(1)}, bf16[32,32,128]{2,1,0:T(8,128)(2,1)S(1)}, bf16[32,128,128]{2,1,0:T(8,128)(2,1)S(1)}) custom-call(s32[64]{0:T(128)S(1)} %pad_add_fusion.1.lists, bf16[128,256,128]{2,1,0:T(8,128)(2,1)} %amplitudes.3), custom_call_target="tpu_custom_call" | custom-call | flops 536870912 | bytes 10485760 | tf_op jit(solution)/shard_map/pick/pallas_call | solution.py:130
  34.0 0.1 collective-permute-start.2
  34.1 0.1 copy.18
  34.2 0.1 copy.19
  34.3 0.1 reshape.42
  34.4 0.1 copy.17
  34.4 0.1 reshape.40
  34.5 0.1 pad_add_fusion.meta
  34.6 0.4 collective-permute-done.1
  35.0 0.7 %collective-permute-done.2 = bf16[32,32,128]{2,1,0:T(8,128)(2,1)} collective-permute-done((bf16[32,32,128]{2,1,0:T(8,128)(2,1)S(1)}, bf16[32,32,128]{2,1,0:T(8,128)(2,1)}, u32[]{:S(2)}, u32[]{:S(2)}) %collective-permute-start.2) | collective-permute-done | bytes 262176 | tf_op jit(solution)/shard_map/ppermute | solution.py:258
  35.7 1.0 %add_add_fusion.extras = bf16[32,32,128]{2,1,0:T(8,128)(2,1)S(1)} fusion(bf16[32,32,128]{2,1,0:T(8,128)(2,1)} %collective-permute-done.2, bf16[32,32,128]{2,1,0:T(8,128)(2,1)S(1)} %get-tuple-element.23, bf16[32,32,128]{2,1,0:T(8,128)(2,1)S(1)} %collective-permute-done.1), kind=kLoop, calls=%fused_computation | loop fusion | flops 262144 | bytes 1048576 | tf_op jit(solution)/shard_map/add | solution.py:259
  36.7 3.9 %all-to-all-done.tiles = bf16[32,160,128]{2,1,0:T(8,128)(2,1)S(1)} async-done(((bf16[32,160,128]{2,1,0:T(8,128)(2,1)}), bf16[32,160,128]{2,1,0:T(8,128)(2,1)S(1)}, u32[]{:S(2)}, u32[]{:S(2)}) %all-to-all-start) | async-done | bytes 1310752 | tf_op jit(solution)/shard_map/all_to_all | solution.py:230
  40.6 1.4 %ladder.1 = (f32[8,2,4,16,128]{4,3,2,1,0:T(8,128)S(1)}, f32[16,128,128]{2,1,0:T(8,128)S(1)}) custom-call(s32[65]{0:T(128)S(1)} %pad_add_fusion.meta, bf16[32,128,128]{2,1,0:T(8,128)(2,1)S(1)} %get-tuple-element.22.columns, bf16[32,160,128]{2,1,0:T(8,128)(2,1)S(1)} %all-to-all-done.tiles, bf16[32,32,128]{2,1,0:T(8,128)(2,1)S(1)} %add_add_fusion.extras), custom_call_target="tpu_custom_call" | custom-call | flops 167772160 | bytes 3670016 | tf_op jit(solution)/shard_map/ladder/pallas_call | solution.py:263
  42.0 1.7 %collective-permute-start.3 = (f32[8,2,4,16,128]{4,3,2,1,0:T(8,128)S(1)}, f32[8,2,4,16,128]{4,3,2,1,0:T(8,128)S(1)}, u32[]{:S(2)}, u32[]{:S(2)}) collective-permute-start(f32[8,2,4,16,128]{4,3,2,1,0:T(8,128)S(1)} %get-tuple-element.26), channel_id=1, source_target_pairs={{0,1},{1,0},{2,3},{3,2},{4,5},{5,4},{6,7},{7,6},{8,9},{9,8},{10,11... | collective-permute-start | bytes 1572872 | tf_op jit(solution)/shard_map/ppermute | solution.py:277
  43.7 1.5 %collective-permute-done.3 = f32[8,2,4,16,128]{4,3,2,1,0:T(8,128)S(1)} collective-permute-done((f32[8,2,4,16,128]{4,3,2,1,0:T(8,128)S(1)}, f32[8,2,4,16,128]{4,3,2,1,0:T(8,128)S(1)}, u32[]{:S(2)}, u32[]{:S(2)}) %collective-permute-start.3) | collective-permute-done | bytes 524320 | tf_op jit(solution)/shard_map/ppermute | solution.py:277
  45.2 0.3 code.1
  45.5 15.1 %all_to_all.10.parts = s16[16,72,128]{2,1,0:T(8,128)(2,1)S(1)} all-to-all(s16[16,72,128]{2,1,0:T(8,128)(2,1)S(1)} %code.1), channel_id=1, replica_groups=mesh['z'=4,'x'=2,'ty'=2,'core'=2] {'z','x','ty'}, dimensions={0} | all-to-all | bytes 589824 | tf_op jit(solution)/shard_map/all_to_all | solution.py:288
  60.6 0.8 %decode.1 = f32[16,512]{1,0:T(8,128)} custom-call(s16[16,72,128]{2,1,0:T(8,128)(2,1)S(1)} %all_to_all.10.parts), custom_call_target="tpu_custom_call" | custom-call | tf_op jit(solution)/shard_map/decode/pallas_call | solution.py:289
  (8 shorter events, 0.1 us)
Async XLA Ops:
  2.7 7.4 %copy-start.1 = (s32[8,1,4,2]{0,3,2,1:T(2,128)S(1)}, s32[8,1,4,2]{0,3,2,1:T(2,128)}, u32[]{:S(2)}) copy-start(s32[8,1,4,2]{0,3,2,1:T(2,128)} %param.8) | copy-start | bytes 772
  2.7 7.4 %copy-start.2 = (s32[8,1,4,2]{0,3,2,1:T(2,128)S(1)}, s32[8,1,4,2]{0,3,2,1:T(2,128)}, u32[]{:S(2)}) copy-start(s32[8,1,4,2]{0,3,2,1:T(2,128)} %param.7) | copy-start | bytes 772
  2.7 15.4 %copy-start = (s32[8,1,4]{0,2,1:T(4,128)S(1)}, s32[8,1,4]{0,2,1:T(4,128)}, u32[]{:S(2)}) copy-start(s32[8,1,4]{0,2,1:T(4,128)} %param.9) | copy-start | bytes 388
  2.8 37.8 %all-to-all-start = ((bf16[32,160,128]{2,1,0:T(8,128)(2,1)}), bf16[32,160,128]{2,1,0:T(8,128)(2,1)S(1)}, u32[]{:S(2)}, u32[]{:S(2)}) async-start(bf16[32,160,128]{2,1,0:T(8,128)(2,1)} %bitcast.29), calls=%async_computation | async-start | bytes 2621440 | tf_op jit(solution)/shard_map/all_to_all | solution.py:230
  22.7 1.6 %collective-permute-start = (bf16[32,32,128]{2,1,0:T(8,128)(2,1)S(1)}, bf16[32,32,128]{2,1,0:T(8,128)(2,1)S(1)}, u32[]{:S(2)}, u32[]{:S(2)}) collective-permute-start(bf16[32,32,128]{2,1,0:T(8,128)(2,1)S(1)} %get-tuple-element.19), channel_id=1, source_target_pairs={{0,1},{1,0},{2,3},{3,2},{4,5},{5,4},{6,7},{7,6},{8,9},{9,8},{10,11... | collective-permute-start | bytes 786440 | tf_op jit(solution)/shard_map/ppermute | solution.py:249
  24.4 10.6 %collective-permute-start.1 = (bf16[32,32,128]{2,1,0:T(8,128)(2,1)S(1)}, bf16[32,32,128]{2,1,0:T(8,128)(2,1)S(1)}, u32[]{:S(2)}, u32[]{:S(2)}) collective-permute-start(bf16[32,32,128]{2,1,0:T(8,128)(2,1)S(1)} %add.43), channel_id=1, source_target_pairs={{0,2},{2,0},{1,3},{3,1},{4,6},{6,4},{5,7},{7,5},{8,10},{10,8},{9,1... | collective-permute-start | bytes 786440 | tf_op jit(solution)/shard_map/ppermute | solution.py:250
  34.0 1.7 %collective-permute-start.2 = (bf16[32,32,128]{2,1,0:T(8,128)(2,1)S(1)}, bf16[32,32,128]{2,1,0:T(8,128)(2,1)}, u32[]{:S(2)}, u32[]{:S(2)}) collective-permute-start(bf16[32,32,128]{2,1,0:T(8,128)(2,1)S(1)} %get-tuple-element.24), channel_id=1, source_target_pairs={{0,1},{1,0},{2,3},{3,2},{4,5},{5,4},{6,7},{7,6},{8,9},{9,8},{10,11... | collective-permute-start | bytes 786440 | tf_op jit(solution)/shard_map/ppermute | solution.py:258
  42.0 3.3 %collective-permute-start.3 = (f32[8,2,4,16,128]{4,3,2,1,0:T(8,128)S(1)}, f32[8,2,4,16,128]{4,3,2,1,0:T(8,128)S(1)}, u32[]{:S(2)}, u32[]{:S(2)}) collective-permute-start(f32[8,2,4,16,128]{4,3,2,1,0:T(8,128)S(1)} %get-tuple-element.26), channel_id=1, source_target_pairs={{0,1},{1,0},{2,3},{3,2},{4,5},{5,4},{6,7},{7,6},{8,9},{9,8},{10,11... | collective-permute-start | bytes 1572872 | tf_op jit(solution)/shard_map/ppermute | solution.py:277

commit v10 on v9

--- a/solution.py
+++ b/solution.py
@@ -14,13 +14,13 @@
 EVERY = ("x", "ty", "core", "z")
 
 
-def pack_kernel(counts, tiles, pieces, out, held, busy, in_sem, out_sem, count_sem):
-    tasks, _, _, rows, _ = held.shape
-    chunk = tiles.shape[3]
+def pack_kernel(counts, tiles, pieces, out, held, cut, busy, in_sem, out_sem, count_sem):
+    tasks, _, _, chunk, _ = held.shape
+    rows = out.shape[3]
     upper, lower = pl.ds(0, chunk), pl.ds(chunk, rows - chunk)
     count_copy = pltpu.make_async_copy(counts, busy, count_sem)
     count_copy.start()
-    first = [pltpu.make_async_copy(tiles.at[2 * w], held.at[w, :, :, upper], in_sem.at[0, w]) for w in range(tasks)]
+    first = [pltpu.make_async_copy(tiles.at[2 * w], held.at[w], in_sem.at[0, w, 0]) for w in range(tasks)]
     for copy in first:
         copy.start()
     count_copy.wait()
@@ -29,23 +29,22 @@
     for w in range(1, tasks):
         tile = jnp.where(busy[w, group] == 2, 2 * w + 1, tile)
     second = [
-        pltpu.make_async_copy(pieces.at[tile, :, :, w], held.at[w, :, :, lower], in_sem.at[1, w]) for w in range(tasks)
+        pltpu.make_async_copy(pieces.at[tile, :, x, w], cut.at[x, w], in_sem.at[1, w, x])
+        for w in range(tasks)
+        for x in range(2)
     ]
     for copy in second:
         copy.start()
-    leave = [
-        [
-            pltpu.make_async_copy(held.at[w, :, x, span], out.at[x, w, :, span], out_sem.at[half, w, x])
-            for x in range(2)
-        ]
-        for half, span in enumerate((upper, lower))
-        for w in range(tasks)
-    ]
-    for arrive, go in zip(first + second, leave):
-        arrive.wait()
-        for copy in go:
-            copy.start()
-    leave = sum(leave, [])
+    leave = []
+    for w, copy in enumerate(first):
+        copy.wait()
+        for x in range(2):
+            leave.append(pltpu.make_async_copy(held.at[w, :, x], out.at[x, w, :, upper], out_sem.at[0, w, x]))
+            leave[-1].start()
+    for copy in second:
+        copy.wait()
+    leave.append(pltpu.make_async_copy(cut, out.at[:, :, :, lower], out_sem.at[1, 0, 0]))
+    leave[-1].start()
     for copy in leave:
         copy.wait()
 
@@ -67,10 +66,11 @@
         in_specs=[pl.BlockSpec(memory_space=pl.ANY)] * 3,
         out_specs=pl.BlockSpec(memory_space=pl.ANY),
         scratch_shapes=[
-            pltpu.VMEM((tasks, blocks // 2, 2, chunk + piece, row_block), tiles.dtype),
+            pltpu.VMEM((tasks, blocks // 2, 2, chunk, row_block), tiles.dtype),
+            pltpu.VMEM((2, tasks, blocks // 2, piece, row_block), tiles.dtype),
             pltpu.SMEM(counts.shape, counts.dtype),
         ]
-        + [pltpu.SemaphoreType.DMA((2, tasks)), pltpu.SemaphoreType.DMA((2, tasks, 2))]
+        + [pltpu.SemaphoreType.DMA((2, tasks, 2))] * 2
         + [pltpu.SemaphoreType.DMA],
         compiler_params=pltpu.CompilerParams(vmem_limit_bytes=58 << 20),
         name="pack",

time: 61.8 us -> 61.9 us (level)
  no operation moved by 1% of the time
where the time goes in v10:
time: 61.9 us; the launch traced here: 61.5 us
  blocking collectives  23.1 us (37%)
  Pallas kernels  17.2 us (28%)
  starting transfers between devices  11.2 us (18%)
  waiting for transfers between devices  7.42 us (12%)
  other arithmetic  1.39 us (2%)
  local copies, waits for them, and re-layouts  1.11 us (2%)
    all_to_all x1, blocking collectives, body(): parts = lax.all_to_all(coded, BLK + ('ty',), 0, 0, tiled=True)  15.1 us
    pallas_call x2, Pallas kernels, pick(): pl.pallas_call(functools.partial(pick_kernel, hop=hop, row_tasks=row_task...  11.8 us
    all_gather x1, blocking collectives, body(): lax.all_gather(task_list * NRB + block_offsets, TASK, axis=1, tiled=True)  8.01 us
    all_to_all x1, starting transfers between devices, body(): arrived = lax.all_to_all(sent, EVERY, 0, 0, tiled=True)  7.3 us
    all_to_all x1, waiting for transfers between devices, body(): arrived = lax.all_to_all(sent, EVERY, 0, 0, tiled=True)  3.88 us
    pallas_call x1, Pallas kernels, pack(): pl.pallas_call(pack_kernel, out_shape=jax.ShapeDtypeStruct((2, tasks, blo...  2.8 us
    ppermute x1, starting transfers between devices, body(): lax.ppermute(away, 'ty', [(i, (i + hop) % row_tasks) for i in range(row_t...  1.74 us
    ppermute x1, starting transfers between devices, body(): other = lax.ppermute(send, 'core', [(0, 1), (1, 0)])  1.71 us
  transfers between devices with their start and end apart: 5, of which 5 were waited for; matrix products, arithmetic and copies ran while one was open for 4% of the time, Pallas kernels for 19%

profile of v10, /device:TPU:0, one launch (start us, length us, event | category | flops | bytes accessed | tf_op | source)
XLA Modules:
  0.0 61.5 jit_solution(1855825372019041965)
XLA Ops:
  0.0 2.8 %pack.1 = bf16[2,4,4,160,128]{4,3,2,1,0:T(8,128)(2,1)} custom-call(s32[4,8]{1,0:T(4,128)} %bitcast.34, bf16[8,4,2,128,128]{4,3,2,1,0:T(8,128)(2,1)} %bitcast.27, bf16[8,4,2,4,32,128]{5,4,3,2,1,0:T(8,128)(2,1)} %bitcast.28), custom_call_target="tpu_custom_call" | custom-call | tf_op jit(solution)/shard_map/pack/pallas_call | solution.py:63
  2.8 0.0 copy-start.1
  2.8 0.0 copy-start.2
  2.8 0.0 copy-start
  2.8 7.3 %all-to-all-start = ((bf16[32,160,128]{2,1,0:T(8,128)(2,1)}), bf16[32,160,128]{2,1,0:T(8,128)(2,1)S(1)}, u32[]{:S(2)}, u32[]{:S(2)}) async-start(bf16[32,160,128]{2,1,0:T(8,128)(2,1)} %bitcast.29), calls=%async_computation | async-start | bytes 2621440 | tf_op jit(solution)/shard_map/all_to_all | solution.py:230
  10.2 0.0 copy-done.1
  10.2 0.0 copy-done.2
  10.2 8.0 %all_gather.3 = s32[8,4,4,2]{0,2,3,1:T(4,128)S(1)} all-gather(s32[8,1,4,2]{0,2,3,1:T(4,128)S(1)} %copy_add_fusion), channel_id=1, replica_groups=mesh['z'=4,'x'=2,'ty'=2,'core'=2] {'ty','core'}, dimensions={1}, use_global_device_ids=true | all-gather | bytes 1280 | tf_op jit(solution)/shard_map/all_gather | solution.py:232
  18.2 0.0 copy-done
  18.2 0.1 broadcast_in_dim.30
  18.4 0.1 copy.20
  18.4 0.1 select_bitcast_fusion
  18.5 0.1 copy.21
  18.6 0.1 reshape.43.lists
  18.7 4.1 %pick.2 = (bf16[32,32,128]{2,1,0:T(8,128)(2,1)S(1)}, bf16[32,32,128]{2,1,0:T(8,128)(2,1)S(1)}) custom-call(s32[32]{0:T(128)S(1)} %reshape.43.lists, bf16[128,256,128]{2,1,0:T(8,128)(2,1)} %amplitudes.3), custom_call_target="tpu_custom_call" | custom-call | flops 134217728 | bytes 4718592 | tf_op jit(solution)/shard_map/pick/pallas_call | solution.py:130
  22.8 0.4 collective-permute-start
  23.1 0.1 copy.16
  23.2 0.1 copy.22
  23.3 0.1 reshape.44
  23.4 0.9 %collective-permute-done = bf16[32,32,128]{2,1,0:T(8,128)(2,1)S(1)} collective-permute-done((bf16[32,32,128]{2,1,0:T(8,128)(2,1)S(1)}, bf16[32,32,128]{2,1,0:T(8,128)(2,1)S(1)}, u32[]{:S(2)}, u32[]{:S(2)}) %collective-permute-start) | collective-permute-done | bytes 262176 | tf_op jit(solution)/shard_map/ppermute | solution.py:249
  24.4 0.1 add.43
  24.4 1.7 %collective-permute-start.1 = (bf16[32,32,128]{2,1,0:T(8,128)(2,1)S(1)}, bf16[32,32,128]{2,1,0:T(8,128)(2,1)S(1)}, u32[]{:S(2)}, u32[]{:S(2)}) collective-permute-start(bf16[32,32,128]{2,1,0:T(8,128)(2,1)S(1)} %add.43), channel_id=1, source_target_pairs={{0,2},{2,0},{1,3},{3,1},{4,6},{6,4},{5,7},{7,5},{8,10},{10,8},{9,1... | collective-permute-start | bytes 786440 | tf_op jit(solution)/shard_map/ppermute | solution.py:250
  26.2 0.1 pad_add_fusion.1.lists
  26.3 7.8 %pick.3 = (bf16[32,32,128]{2,1,0:T(8,128)(2,1)S(1)}, bf16[32,32,128]{2,1,0:T(8,128)(2,1)S(1)}, bf16[32,128,128]{2,1,0:T(8,128)(2,1)S(1)}) custom-call(s32[64]{0:T(128)S(1)} %pad_add_fusion.1.lists, bf16[128,256,128]{2,1,0:T(8,128)(2,1)} %amplitudes.3), custom_call_target="tpu_custom_call" | custom-call | flops 536870912 | bytes 10485760 | tf_op jit(solution)/shard_map/pick/pallas_call | solution.py:130
  34.0 0.1 collective-permute-start.2
  34.2 0.1 copy.18
  34.3 0.1 copy.19
  34.4 0.1 reshape.42
  34.4 0.1 copy.17
  34.5 0.1 reshape.40
  34.6 0.1 pad_add_fusion.meta
  34.7 0.4 collective-permute-done.1
  35.1 0.7 %collective-permute-done.2 = bf16[32,32,128]{2,1,0:T(8,128)(2,1)} collective-permute-done((bf16[32,32,128]{2,1,0:T(8,128)(2,1)S(1)}, bf16[32,32,128]{2,1,0:T(8,128)(2,1)}, u32[]{:S(2)}, u32[]{:S(2)}) %collective-permute-start.2) | collective-permute-done | bytes 262176 | tf_op jit(solution)/shard_map/ppermute | solution.py:258
  35.8 1.0 %add_add_fusion.extras = bf16[32,32,128]{2,1,0:T(8,128)(2,1)S(1)} fusion(bf16[32,32,128]{2,1,0:T(8,128)(2,1)} %collective-permute-done.2, bf16[32,32,128]{2,1,0:T(8,128)(2,1)S(1)} %get-tuple-element.23, bf16[32,32,128]{2,1,0:T(8,128)(2,1)S(1)} %collective-permute-done.1), kind=kLoop, calls=%fused_computation | loop fusion | flops 262144 | bytes 1048576 | tf_op jit(solution)/shard_map/add | solution.py:259
  36.8 3.9 %all-to-all-done.tiles = bf16[32,160,128]{2,1,0:T(8,128)(2,1)S(1)} async-done(((bf16[32,160,128]{2,1,0:T(8,128)(2,1)}), bf16[32,160,128]{2,1,0:T(8,128)(2,1)S(1)}, u32[]{:S(2)}, u32[]{:S(2)}) %all-to-all-start) | async-done | bytes 1310752 | tf_op jit(solution)/shard_map/all_to_all | solution.py:230
  40.7 1.4 %ladder.1 = (f32[8,2,4,16,128]{4,3,2,1,0:T(8,128)S(1)}, f32[16,128,128]{2,1,0:T(8,128)S(1)}) custom-call(s32[65]{0:T(128)S(1)} %pad_add_fusion.meta, bf16[32,128,128]{2,1,0:T(8,128)(2,1)S(1)} %get-tuple-element.22.columns, bf16[32,160,128]{2,1,0:T(8,128)(2,1)S(1)} %all-to-all-done.tiles, bf16[32,32,128]{2,1,0:T(8,128)(2,1)S(1)} %add_add_fusion.extras), custom_call_target="tpu_custom_call" | custom-call | flops 167772160 | bytes 3670016 | tf_op jit(solution)/shard_map/ladder/pallas_call | solution.py:263
  42.1 1.7 %collective-permute-start.3 = (f32[8,2,4,16,128]{4,3,2,1,0:T(8,128)S(1)}, f32[8,2,4,16,128]{4,3,2,1,0:T(8,128)S(1)}, u32[]{:S(2)}, u32[]{:S(2)}) collective-permute-start(f32[8,2,4,16,128]{4,3,2,1,0:T(8,128)S(1)} %get-tuple-element.26), channel_id=1, source_target_pairs={{0,1},{1,0},{2,3},{3,2},{4,5},{5,4},{6,7},{7,6},{8,9},{9,8},{10,11... | collective-permute-start | bytes 1572872 | tf_op jit(solution)/shard_map/ppermute | solution.py:277
  43.8 1.5 %collective-permute-done.3 = f32[8,2,4,16,128]{4,3,2,1,0:T(8,128)S(1)} collective-permute-done((f32[8,2,4,16,128]{4,3,2,1,0:T(8,128)S(1)}, f32[8,2,4,16,128]{4,3,2,1,0:T(8,128)S(1)}, u32[]{:S(2)}, u32[]{:S(2)}) %collective-permute-start.3) | collective-permute-done | bytes 524320 | tf_op jit(solution)/shard_map/ppermute | solution.py:277
  45.3 0.3 code.1
  45.6 15.1 %all_to_all.10.parts = s16[16,72,128]{2,1,0:T(8,128)(2,1)S(1)} all-to-all(s16[16,72,128]{2,1,0:T(8,128)(2,1)S(1)} %code.1), channel_id=1, replica_groups=mesh['z'=4,'x'=2,'ty'=2,'core'=2] {'z','x','ty'}, dimensions={0} | all-to-all | bytes 589824 | tf_op jit(solution)/shard_map/all_to_all | solution.py:288
  60.7 0.8 %decode.1 = f32[16,512]{1,0:T(8,128)} custom-call(s16[16,72,128]{2,1,0:T(8,128)(2,1)S(1)} %all_to_all.10.parts), custom_call_target="tpu_custom_call" | custom-call | tf_op jit(solution)/shard_map/decode/pallas_call | solution.py:289
  (8 shorter events, 0.1 us)
Async XLA Ops:
  2.8 7.4 %copy-start.1 = (s32[8,1,4,2]{0,3,2,1:T(2,128)S(1)}, s32[8,1,4,2]{0,3,2,1:T(2,128)}, u32[]{:S(2)}) copy-start(s32[8,1,4,2]{0,3,2,1:T(2,128)} %param.8) | copy-start | bytes 772
  2.8 7.4 %copy-start.2 = (s32[8,1,4,2]{0,3,2,1:T(2,128)S(1)}, s32[8,1,4,2]{0,3,2,1:T(2,128)}, u32[]{:S(2)}) copy-start(s32[8,1,4,2]{0,3,2,1:T(2,128)} %param.7) | copy-start | bytes 772
  2.8 15.4 %copy-start = (s32[8,1,4]{0,2,1:T(4,128)S(1)}, s32[8,1,4]{0,2,1:T(4,128)}, u32[]{:S(2)}) copy-start(s32[8,1,4]{0,2,1:T(4,128)} %param.9) | copy-start | bytes 388
  2.8 37.8 %all-to-all-start = ((bf16[32,160,128]{2,1,0:T(8,128)(2,1)}), bf16[32,160,128]{2,1,0:T(8,128)(2,1)S(1)}, u32[]{:S(2)}, u32[]{:S(2)}) async-start(bf16[32,160,128]{2,1,0:T(8,128)(2,1)} %bitcast.29), calls=%async_computation | async-start | bytes 2621440 | tf_op jit(solution)/shard_map/all_to_all | solution.py:230
  22.8 1.6 %collective-permute-start = (bf16[32,32,128]{2,1,0:T(8,128)(2,1)S(1)}, bf16[32,32,128]{2,1,0:T(8,128)(2,1)S(1)}, u32[]{:S(2)}, u32[]{:S(2)}) collective-permute-start(bf16[32,32,128]{2,1,0:T(8,128)(2,1)S(1)} %get-tuple-element.19), channel_id=1, source_target_pairs={{0,1},{1,0},{2,3},{3,2},{4,5},{5,4},{6,7},{7,6},{8,9},{9,8},{10,11... | collective-permute-start | bytes 786440 | tf_op jit(solution)/shard_map/ppermute | solution.py:249
  24.4 10.6 %collective-permute-start.1 = (bf16[32,32,128]{2,1,0:T(8,128)(2,1)S(1)}, bf16[32,32,128]{2,1,0:T(8,128)(2,1)S(1)}, u32[]{:S(2)}, u32[]{:S(2)}) collective-permute-start(bf16[32,32,128]{2,1,0:T(8,128)(2,1)S(1)} %add.43), channel_id=1, source_target_pairs={{0,2},{2,0},{1,3},{3,1},{4,6},{6,4},{5,7},{7,5},{8,10},{10,8},{9,1... | collective-permute-start | bytes 786440 | tf_op jit(solution)/shard_map/ppermute | solution.py:250
  34.0 1.7 %collective-permute-start.2 = (bf16[32,32,128]{2,1,0:T(8,128)(2,1)S(1)}, bf16[32,32,128]{2,1,0:T(8,128)(2,1)}, u32[]{:S(2)}, u32[]{:S(2)}) collective-permute-start(bf16[32,32,128]{2,1,0:T(8,128)(2,1)S(1)} %get-tuple-element.24), channel_id=1, source_target_pairs={{0,1},{1,0},{2,3},{3,2},{4,5},{5,4},{6,7},{7,6},{8,9},{9,8},{10,11... | collective-permute-start | bytes 786440 | tf_op jit(solution)/shard_map/ppermute | solution.py:258
  42.1 3.3 %collective-permute-start.3 = (f32[8,2,4,16,128]{4,3,2,1,0:T(8,128)S(1)}, f32[8,2,4,16,128]{4,3,2,1,0:T(8,128)S(1)}, u32[]{:S(2)}, u32[]{:S(2)}) collective-permute-start(f32[8,2,4,16,128]{4,3,2,1,0:T(8,128)S(1)} %get-tuple-element.26), channel_id=1, source_target_pairs={{0,1},{1,0},{2,3},{3,2},{4,5},{5,4},{6,7},{7,6},{8,9},{9,8},{10,11... | collective-permute-start | bytes 1572872 | tf_op jit(solution)/shard_map/ppermute | solution.py:277
